TPU v7x, 512 devices: a whole 4x4x16 slice. The times are simulated.
512 devices in a mesh: gz: 64 (over z_lo, x, y), gy: 8 (over z_hi, core).
Axes of the slice: x: 4, y: 4, z: 16 (z_hi: 4, z_lo: 4; z = z_hi * 4 + z_lo), core: 2. Of those that a mesh axis runs over, the one named last changes fastest.
Arguments:
- levels: float32 [4, 256, 64, 512], P(None, 'gz', 'gy'), may hold values from -20 to 20
- ct_image: float32 [256, 64, 512], P('gz', 'gy'), may hold values from -4 to 4
- region_means: float32 [16], replicated, may hold values from -1.5 to 1.5
Outputs:
- evolved: float32 [4, 256, 64, 512], P(None, 'gz', 'gy')
- regularized: float32 [4, 256, 64, 512], P(None, 'gz', 'gy')
All inputs are finite; a program needn't handle non-finite values.
Results may differ from a plain program's by a relative error of at most 0.000022.
Values sent between devices are 32-bit elements; how exact they have to be, the bound alone decides.
A program may use at most 64 MiB of HBM per device.

v0:
```python
import math

import jax
import jax.numpy as jnp
from jax import lax
from jax.sharding import PartitionSpec as P

LEVELS = 4
PHASES = 16
UPDATES = 2
KERNEL = 200


PENALTY = 0.0005
STEP_SIZE = 0.5


def with_halo(block, sides, width):
    for axis, dim in sides:
        count = lax.axis_size(axis)
        forward = [(i, i + 1) for i in range(count - 1)]
        backward = [(target, source) for source, target in forward]
        low = lax.ppermute(
            lax.slice_in_dim(block, block.shape[dim] - width, None, axis=dim), axis, forward
        )
        high = lax.ppermute(lax.slice_in_dim(block, 0, width, axis=dim), axis, backward)
        block = jnp.concatenate([low, block, high], axis=dim)
    return block


def evolve(level_pad, picture, region_means):
    interior = level_pad[:, 1:-1, 1:-1, :]
    side_x = jnp.pad(interior, ((0, 0), (0, 0), (0, 0), (1, 1)))
    laplace = level_pad[:, 2:, 1:-1, :] + level_pad[:, :-2, 1:-1, :]
    laplace = laplace + level_pad[:, 1:-1, 2:, :] + level_pad[:, 1:-1, :-2, :]
    laplace = laplace + side_x[..., 2:] + side_x[..., :-2] - 6.0 * interior
    heaviside = 0.5 + jnp.arctan(interior) / math.pi
    delta_term = 1.0 / (math.pi * (1.0 + interior * interior))
    forces = [jnp.zeros_like(interior[0]) for level_id in range(LEVELS)]
    for phase_id in range(PHASES):
        differ = picture - region_means[phase_id]
        energy = differ * differ
        factors = []
        for level_id in range(LEVELS):
            if phase_id >> level_id & 1:
                factors.append(heaviside[level_id])
            else:
                factors.append(1.0 - heaviside[level_id])
        for level_id in range(LEVELS):
            sign_value = 1.0 if phase_id >> level_id & 1 else -1.0
            others = energy
            for other_id in range(LEVELS):
                if other_id != level_id:
                    others = others * factors[other_id]
            forces[level_id] = forces[level_id] + sign_value * others
    force_all = jnp.stack(forces, axis=0)
    return interior + STEP_SIZE * delta_term * (laplace - force_all)


def minplus_lines(field_in, line_axis, kernel_reach):
    moved_field = jnp.moveaxis(field_in, line_axis, -1)
    line_shape = moved_field.shape
    line_len = line_shape[-1]
    line_rows = moved_field.reshape(-1, line_len)
    row_count = line_rows.shape[0]
    positions = jnp.arange(line_len, dtype=jnp.float32)
    distance = positions[:, None] - positions[None, :]
    penalty_table = jnp.where(
        jnp.abs(distance) <= kernel_reach, PENALTY * (distance * distance), jnp.inf
    )
    row_limit = max(1, 1048576 // (line_len * line_len))
    row_block = 1
    while row_block * 2 <= row_limit and row_count % (row_block * 2) == 0:
        row_block = row_block * 2
    grouped = line_rows.reshape(row_count // row_block, row_block, line_len)

    def block_min(block_rows):
        return jnp.min(block_rows[:, None, :] + penalty_table[None, :, :], axis=2)

    result_rows = lax.map(block_min, grouped)
    return jnp.moveaxis(result_rows.reshape(line_shape), -1, line_axis)


def z_lines(block_lines):
    return minplus_lines(block_lines, 1, KERNEL)


def y_lines(block_lines):
    return minplus_lines(block_lines, 2, KERNEL)


def to_zlines(slab_data):
    return z_lines(lax.all_to_all(slab_data, "gz", split_axis=3, concat_axis=1, tiled=True))


def from_zlines(line_data):
    return lax.all_to_all(line_data, "gz", split_axis=1, concat_axis=3, tiled=True)


def body(levels, ct_image, region_means):
    current = levels
    for update_round in range(UPDATES):
        padded = with_halo(current, (("gz", 1), ("gy", 2)), 1)
        current = evolve(padded, ct_image, region_means)
    smoothed = minplus_lines(current, 3, KERNEL)
    slab_back = from_zlines(to_zlines(smoothed))
    y_done = y_lines(lax.all_to_all(slab_back, "gy", split_axis=3, concat_axis=2, tiled=True))
    result_field = lax.all_to_all(y_done, "gy", split_axis=2, concat_axis=3, tiled=True)
    return (current, result_field)


def solution(mesh):
    return jax.shard_map(
        body,
        mesh=mesh,
        in_specs=(P(None, "gz", "gy", None), P("gz", "gy", None), P()),
        out_specs=(P(None, "gz", "gy", None), P(None, "gz", "gy", None)),
        check_vma=False,
    )
```

profile of v0, /device:TPU:33, one launch (start us, length us, event | category | flops | bytes accessed | tf_op | source)
XLA Modules:
  0.0 327.7 jit_solution(18089065072215951858)
XLA Ops:
  1.6 3.2 collective-permute-start.1
  4.8 6.3 %collective-permute-start = (f32[4,1,8,512]{3,2,1,0:T(8,128)S(1)}, f32[4,1,8,512]{3,2,1,0:T(8,128)S(1)}, u32[]{:S(2)}, u32[]{:S(2)}) collective-permute-start(f32[4,1,8,512]{3,2,1,0:T(8,128)S(1)} %get-tuple-element.130), channel_id=1, source_target_pairs={{8,0},{16,8},{24,16},{32,24},{40,32},{48,40},{56,48},{64,56},{72,6... | collective-permute-start | bytes 196616 | tf_op jit(solution)/shard_map/ppermute | solution.py:26
  14.3 11.0 %fusion.180 = f32[1,4,8,512]{3,2,1,0:T(8,128)S(1)} fusion(f32[4,4,8,512]{3,2,1,0:T(8,128)S(1)} %get-tuple-element.133, f32[4,8,512]{2,1,0:T(8,128)} %param.10, f32[]{:T(128)} %bitcast.6, f32[]{:T(128)} %bitcast.5, f32[]{:T(128)} %bitcast.4, f32[]{:T(128)} %bitcast, f32[]{:T(128)} %bitcast.18, f32[]{:T(128)} %bitcast.16, f32[]{:T(128)} %bitcast.14, ...), kind=kLoop, calls=%fused_computation.319 | loop fusion | flops 1687552 | bytes 327744 | tf_op jit(solution)/shard_map/stack | solution.py:56
  25.3 11.0 %fusion.182 = f32[1,4,8,512]{3,2,1,0:T(8,128)S(1)} fusion(f32[4,4,8,512]{3,2,1,0:T(8,128)S(1)} %get-tuple-element.133, f32[4,8,512]{2,1,0:T(8,128)} %param.10, f32[]{:T(128)} %bitcast.18, f32[]{:T(128)} %bitcast.17, f32[]{:T(128)} %bitcast.16, f32[]{:T(128)} %bitcast.15, f32[]{:T(128)} %bitcast.14, f32[]{:T(128)} %bitcast.13, f32[]{:T(128)} %bitcast.12, ...), kind=kLoop, calls=%fused_computation.321 | loop fusion | flops 1736704 | bytes 327744 | tf_op jit(solution)/shard_map/stack | solution.py:56
  36.3 10.9 %fusion.107 = f32[1,4,8,512]{3,2,1,0:T(8,128)S(1)} fusion(f32[4,4,8,512]{3,2,1,0:T(8,128)S(1)} %get-tuple-element.133, f32[4,8,512]{2,1,0:T(8,128)} %param.10, f32[]{:T(128)} %bitcast.18, f32[]{:T(128)} %bitcast.16, f32[]{:T(128)} %bitcast.14, f32[]{:T(128)} %bitcast.12, f32[]{:T(128)} %bitcast.10, f32[]{:T(128)} %bitcast.8, f32[]{:T(128)} %bitcast.17, ...), kind=kLoop, calls=%fused_computation.154 | loop fusion | flops 1622016 | bytes 327744 | tf_op jit(solution)/shard_map/stack | solution.py:56
  50.4 8.7 %collective-permute-start.3 = (f32[4,6,1,512]{3,2,1,0:T(1,128)S(1)}, f32[4,6,1,512]{3,2,1,0:T(1,128)S(1)}, u32[]{:S(2)}, u32[]{:S(2)}) collective-permute-start(f32[4,6,1,512]{3,2,1,0:T(1,128)S(1)} %get-tuple-element.127), channel_id=1, source_target_pairs={{0,1},{1,2},{2,3},{3,4},{4,5},{5,6},{6,7},{8,9},{9,10},{10,11},{11... | collective-permute-start | bytes 147464 | tf_op jit(solution)/shard_map/ppermute | solution.py:23
  59.2 10.9 %fusion.94 = f32[1,4,8,512]{3,2,1,0:T(8,128)S(1)} fusion(f32[4,4,8,512]{3,2,1,0:T(8,128)S(1)} %get-tuple-element.133, f32[4,8,512]{2,1,0:T(8,128)} %param.10, f32[]{:T(128)} %bitcast.18, f32[]{:T(128)} %bitcast.16, f32[]{:T(128)} %bitcast.14, f32[]{:T(128)} %bitcast.12, f32[]{:T(128)} %bitcast.10, f32[]{:T(128)} %bitcast.8, f32[]{:T(128)} %bitcast.17, ...), kind=kLoop, calls=%fused_computation.140 | loop fusion | flops 1556480 | bytes 327744 | tf_op jit(solution)/shard_map/stack | solution.py:56
  72.3 10.1 %fusion.181 = f32[1,4,8,512]{3,2,1,0:T(8,128)S(1)} fusion(f32[4,4,8,512]{3,2,1,0:T(8,128)S(1)} %get-tuple-element.122, f32[4,8,512]{2,1,0:T(8,128)S(1)} %copy-done, f32[]{:T(128)} %bitcast.6, f32[]{:T(128)} %bitcast.5, f32[]{:T(128)} %bitcast.4, f32[]{:T(128)} %bitcast, f32[]{:T(128)} %bitcast.18, f32[]{:T(128)} %bitcast.16, f32[]{:T(128)} %bitcast.14, ...), kind=kLoop, calls=%fused_computation.320 | loop fusion | flops 1687552 | bytes 327744 | tf_op jit(solution)/shard_map/stack | solution.py:56
  82.5 10.1 %fusion.183 = f32[1,4,8,512]{3,2,1,0:T(8,128)S(1)} fusion(f32[4,4,8,512]{3,2,1,0:T(8,128)S(1)} %get-tuple-element.122, f32[4,8,512]{2,1,0:T(8,128)S(1)} %copy-done, f32[]{:T(128)} %bitcast.18, f32[]{:T(128)} %bitcast.17, f32[]{:T(128)} %bitcast.16, f32[]{:T(128)} %bitcast.15, f32[]{:T(128)} %bitcast.14, f32[]{:T(128)} %bitcast.13, f32[]{:T(128)} %bitcast.12, ...), kind=kLoop, calls=%fused_computation.322 | loop fusion | flops 1736704 | bytes 327744 | tf_op jit(solution)/shard_map/stack | solution.py:56
  97.9 10.1 %fusion.68 = f32[1,4,8,512]{3,2,1,0:T(8,128)S(1)} fusion(f32[4,4,8,512]{3,2,1,0:T(8,128)S(1)} %get-tuple-element.122, f32[4,8,512]{2,1,0:T(8,128)S(1)} %copy-done, f32[]{:T(128)} %bitcast.18, f32[]{:T(128)} %bitcast.16, f32[]{:T(128)} %bitcast.14, f32[]{:T(128)} %bitcast.12, f32[]{:T(128)} %bitcast.10, f32[]{:T(128)} %bitcast.8, f32[]{:T(128)} %bitcast.17, ...), kind=kLoop, calls=%fused_computation.112 | loop fusion | flops 1556480 | bytes 327744 | tf_op jit(solution)/shard_map/stack | solution.py:56
  110.0 7.5 %collective-permute-start.7 = (f32[4,6,1,512]{3,2,1,0:T(1,128)S(1)}, f32[4,6,1,512]{3,2,1,0:T(1,128)S(1)}, u32[]{:S(2)}, u32[]{:S(2)}) collective-permute-start(f32[4,6,1,512]{3,2,1,0:T(1,128)S(1)} %get-tuple-element.125), channel_id=1, source_target_pairs={{0,1},{1,2},{2,3},{3,4},{4,5},{5,6},{6,7},{8,9},{9,10},{10,11},{11... | collective-permute-start | bytes 147464 | tf_op jit(solution)/shard_map/ppermute | solution.py:23
  117.6 10.1 %fusion.81 = f32[1,4,8,512]{3,2,1,0:T(8,128)S(1)} fusion(f32[4,4,8,512]{3,2,1,0:T(8,128)S(1)} %get-tuple-element.122, f32[4,8,512]{2,1,0:T(8,128)S(1)} %copy-done, f32[]{:T(128)} %bitcast.18, f32[]{:T(128)} %bitcast.16, f32[]{:T(128)} %bitcast.14, f32[]{:T(128)} %bitcast.12, f32[]{:T(128)} %bitcast.10, f32[]{:T(128)} %bitcast.8, f32[]{:T(128)} %bitcast.17, ...), kind=kLoop, calls=%fused_computation.126 | loop fusion | flops 1622016 | bytes 327744 | tf_op jit(solution)/shard_map/stack | solution.py:56
  128.7 22.1 %while.33 = (s32[]{:T(128)}, f32[32,4,512]{2,1,0:T(4,128)S(1)}, f32[32,4,512]{2,1,0:T(4,128)S(1)}, s32[]{:T(128)}) while((s32[]{:T(128)}, f32[32,4,512]{2,1,0:T(4,128)S(1)}, f32[32,4,512]{2,1,0:T(4,128)S(1)}, s32[]{:T(128)}) %tuple.81), condition=%wide.region_2.3_spmd.clone, body=%wide.region_0.2_spmd.clone.sunk | while | flops 3667970 | bytes 2146365 | solution.py:80
  150.9 3.2 copy.52
  154.1 6.9 %reshape.25 = f32[64,1,1024]{2,1,0:T(1,128)} reshape(f32[512,4,4,8]{3,2,1,0:T(4,128)} %bitcast.459) | data formatting | bytes 524288
  161.0 9.3 %all-to-all-start = ((f32[64,1,1024]{2,1,0:T(1,128)}), f32[64,1,1024]{2,1,0:T(1,128)S(1)}, u32[]{:S(2)}, u32[]{:S(2)}) async-start(f32[64,1,1024]{2,1,0:T(1,128)} %reshape.25), calls=%async_computation | async-start | bytes 524288 | tf_op jit(solution)/shard_map/all_to_all | solution.py:93
  170.3 9.6 %all-to-all-done = f32[64,1,1024]{2,1,0:T(1,128)S(1)} async-done(((f32[64,1,1024]{2,1,0:T(1,128)}), f32[64,1,1024]{2,1,0:T(1,128)S(1)}, u32[]{:S(2)}, u32[]{:S(2)}) %all-to-all-start) | async-done | bytes 262176 | tf_op jit(solution)/shard_map/all_to_all | solution.py:93
  181.8 6.3 %reshape.26 = f32[512,4,4,8]{3,2,1,0:T(4,128)} reshape(f32[64,1024]{1,0:T(8,128)S(1)} %reduce) | data formatting | bytes 524288
  188.1 5.3 %copy.67 = f32[4,4,8,64,8]{4,2,1,3,0:T(8,128)} copy(f32[4,4,8,64,8]{2,1,0,4,3:T(4,128)} %bitcast.460) | data formatting | bytes 524288 | tf_op jit(solution)/shard_map/all_to_all | solution.py:93
  196.1 12.2 %while.34 = (s32[]{:T(128)}, f32[16,16,256]{2,1,0:T(8,128)S(1)}, f32[16,16,256]{2,1,0:T(8,128)S(1)}, s32[]{:T(128)}) while((s32[]{:T(128)}, f32[16,16,256]{2,1,0:T(8,128)S(1)}, f32[16,16,256]{2,1,0:T(8,128)S(1)}, s32[]{:T(128)}) %tuple.90), condition=%wide.region_5.6_spmd.clone, body=%wide.region_3.5_spmd.clone.sunk | while | flops 2486274 | bytes 622653 | solution.py:80
  208.3 4.3 %copy.56 = f32[4,256,8,8]{3,2,0,1:T(8,128)} copy(f32[4,256,8,8]{1,3,2,0:T(8,128)S(1)} %bitcast.470) | data formatting | bytes 524288 | tf_op jit(solution)/shard_map/transpose | solution.py:81
  212.7 3.9 %reshape.27 = f32[64,1,1024]{2,1,0:T(1,128)S(1)} reshape(f32[256,4,8,8]{3,2,1,0:T(8,128)} %bitcast.462) | data formatting | bytes 524288
  216.6 14.6 %all_to_all.72 = f32[64,1,1024]{2,1,0:T(1,128)S(1)} all-to-all(f32[64,1,1024]{2,1,0:T(1,128)S(1)} %reshape.27), channel_id=1, replica_groups=mesh['gz'=64,'gy'=8] {'gz'}, dimensions={0} | all-to-all | bytes 524288 | tf_op jit(solution)/shard_map/all_to_all | solution.py:97
  232.4 3.6 %reshape.28 = f32[256,4,8,8]{3,2,1,0:T(8,128)} reshape(f32[64,1024]{1,0:T(8,128)S(1)} %reduce.1) | data formatting | bytes 524288
  236.1 5.3 %copy.69 = f32[4,4,8,64,8]{2,1,0,4,3:T(4,128)} copy(f32[4,4,8,64,8]{4,2,0,1,3:T(8,128)} %bitcast.463) | data formatting | bytes 524288 | tf_op jit(solution)/shard_map/all_to_all | solution.py:97
  241.4 7.2 %reshape.29 = f32[8,1,8192]{2,1,0:T(1,128)} reshape(f32[512,4,4,8]{3,2,1,0:T(4,128)} %bitcast.464) | data formatting | bytes 524288
  248.6 11.0 %all-to-all-start.2 = ((f32[8,1,8192]{2,1,0:T(1,128)}), f32[8,1,8192]{2,1,0:T(1,128)S(1)}, u32[]{:S(2)}, u32[]{:S(2)}) async-start(f32[8,1,8192]{2,1,0:T(1,128)} %reshape.29), calls=%async_computation.2 | async-start | bytes 524288 | tf_op jit(solution)/shard_map/all_to_all | solution.py:107
  259.6 19.2 %all-to-all-done.2 = f32[8,1,8192]{2,1,0:T(1,128)S(1)} async-done(((f32[8,1,8192]{2,1,0:T(1,128)}), f32[8,1,8192]{2,1,0:T(1,128)S(1)}, u32[]{:S(2)}, u32[]{:S(2)}) %all-to-all-start.2) | async-done | bytes 262176 | tf_op jit(solution)/shard_map/all_to_all | solution.py:107
  280.1 6.9 %reshape.30 = f32[512,4,4,8]{3,2,1,0:T(4,128)} reshape(f32[8,8192]{1,0:T(8,128)S(1)} %reduce.2) | data formatting | bytes 524288
  287.0 3.5 %copy.71 = f32[4,4,8,8,64]{4,2,3,1,0:T(8,128)S(1)} copy(f32[4,4,8,8,64]{2,1,0,4,3:T(4,128)} %bitcast.465) | data formatting | bytes 524288 | tf_op jit(solution)/shard_map/all_to_all | solution.py:107
  291.2 5.1 %while.35 = (s32[]{:T(128)}, f32[4,256,64]{1,2,0:T(8,128)S(1)}, f32[4,256,64]{1,2,0:T(8,128)S(1)}, s32[]{:T(128)}) while((s32[]{:T(128)}, f32[4,256,64]{1,2,0:T(8,128)S(1)}, f32[4,256,64]{1,2,0:T(8,128)S(1)}, s32[]{:T(128)}) %tuple.87), condition=%wide.region_8.9_spmd.clone, body=%wide.region_6.8_spmd.clone.sunk | while | flops 2105346 | bytes 426045 | solution.py:80
  297.1 27.8 %all_to_all.73 = f32[8,1,8192]{2,1,0:T(1,128)S(1)} all-to-all(f32[8,1,8192]{2,1,0:T(1,128)S(1)} %reshape.31), channel_id=1, replica_groups=mesh['gz'=64,'gy'=8] {'gy'}, dimensions={0} | all-to-all | bytes 524288 | tf_op jit(solution)/shard_map/all_to_all | solution.py:108
  (254 shorter events, 67.0 us)
Async XLA Ops:
  0.6 71.7 %copy-start = (f32[4,8,512]{2,1,0:T(8,128)S(1)}, f32[4,8,512]{2,1,0:T(8,128)}, u32[]{:S(2)}) copy-start(f32[4,8,512]{2,1,0:T(8,128)} %param.10) | copy-start | bytes 196612
  1.6 11.5 %collective-permute-start.1 = (f32[4,1,8,512]{3,2,1,0:T(8,128)S(1)}, f32[4,1,8,512]{3,2,1,0:T(8,128)S(1)}, u32[]{:S(2)}, u32[]{:S(2)}) collective-permute-start(f32[4,1,8,512]{3,2,1,0:T(8,128)S(1)} %get-tuple-element.131), channel_id=1, source_target_pairs={{0,8},{8,16},{16,24},{24,32},{32,40},{40,48},{48,56},{56,64},{64,7... | collective-permute-start | bytes 196616 | tf_op jit(solution)/shard_map/ppermute | solution.py:23
  4.8 42.4 %collective-permute-start = (f32[4,1,8,512]{3,2,1,0:T(8,128)S(1)}, f32[4,1,8,512]{3,2,1,0:T(8,128)S(1)}, u32[]{:S(2)}, u32[]{:S(2)}) collective-permute-start(f32[4,1,8,512]{3,2,1,0:T(8,128)S(1)} %get-tuple-element.130), channel_id=1, source_target_pairs={{8,0},{16,8},{24,16},{32,24},{40,32},{48,40},{56,48},{64,56},{72,6... | collective-permute-start | bytes 196616 | tf_op jit(solution)/shard_map/ppermute | solution.py:26
  47.3 22.8 %collective-permute-start.2 = (f32[4,6,1,512]{3,2,1,0:T(1,128)S(1)}, f32[4,6,1,512]{3,2,1,0:T(1,128)S(1)}, u32[]{:S(2)}, u32[]{:S(2)}) collective-permute-start(f32[4,6,1,512]{3,2,1,0:T(1,128)S(1)} %get-tuple-element.126), channel_id=1, source_target_pairs={{1,0},{2,1},{3,2},{4,3},{5,4},{6,5},{7,6},{9,8},{10,9},{11,10},{12... | collective-permute-start | bytes 147464 | tf_op jit(solution)/shard_map/ppermute | solution.py:26
  50.4 19.7 %collective-permute-start.3 = (f32[4,6,1,512]{3,2,1,0:T(1,128)S(1)}, f32[4,6,1,512]{3,2,1,0:T(1,128)S(1)}, u32[]{:S(2)}, u32[]{:S(2)}) collective-permute-start(f32[4,6,1,512]{3,2,1,0:T(1,128)S(1)} %get-tuple-element.127), channel_id=1, source_target_pairs={{0,1},{1,2},{2,3},{3,4},{4,5},{5,6},{6,7},{8,9},{9,10},{10,11},{11... | collective-permute-start | bytes 147464 | tf_op jit(solution)/shard_map/ppermute | solution.py:23
  92.6 15.4 %collective-permute-start.4 = (f32[4,1,8,512]{3,2,1,0:T(8,128)S(1)}, f32[4,1,8,512]{3,2,1,0:T(8,128)S(1)}, u32[]{:S(2)}, u32[]{:S(2)}) collective-permute-start(f32[4,1,8,512]{3,2,1,0:T(8,128)S(1)} %get-tuple-element.129), channel_id=1, source_target_pairs={{8,0},{16,8},{24,16},{32,24},{40,32},{48,40},{56,48},{64,56},{72,6... | collective-permute-start | bytes 196616 | tf_op jit(solution)/shard_map/ppermute | solution.py:26
  94.8 13.2 %collective-permute-start.5 = (f32[4,1,8,512]{3,2,1,0:T(8,128)S(1)}, f32[4,1,8,512]{3,2,1,0:T(8,128)S(1)}, u32[]{:S(2)}, u32[]{:S(2)}) collective-permute-start(f32[4,1,8,512]{3,2,1,0:T(8,128)S(1)} %get-tuple-element.128), channel_id=1, source_target_pairs={{0,8},{8,16},{16,24},{24,32},{32,40},{40,48},{48,56},{56,64},{64,7... | collective-permute-start | bytes 196616 | tf_op jit(solution)/shard_map/ppermute | solution.py:23
  108.1 19.6 %collective-permute-start.6 = (f32[4,6,1,512]{3,2,1,0:T(1,128)S(1)}, f32[4,6,1,512]{3,2,1,0:T(1,128)S(1)}, u32[]{:S(2)}, u32[]{:S(2)}) collective-permute-start(f32[4,6,1,512]{3,2,1,0:T(1,128)S(1)} %get-tuple-element.124), channel_id=1, source_target_pairs={{1,0},{2,1},{3,2},{4,3},{5,4},{6,5},{7,6},{9,8},{10,9},{11,10},{12... | collective-permute-start | bytes 147464 | tf_op jit(solution)/shard_map/ppermute | solution.py:26
  110.0 17.7 %collective-permute-start.7 = (f32[4,6,1,512]{3,2,1,0:T(1,128)S(1)}, f32[4,6,1,512]{3,2,1,0:T(1,128)S(1)}, u32[]{:S(2)}, u32[]{:S(2)}) collective-permute-start(f32[4,6,1,512]{3,2,1,0:T(1,128)S(1)} %get-tuple-element.125), channel_id=1, source_target_pairs={{0,1},{1,2},{2,3},{3,4},{4,5},{5,6},{6,7},{8,9},{9,10},{10,11},{11... | collective-permute-start | bytes 147464 | tf_op jit(solution)/shard_map/ppermute | solution.py:23
  128.0 0.7 copy-start.1
  161.0 18.9 %all-to-all-start = ((f32[64,1,1024]{2,1,0:T(1,128)}), f32[64,1,1024]{2,1,0:T(1,128)S(1)}, u32[]{:S(2)}, u32[]{:S(2)}) async-start(f32[64,1,1024]{2,1,0:T(1,128)} %reshape.25), calls=%async_computation | async-start | bytes 524288 | tf_op jit(solution)/shard_map/all_to_all | solution.py:93
  248.6 30.2 %all-to-all-start.2 = ((f32[8,1,8192]{2,1,0:T(1,128)}), f32[8,1,8192]{2,1,0:T(1,128)S(1)}, u32[]{:S(2)}, u32[]{:S(2)}) async-start(f32[8,1,8192]{2,1,0:T(1,128)} %reshape.29), calls=%async_computation.2 | async-start | bytes 524288 | tf_op jit(solution)/shard_map/all_to_all | solution.py:107
where the time goes:
time: 330 us; the launch traced here: 328 us
  other arithmetic  130 us (39%)
  local copies, waits for them, and re-layouts  67.4 us (20%)
  starting transfers between devices  56.4 us (17%)
  blocking collectives  42.3 us (13%)
  waiting for transfers between devices  28.8 us (9%)
    another operation x8, other arithmetic, evolve(): force_all = jnp.stack(forces, axis=0)  84.3 us
    unnamed x14, local copies, waits for them, and re-layouts  36.3 us
    all_to_all x1, blocking collectives, body(): lax.all_to_all(y_done, 'gy', split_axis=2, concat_axis=3, tiled=True)  27.8 us
    reduce_min x52, other arithmetic, block_min(): return jnp.min(block_rows[:, None, :] + penalty_table[None, :, :], axis=2)  26.4 us
    ppermute x4, starting transfers between devices, with_halo(): lax.ppermute(lax.slice_in_dim(block, block.shape[dim] - width, None, axis...  22.6 us
    all_to_all x1, waiting for transfers between devices, body(): lax.all_to_all(slab_back, 'gy', split_axis=3, concat_axis=2, tiled=True)  19.2 us
    all_to_all x1, blocking collectives, from_zlines(): lax.all_to_all(line_data, 'gz', split_axis=1, concat_axis=3, tiled=True)  14.6 us
    ppermute x4, starting transfers between devices, with_halo(): lax.ppermute(lax.slice_in_dim(block, 0, width, axis=dim), axis, backward)  13.5 us
  transfers between devices with their start and end apart: 10, of which 2 were waited for; matrix products, arithmetic and copies ran while one was open for 21% of the time, Pallas kernels for 0%

commit v1 on v0

v1 whole, which is shorter than its diff:
```python
import math

import jax
import jax.numpy as jnp
from jax import lax
from jax.experimental import pallas as pl
from jax.experimental.pallas import tpu as pltpu
from jax.sharding import PartitionSpec as P

LEVELS = 4
PHASES = 16
UPDATES = 2
KERNEL = 200


PENALTY = 0.0005
STEP_SIZE = 0.5


def arctan(x):
    ax = jnp.abs(x)
    big = ax > 2.414213562373095
    mid = ax > 0.4142135623730950
    z_big = -1.0 / jnp.where(big, ax, 1.0)
    z_mid = (ax - 1.0) / (ax + 1.0)
    z = jnp.where(big, z_big, jnp.where(mid, z_mid, ax))
    base = jnp.where(big, math.pi / 2, jnp.where(mid, math.pi / 4, 0.0))
    zz = z * z
    poly = (((8.05374449538e-2 * zz - 1.38776856032e-1) * zz + 1.99777106478e-1) * zz
            - 3.33329491539e-1) * zz * z + z
    r = base + poly
    return jnp.where(x < 0, -r, r)


def evolve_kernel(means_ref, cur_ref, zlo_ref, zhi_ref, ylo_ref, yhi_ref, ct_ref, out_ref):
    nz, ny, nx = cur_ref.shape[1], cur_ref.shape[2], cur_ref.shape[3]
    shape = (ny, nx)
    xi = lax.broadcasted_iota(jnp.int32, shape, 1)
    yi = lax.broadcasted_iota(jnp.int32, shape, 0)
    xa = pltpu.roll(xi, 1, 1)
    xb = pltpu.roll(xi, nx - 1, 1)
    xa_ok = jnp.abs(xa - xi) == 1
    xb_ok = jnp.abs(xb - xi) == 1
    ya = pltpu.roll(yi, 1, 0)
    yb = pltpu.roll(yi, ny - 1, 0)
    ya_ok = jnp.abs(ya - yi) == 1
    yb_ok = jnp.abs(yb - yi) == 1
    low_row = yi == 0
    means = [means_ref[p] for p in range(PHASES)]
    for z in range(nz):
        picture = ct_ref[z]
        energy = []
        for p in range(PHASES):
            differ = picture - means[p]
            energy.append(differ * differ)
        phis, lap, g1, g0, dl = [], [], [], [], []
        for k in range(LEVELS):
            c = cur_ref[k, z]
            zm = zlo_ref[k, 0] if z == 0 else cur_ref[k, z - 1]
            zp = zhi_ref[k, 0] if z == nz - 1 else cur_ref[k, z + 1]
            edge = jnp.where(low_row, ylo_ref[k, z], yhi_ref[k, z])
            ym = jnp.where(ya_ok, pltpu.roll(c, 1, 0), edge)
            yp = jnp.where(yb_ok, pltpu.roll(c, ny - 1, 0), edge)
            xm = jnp.where(xa_ok, pltpu.roll(c, 1, 1), 0.0)
            xp = jnp.where(xb_ok, pltpu.roll(c, nx - 1, 1), 0.0)
            lap.append(zm + zp + ym + yp + xm + xp - 6.0 * c)
            h = 0.5 + arctan(c) / math.pi
            g1.append(h)
            g0.append(1.0 - h)
            dl.append(1.0 / (math.pi * (1.0 + c * c)))
            phis.append(c)
        g = (g0, g1)
        pair_lo = {(a, b): g[a][0] * g[b][1] for a in (0, 1) for b in (0, 1)}
        pair_hi = {(a, b): g[a][2] * g[b][3] for a in (0, 1) for b in (0, 1)}
        for k in range(LEVELS):
            force = None
            for q in range(PHASES // 2):
                low = q & ((1 << k) - 1)
                high = (q >> k) << (k + 1)
                p0 = high | low
                p1 = p0 | (1 << k)
                bits = [(p0 >> j) & 1 for j in range(LEVELS)]
                if k == 0:
                    prod = g[bits[1]][1] * pair_hi[(bits[2], bits[3])]
                elif k == 1:
                    prod = g[bits[0]][0] * pair_hi[(bits[2], bits[3])]
                elif k == 2:
                    prod = pair_lo[(bits[0], bits[1])] * g[bits[3]][3]
                else:
                    prod = pair_lo[(bits[0], bits[1])] * g[bits[2]][2]
                term = (energy[p1] - energy[p0]) * prod
                force = term if force is None else force + term
            out_ref[k, z] = phis[k] + STEP_SIZE * dl[k] * (lap[k] - force)


def evolve_step(current, picture, region_means):
    fwd_z = [(i, i + 1) for i in range(lax.axis_size("gz") - 1)]
    fwd_y = [(i, i + 1) for i in range(lax.axis_size("gy") - 1)]
    bwd_z = [(t, s) for s, t in fwd_z]
    bwd_y = [(t, s) for s, t in fwd_y]
    nz, ny = current.shape[1], current.shape[2]
    zlo = lax.ppermute(current[:, nz - 1:nz], "gz", fwd_z)
    zhi = lax.ppermute(current[:, 0:1], "gz", bwd_z)
    ylo = lax.ppermute(current[:, :, ny - 1:ny], "gy", fwd_y)
    yhi = lax.ppermute(current[:, :, 0:1], "gy", bwd_y)
    vmem = pl.BlockSpec(memory_space=pltpu.VMEM)
    return pl.pallas_call(
        evolve_kernel,
        out_shape=jax.ShapeDtypeStruct(current.shape, current.dtype),
        in_specs=[pl.BlockSpec(memory_space=pltpu.SMEM)] + [vmem] * 6,
        out_specs=vmem,
    )(region_means, current, zlo, zhi, ylo, yhi, picture)


def minplus_lines(field_in, line_axis, kernel_reach):
    moved_field = jnp.moveaxis(field_in, line_axis, -1)
    line_shape = moved_field.shape
    line_len = line_shape[-1]
    line_rows = moved_field.reshape(-1, line_len)
    row_count = line_rows.shape[0]
    positions = jnp.arange(line_len, dtype=jnp.float32)
    distance = positions[:, None] - positions[None, :]
    penalty_table = jnp.where(
        jnp.abs(distance) <= kernel_reach, PENALTY * (distance * distance), jnp.inf
    )
    row_limit = max(1, 1048576 // (line_len * line_len))
    row_block = 1
    while row_block * 2 <= row_limit and row_count % (row_block * 2) == 0:
        row_block = row_block * 2
    grouped = line_rows.reshape(row_count // row_block, row_block, line_len)

    def block_min(block_rows):
        return jnp.min(block_rows[:, None, :] + penalty_table[None, :, :], axis=2)

    result_rows = lax.map(block_min, grouped)
    return jnp.moveaxis(result_rows.reshape(line_shape), -1, line_axis)


def z_lines(block_lines):
    return minplus_lines(block_lines, 1, KERNEL)


def y_lines(block_lines):
    return minplus_lines(block_lines, 2, KERNEL)


def to_zlines(slab_data):
    return z_lines(lax.all_to_all(slab_data, "gz", split_axis=3, concat_axis=1, tiled=True))


def from_zlines(line_data):
    return lax.all_to_all(line_data, "gz", split_axis=1, concat_axis=3, tiled=True)


def body(levels, ct_image, region_means):
    current = levels
    for update_round in range(UPDATES):
        current = evolve_step(current, ct_image, region_means)
    smoothed = minplus_lines(current, 3, KERNEL)
    slab_back = from_zlines(to_zlines(smoothed))
    y_done = y_lines(lax.all_to_all(slab_back, "gy", split_axis=3, concat_axis=2, tiled=True))
    result_field = lax.all_to_all(y_done, "gy", split_axis=2, concat_axis=3, tiled=True)
    return (current, result_field)


def solution(mesh):
    return jax.shard_map(
        body,
        mesh=mesh,
        in_specs=(P(None, "gz", "gy", None), P("gz", "gy", None), P()),
        out_specs=(P(None, "gz", "gy", None), P(None, "gz", "gy", None)),
        check_vma=False,
    )
```

time: 330 us -> 261 us (0.79)
  the two profiles are of different devices: /device:TPU:33 before, /device:TPU:6 now
where the time goes in v1:
time: 261 us; the launch traced here: 258 us
  local copies, waits for them, and re-layouts  71.3 us (27%)
  starting transfers between devices  53.2 us (20%)
  blocking collectives  43 us (16%)
  other arithmetic  41.8 us (16%)
  waiting for transfers between devices  40.5 us (16%)
  Pallas kernels  5.18 us (2%)
    unnamed x25, local copies, waits for them, and re-layouts  38.2 us
    all_to_all x1, blocking collectives, body(): lax.all_to_all(y_done, 'gy', split_axis=2, concat_axis=3, tiled=True)  26.9 us
    reduce_min x52, other arithmetic, block_min(): return jnp.min(block_rows[:, None, :] + penalty_table[None, :, :], axis=2)  26.4 us
    all_to_all x1, waiting for transfers between devices, body(): lax.all_to_all(slab_back, 'gy', split_axis=3, concat_axis=2, tiled=True)  19.2 us
    all_to_all x1, blocking collectives, from_zlines(): lax.all_to_all(line_data, 'gz', split_axis=1, concat_axis=3, tiled=True)  16.1 us
    all_to_all x1, starting transfers between devices, body(): lax.all_to_all(slab_back, 'gy', split_axis=3, concat_axis=2, tiled=True)  15.1 us
    ppermute x2, waiting for transfers between devices, evolve_step(): yhi = lax.ppermute(current[:, :, 0:1], 'gy', bwd_y)  11.8 us
    ppermute x2, starting transfers between devices, evolve_step(): zhi = lax.ppermute(current[:, 0:1], 'gz', bwd_z)  10.5 us
  transfers between devices with their start and end apart: 10, of which 4 were waited for; matrix products, arithmetic and copies ran while one was open for 1% of the time, Pallas kernels for 0%

profile of v1, /device:TPU:6, one launch (start us, length us, event | category | flops | bytes accessed | tf_op | source)
XLA Modules:
  0.0 257.8 jit_solution(15905728767042127927)
XLA Ops:
  1.5 3.5 %collective-permute-start = (f32[4,1,8,512]{3,2,1,0:T(8,128)S(1)}, f32[4,1,8,512]{3,2,1,0:T(8,128)S(1)}, u32[]{:S(2)}, u32[]{:S(2)}) collective-permute-start(f32[4,1,8,512]{3,2,1,0:T(8,128)S(1)} %get-tuple-element.129), channel_id=1, source_target_pairs={{0,8},{8,16},{16,24},{24,32},{32,40},{40,48},{48,56},{56,64},{64,7... | collective-permute-start | bytes 196616 | tf_op jit(solution)/shard_map/ppermute | solution.py:102
  5.0 4.5 %collective-permute-start.1 = (f32[4,1,8,512]{3,2,1,0:T(8,128)S(1)}, f32[4,1,8,512]{3,2,1,0:T(8,128)S(1)}, u32[]{:S(2)}, u32[]{:S(2)}) collective-permute-start(f32[4,1,8,512]{3,2,1,0:T(8,128)S(1)} %get-tuple-element.128), channel_id=1, source_target_pairs={{8,0},{16,8},{24,16},{32,24},{40,32},{48,40},{56,48},{64,56},{72,6... | collective-permute-start | bytes 196616 | tf_op jit(solution)/shard_map/ppermute | solution.py:103
  11.9 1.3 collective-permute-start.3
  13.2 9.2 %collective-permute-done.3.yhi_ref = f32[4,4,1,512]{3,2,1,0:T(1,128)S(1)} collective-permute-done((f32[4,4,1,512]{3,2,1,0:T(1,128)S(1)}, f32[4,4,1,512]{3,2,1,0:T(1,128)S(1)}, u32[]{:S(2)}, u32[]{:S(2)}) %collective-permute-start.3) | collective-permute-done | bytes 32800 | tf_op jit(solution)/shard_map/ppermute | solution.py:105
  23.7 2.6 %shard_map.50.cur_ref = f32[4,4,8,512]{3,2,1,0:T(8,128)} custom-call(f32[16]{0:T(128)} %means_ref.3, f32[4,4,8,512]{3,2,1,0:T(8,128)} %cur_ref.1, f32[4,1,8,512]{3,2,1,0:T(8,128)} %copy-done.2, f32[4,1,8,512]{3,2,1,0:T(8,128)} %copy-done.3, f32[4,4,1,512]{3,2,1,0:T(1,128)} %copy-done.6, f32[4,4,1,512]{3,2,1,0:T(1,128)} %copy-done.7, f32[4,8,512]{2,1,0:T(8,128)} %ct_ref.3), custom_call_target="tpu_custom_call" | custom-call | tf_op jit(solution)/shard_map/pallas_call | solution.py:107
  27.2 1.9 collective-permute-start.4
  29.1 6.0 %collective-permute-start.5 = (f32[4,1,8,512]{3,2,1,0:T(8,128)S(1)}, f32[4,1,8,512]{3,2,1,0:T(8,128)S(1)}, u32[]{:S(2)}, u32[]{:S(2)}) collective-permute-start(f32[4,1,8,512]{3,2,1,0:T(8,128)S(1)} %get-tuple-element.124), channel_id=1, source_target_pairs={{8,0},{16,8},{24,16},{32,24},{40,32},{48,40},{56,48},{64,56},{72,6... | collective-permute-start | bytes 196616 | tf_op jit(solution)/shard_map/ppermute | solution.py:103
  36.2 7.9 %collective-permute-start.6 = (f32[4,4,1,512]{3,2,1,0:T(1,128)S(1)}, f32[4,4,1,512]{3,2,1,0:T(1,128)S(1)}, u32[]{:S(2)}, u32[]{:S(2)}) collective-permute-start(f32[4,4,1,512]{3,2,1,0:T(1,128)S(1)} %get-tuple-element.123), channel_id=1, source_target_pairs={{0,1},{1,2},{2,3},{3,4},{4,5},{5,6},{6,7},{8,9},{9,10},{10,11},{11... | collective-permute-start | bytes 98312 | tf_op jit(solution)/shard_map/ppermute | solution.py:104
  44.1 1.3 collective-permute-start.7
  45.4 2.6 %collective-permute-done.7.yhi_ref = f32[4,4,1,512]{3,2,1,0:T(1,128)S(1)} collective-permute-done((f32[4,4,1,512]{3,2,1,0:T(1,128)S(1)}, f32[4,4,1,512]{3,2,1,0:T(1,128)S(1)}, u32[]{:S(2)}, u32[]{:S(2)}) %collective-permute-start.7) | collective-permute-done | bytes 32800 | tf_op jit(solution)/shard_map/ppermute | solution.py:105
  49.3 2.6 %shard_map.51 = f32[4,4,8,512]{3,2,1,0:T(8,128)} custom-call(f32[16]{0:T(128)} %means_ref.3, f32[4,4,8,512]{3,2,1,0:T(8,128)} %shard_map.50.cur_ref, f32[4,1,8,512]{3,2,1,0:T(8,128)} %copy-done, f32[4,1,8,512]{3,2,1,0:T(8,128)} %copy-done.1, f32[4,4,1,512]{3,2,1,0:T(1,128)} %copy-done.4, f32[4,4,1,512]{3,2,1,0:T(1,128)} %copy-done.5, f32[4,8,512]{2,1,0:T(8,128)} %ct_ref.3), custom_call_target="tpu_custom_call" | custom-call | tf_op jit(solution)/shard_map/pallas_call | solution.py:107
  52.9 22.1 %while.33 = (s32[]{:T(128)}, f32[32,4,512]{2,1,0:T(4,128)S(1)}, f32[32,4,512]{2,1,0:T(4,128)S(1)}, s32[]{:T(128)}) while((s32[]{:T(128)}, f32[32,4,512]{2,1,0:T(4,128)S(1)}, f32[32,4,512]{2,1,0:T(4,128)S(1)}, s32[]{:T(128)}) %tuple.64), condition=%wide.region_2.3_spmd.clone, body=%wide.region_0.2_spmd.clone.sunk | while | flops 3667970 | bytes 2146365 | solution.py:135
  75.1 3.3 %copy.52 = f32[4,4,8,512]{2,1,0,3:T(4,128)} copy(f32[4,4,8,512]{3,2,1,0:T(8,128)S(1)} %reshape.22) | data formatting | bytes 524288 | tf_op jit(solution)/shard_map/reshape | solution.py:136
  78.4 6.9 %reshape.25 = f32[64,1,1024]{2,1,0:T(1,128)} reshape(f32[512,4,4,8]{3,2,1,0:T(4,128)} %bitcast.71) | data formatting | bytes 524288
  85.3 10.4 %all-to-all-start = ((f32[64,1,1024]{2,1,0:T(1,128)}), f32[64,1,1024]{2,1,0:T(1,128)S(1)}, u32[]{:S(2)}, u32[]{:S(2)}) async-start(f32[64,1,1024]{2,1,0:T(1,128)} %reshape.25), calls=%async_computation | async-start | bytes 524288 | tf_op jit(solution)/shard_map/all_to_all | solution.py:148
  95.7 9.5 %all-to-all-done = f32[64,1,1024]{2,1,0:T(1,128)S(1)} async-done(((f32[64,1,1024]{2,1,0:T(1,128)}), f32[64,1,1024]{2,1,0:T(1,128)S(1)}, u32[]{:S(2)}, u32[]{:S(2)}) %all-to-all-start) | async-done | bytes 262176 | tf_op jit(solution)/shard_map/all_to_all | solution.py:148
  107.1 6.3 %reshape.26 = f32[512,4,4,8]{3,2,1,0:T(4,128)} reshape(f32[64,1024]{1,0:T(8,128)S(1)} %reduce) | data formatting | bytes 524288
  113.4 5.3 %copy.67 = f32[4,4,8,64,8]{4,2,1,3,0:T(8,128)} copy(f32[4,4,8,64,8]{2,1,0,4,3:T(4,128)} %bitcast.72) | data formatting | bytes 524288 | tf_op jit(solution)/shard_map/all_to_all | solution.py:148
  118.6 2.8 %copy.55 = f32[4,8,8,256]{3,2,1,0:T(8,128)S(1)} copy(f32[4,8,8,256]{2,1,3,0:T(8,128)} %bitcast.73) | data formatting | bytes 524288 | tf_op jit(solution)/shard_map/transpose | solution.py:116
  121.4 12.2 %while.34 = (s32[]{:T(128)}, f32[16,16,256]{2,1,0:T(8,128)S(1)}, f32[16,16,256]{2,1,0:T(8,128)S(1)}, s32[]{:T(128)}) while((s32[]{:T(128)}, f32[16,16,256]{2,1,0:T(8,128)S(1)}, f32[16,16,256]{2,1,0:T(8,128)S(1)}, s32[]{:T(128)}) %tuple.73), condition=%wide.region_5.6_spmd.clone, body=%wide.region_3.5_spmd.clone.sunk | while | flops 2486274 | bytes 622653 | solution.py:135
  133.7 4.3 %copy.56 = f32[4,256,8,8]{3,2,0,1:T(8,128)} copy(f32[4,256,8,8]{1,3,2,0:T(8,128)S(1)} %bitcast.82) | data formatting | bytes 524288 | tf_op jit(solution)/shard_map/transpose | solution.py:136
  138.0 3.9 %reshape.27 = f32[64,1,1024]{2,1,0:T(1,128)S(1)} reshape(f32[256,4,8,8]{3,2,1,0:T(8,128)} %bitcast.74) | data formatting | bytes 524288
  141.9 16.1 %all_to_all.72 = f32[64,1,1024]{2,1,0:T(1,128)S(1)} all-to-all(f32[64,1,1024]{2,1,0:T(1,128)S(1)} %reshape.27), channel_id=1, replica_groups=mesh['gz'=64,'gy'=8] {'gz'}, dimensions={0} | all-to-all | bytes 524288 | tf_op jit(solution)/shard_map/all_to_all | solution.py:152
  159.3 3.6 %reshape.28 = f32[256,4,8,8]{3,2,1,0:T(8,128)} reshape(f32[64,1024]{1,0:T(8,128)S(1)} %reduce.1) | data formatting | bytes 524288
  162.9 5.3 %copy.69 = f32[4,4,8,64,8]{2,1,0,4,3:T(4,128)} copy(f32[4,4,8,64,8]{4,2,0,1,3:T(8,128)} %bitcast.75) | data formatting | bytes 524288 | tf_op jit(solution)/shard_map/all_to_all | solution.py:152
  168.3 7.2 %reshape.29 = f32[8,1,8192]{2,1,0:T(1,128)} reshape(f32[512,4,4,8]{3,2,1,0:T(4,128)} %bitcast.76) | data formatting | bytes 524288
  175.4 15.1 %all-to-all-start.2 = ((f32[8,1,8192]{2,1,0:T(1,128)}), f32[8,1,8192]{2,1,0:T(1,128)S(1)}, u32[]{:S(2)}, u32[]{:S(2)}) async-start(f32[8,1,8192]{2,1,0:T(1,128)} %reshape.29), calls=%async_computation.2 | async-start | bytes 524288 | tf_op jit(solution)/shard_map/all_to_all | solution.py:161
  190.5 19.2 %all-to-all-done.2 = f32[8,1,8192]{2,1,0:T(1,128)S(1)} async-done(((f32[8,1,8192]{2,1,0:T(1,128)}), f32[8,1,8192]{2,1,0:T(1,128)S(1)}, u32[]{:S(2)}, u32[]{:S(2)}) %all-to-all-start.2) | async-done | bytes 262176 | tf_op jit(solution)/shard_map/all_to_all | solution.py:161
  211.1 6.9 %reshape.30 = f32[512,4,4,8]{3,2,1,0:T(4,128)} reshape(f32[8,8192]{1,0:T(8,128)S(1)} %reduce.2) | data formatting | bytes 524288
  218.0 3.5 %copy.71 = f32[4,4,8,8,64]{4,2,3,1,0:T(8,128)S(1)} copy(f32[4,4,8,8,64]{2,1,0,4,3:T(4,128)} %bitcast.77) | data formatting | bytes 524288 | tf_op jit(solution)/shard_map/all_to_all | solution.py:161
  222.2 5.1 %while.35 = (s32[]{:T(128)}, f32[4,256,64]{1,2,0:T(8,128)S(1)}, f32[4,256,64]{1,2,0:T(8,128)S(1)}, s32[]{:T(128)}) while((s32[]{:T(128)}, f32[4,256,64]{1,2,0:T(8,128)S(1)}, f32[4,256,64]{1,2,0:T(8,128)S(1)}, s32[]{:T(128)}) %tuple.70), condition=%wide.region_8.9_spmd.clone, body=%wide.region_6.8_spmd.clone.sunk | while | flops 2105346 | bytes 426045 | solution.py:135
  228.1 26.9 %all_to_all.73 = f32[8,1,8192]{2,1,0:T(1,128)S(1)} all-to-all(f32[8,1,8192]{2,1,0:T(1,128)S(1)} %reshape.31), channel_id=1, replica_groups=mesh['gz'=64,'gy'=8] {'gy'}, dimensions={0} | all-to-all | bytes 524288 | tf_op jit(solution)/shard_map/all_to_all | solution.py:162
  (254 shorter events, 55.2 us)
Async XLA Ops:
  1.5 20.9 %collective-permute-start = (f32[4,1,8,512]{3,2,1,0:T(8,128)S(1)}, f32[4,1,8,512]{3,2,1,0:T(8,128)S(1)}, u32[]{:S(2)}, u32[]{:S(2)}) collective-permute-start(f32[4,1,8,512]{3,2,1,0:T(8,128)S(1)} %get-tuple-element.129), channel_id=1, source_target_pairs={{0,8},{8,16},{16,24},{24,32},{32,40},{40,48},{48,56},{56,64},{64,7... | collective-permute-start | bytes 196616 | tf_op jit(solution)/shard_map/ppermute | solution.py:102
  5.0 17.4 %collective-permute-start.1 = (f32[4,1,8,512]{3,2,1,0:T(8,128)S(1)}, f32[4,1,8,512]{3,2,1,0:T(8,128)S(1)}, u32[]{:S(2)}, u32[]{:S(2)}) collective-permute-start(f32[4,1,8,512]{3,2,1,0:T(8,128)S(1)} %get-tuple-element.128), channel_id=1, source_target_pairs={{8,0},{16,8},{24,16},{32,24},{40,32},{48,40},{56,48},{64,56},{72,6... | collective-permute-start | bytes 196616 | tf_op jit(solution)/shard_map/ppermute | solution.py:103
  10.6 2.6 %collective-permute-start.2 = (f32[4,4,1,512]{3,2,1,0:T(1,128)S(1)}, f32[4,4,1,512]{3,2,1,0:T(1,128)S(1)}, u32[]{:S(2)}, u32[]{:S(2)}) collective-permute-start(f32[4,4,1,512]{3,2,1,0:T(1,128)S(1)} %get-tuple-element.127), channel_id=1, source_target_pairs={{0,1},{1,2},{2,3},{3,4},{4,5},{5,6},{6,7},{8,9},{9,10},{10,11},{11... | collective-permute-start | bytes 98312 | tf_op jit(solution)/shard_map/ppermute | solution.py:104
  11.9 10.5 %collective-permute-start.3 = (f32[4,4,1,512]{3,2,1,0:T(1,128)S(1)}, f32[4,4,1,512]{3,2,1,0:T(1,128)S(1)}, u32[]{:S(2)}, u32[]{:S(2)}) collective-permute-start(f32[4,4,1,512]{3,2,1,0:T(1,128)S(1)} %get-tuple-element.126), channel_id=1, source_target_pairs={{1,0},{2,1},{3,2},{4,3},{5,4},{6,5},{7,6},{9,8},{10,9},{11,10},{12... | collective-permute-start | bytes 98312 | tf_op jit(solution)/shard_map/ppermute | solution.py:105
  13.2 9.2 %copy-start.6 = (f32[4,4,1,512]{3,2,1,0:T(1,128)}, f32[4,4,1,512]{3,2,1,0:T(1,128)S(1)}, u32[]{:S(2)}) copy-start(f32[4,4,1,512]{3,2,1,0:T(1,128)S(1)} %collective-permute-done.2.ylo_ref) | copy-start | bytes 98308
  22.4 0.6 copy-start.7
  22.4 0.6 copy-start.2
  23.1 0.6 copy-start.3
  27.2 20.9 %collective-permute-start.4 = (f32[4,1,8,512]{3,2,1,0:T(8,128)S(1)}, f32[4,1,8,512]{3,2,1,0:T(8,128)S(1)}, u32[]{:S(2)}, u32[]{:S(2)}) collective-permute-start(f32[4,1,8,512]{3,2,1,0:T(8,128)S(1)} %get-tuple-element.125), channel_id=1, source_target_pairs={{0,8},{8,16},{16,24},{24,32},{32,40},{40,48},{48,56},{56,64},{64,7... | collective-permute-start | bytes 196616 | tf_op jit(solution)/shard_map/ppermute | solution.py:102
  29.1 19.0 %collective-permute-start.5 = (f32[4,1,8,512]{3,2,1,0:T(8,128)S(1)}, f32[4,1,8,512]{3,2,1,0:T(8,128)S(1)}, u32[]{:S(2)}, u32[]{:S(2)}) collective-permute-start(f32[4,1,8,512]{3,2,1,0:T(8,128)S(1)} %get-tuple-element.124), channel_id=1, source_target_pairs={{8,0},{16,8},{24,16},{32,24},{40,32},{48,40},{56,48},{64,56},{72,6... | collective-permute-start | bytes 196616 | tf_op jit(solution)/shard_map/ppermute | solution.py:103
  36.2 9.2 %collective-permute-start.6 = (f32[4,4,1,512]{3,2,1,0:T(1,128)S(1)}, f32[4,4,1,512]{3,2,1,0:T(1,128)S(1)}, u32[]{:S(2)}, u32[]{:S(2)}) collective-permute-start(f32[4,4,1,512]{3,2,1,0:T(1,128)S(1)} %get-tuple-element.123), channel_id=1, source_target_pairs={{0,1},{1,2},{2,3},{3,4},{4,5},{5,6},{6,7},{8,9},{9,10},{10,11},{11... | collective-permute-start | bytes 98312 | tf_op jit(solution)/shard_map/ppermute | solution.py:104
  44.1 3.9 %collective-permute-start.7 = (f32[4,4,1,512]{3,2,1,0:T(1,128)S(1)}, f32[4,4,1,512]{3,2,1,0:T(1,128)S(1)}, u32[]{:S(2)}, u32[]{:S(2)}) collective-permute-start(f32[4,4,1,512]{3,2,1,0:T(1,128)S(1)} %get-tuple-element.122), channel_id=1, source_target_pairs={{1,0},{2,1},{3,2},{4,3},{5,4},{6,5},{7,6},{9,8},{10,9},{11,10},{12... | collective-permute-start | bytes 98312 | tf_op jit(solution)/shard_map/ppermute | solution.py:105
  45.4 2.6 %copy-start.4 = (f32[4,4,1,512]{3,2,1,0:T(1,128)}, f32[4,4,1,512]{3,2,1,0:T(1,128)S(1)}, u32[]{:S(2)}) copy-start(f32[4,4,1,512]{3,2,1,0:T(1,128)S(1)} %collective-permute-done.6.ylo_ref) | copy-start | bytes 98308
  48.0 0.6 copy-start.5
  48.1 0.6 copy-start
  48.7 0.6 copy-start.1
  85.3 19.9 %all-to-all-start = ((f32[64,1,1024]{2,1,0:T(1,128)}), f32[64,1,1024]{2,1,0:T(1,128)S(1)}, u32[]{:S(2)}, u32[]{:S(2)}) async-start(f32[64,1,1024]{2,1,0:T(1,128)} %reshape.25), calls=%async_computation | async-start | bytes 524288 | tf_op jit(solution)/shard_map/all_to_all | solution.py:148
  175.4 34.3 %all-to-all-start.2 = ((f32[8,1,8192]{2,1,0:T(1,128)}), f32[8,1,8192]{2,1,0:T(1,128)S(1)}, u32[]{:S(2)}, u32[]{:S(2)}) async-start(f32[8,1,8192]{2,1,0:T(1,128)} %reshape.29), calls=%async_computation.2 | async-start | bytes 524288 | tf_op jit(solution)/shard_map/all_to_all | solution.py:161

commit v2 on v1

--- a/solution.py
+++ b/solution.py
@@ -112,55 +112,172 @@
     )(region_means, current, zlo, zhi, ylo, yhi, picture)
 
 
-def minplus_lines(field_in, line_axis, kernel_reach):
-    moved_field = jnp.moveaxis(field_in, line_axis, -1)
-    line_shape = moved_field.shape
-    line_len = line_shape[-1]
-    line_rows = moved_field.reshape(-1, line_len)
-    row_count = line_rows.shape[0]
-    positions = jnp.arange(line_len, dtype=jnp.float32)
-    distance = positions[:, None] - positions[None, :]
-    penalty_table = jnp.where(
-        jnp.abs(distance) <= kernel_reach, PENALTY * (distance * distance), jnp.inf
-    )
-    row_limit = max(1, 1048576 // (line_len * line_len))
-    row_block = 1
-    while row_block * 2 <= row_limit and row_count % (row_block * 2) == 0:
-        row_block = row_block * 2
-    grouped = line_rows.reshape(row_count // row_block, row_block, line_len)
-
-    def block_min(block_rows):
-        return jnp.min(block_rows[:, None, :] + penalty_table[None, :, :], axis=2)
-
-    result_rows = lax.map(block_min, grouped)
-    return jnp.moveaxis(result_rows.reshape(line_shape), -1, line_axis)
-
-
-def z_lines(block_lines):
-    return minplus_lines(block_lines, 1, KERNEL)
-
-
-def y_lines(block_lines):
-    return minplus_lines(block_lines, 2, KERNEL)
-
-
-def to_zlines(slab_data):
-    return z_lines(lax.all_to_all(slab_data, "gz", split_axis=3, concat_axis=1, tiled=True))
-
-
-def from_zlines(line_data):
-    return lax.all_to_all(line_data, "gz", split_axis=1, concat_axis=3, tiled=True)
+def penalty_table(count, offset):
+    distance = (jnp.arange(count, dtype=jnp.int32) - offset).astype(jnp.float32)
+    return jnp.where(
+        jnp.abs(distance) <= KERNEL, PENALTY * (distance * distance), jnp.inf
+    ).astype(jnp.float32)
+
+
+def scan_offsets(u_ref, pen_ref, out_ref, n_out, group, nrot, q_range):
+    for g0 in range(0, n_out, group):
+        q_lo, q_hi = q_range(g0, group)
+        q_hi = min(q_hi, pen_ref.shape[0] // nrot - 1, u_ref.shape[1] - g0 - group)
+
+        def body(q, acc, g0=g0):
+            for r in range(nrot):
+                vals = u_ref[r, pl.ds(g0 + q, group)]
+                acc = jnp.minimum(acc, vals + pen_ref[q * nrot + r])
+            return acc
+
+        init = jnp.full((group,) + tuple(out_ref.shape[1:]), jnp.inf, jnp.float32)
+        out_ref[g0:g0 + group] = lax.fori_loop(q_lo, q_hi + 1, body, init)
+
+
+def build_rotations(v_ref, u_ref, nrot, pick):
+    def body(b, carry):
+        here = v_ref[b]
+        after = v_ref[b + 1]
+        for r in range(nrot):
+            u_ref[r, b] = pick(r, here, after)
+        return carry
+
+    lax.fori_loop(0, u_ref.shape[1], body, 0)
+
+
+def xpass_kernel(pen_ref, src_ref, out_ref, pad_ref, u_ref):
+    lines, nx = src_ref.shape
+    reach = KERNEL
+    pad_ref[...] = jnp.full(pad_ref.shape, jnp.inf, jnp.float32)
+    pad_ref[reach:reach + nx, :] = src_ref[...].T
+    sub = lax.broadcasted_iota(jnp.int32, (8, lines), 0)
+
+    def body(b, carry):
+        here = pad_ref[pl.ds(pl.multiple_of(b * 8, 8), 8), :]
+        after = pad_ref[pl.ds(pl.multiple_of(b * 8 + 8, 8), 8), :]
+        u_ref[0, b] = here
+        for r in range(1, 8):
+            u_ref[r, b] = jnp.where(sub < 8 - r, pltpu.roll(here, 8 - r, 0), pltpu.roll(after, 8 - r, 0))
+        return carry
+
+    lax.fori_loop(0, u_ref.shape[1], body, 0)
+    n_out = nx // 8
+
+    def q_range(g0, group):
+        lo = max(0, -((8 * (g0 + group - 1) + 14 - reach) // 8))
+        hi = (reach + nx - 1 - 8 * g0) // 8
+        return lo, hi
+
+    scan_offsets(u_ref, pen_ref, out_ref, n_out, 16, 8, q_range)
+
+
+def zpass_kernel(pen_ref, src_ref, out_ref, pad_ref, u_ref):
+    n_out = src_ref.shape[0]
+    padc = KERNEL // 4
+    pad_ref[...] = jnp.full(pad_ref.shape, jnp.inf, jnp.float32)
+    pad_ref[padc:padc + n_out] = src_ref[...]
+    lane = lax.broadcasted_iota(jnp.int32, src_ref.shape[1:], 1)
+    sub_z = (lane // 8) % 4
+
+    def body(b, carry):
+        here = pad_ref[b]
+        after = pad_ref[b + 1]
+        u_ref[0, b] = here
+        for r in range(1, 4):
+            u_ref[r, b] = jnp.where(sub_z + r < 4, pltpu.roll(here, 128 - 8 * r, 1),
+                                    pltpu.roll(after, 32 - 8 * r, 1))
+        return carry
+
+    lax.fori_loop(0, u_ref.shape[1], body, 0)
+
+    def q_range(g0, group):
+        lo = max(0, padc - 1 - (g0 + group - 1))
+        hi = padc + n_out - 1 - g0
+        return lo, hi
+
+    scan_offsets(u_ref, pen_ref, out_ref, n_out, 16, 4, q_range)
+
+
+def ypass_kernel(pen_ref, src_ref, out_ref, pad_ref, u_ref):
+    n_out = src_ref.shape[0]
+    padc = n_out
+    pad_ref[...] = jnp.full(pad_ref.shape, jnp.inf, jnp.float32)
+    pad_ref[padc:padc + n_out] = src_ref[...]
+    lane = lax.broadcasted_iota(jnp.int32, src_ref.shape[1:], 2)
+    sub_y = lane % 8
+
+    def body(b, carry):
+        here = pad_ref[b]
+        after = pad_ref[b + 1]
+        u_ref[0, b] = here
+        for r in range(1, 8):
+            u_ref[r, b] = jnp.where(sub_y + r < 8, pltpu.roll(here, 128 - r, 2),
+                                    pltpu.roll(after, 8 - r, 2))
+        return carry
+
+    lax.fori_loop(0, u_ref.shape[1], body, 0)
+
+    def q_range(g0, group):
+        lo = max(0, padc - 1 - (g0 + group - 1))
+        hi = padc + n_out - 1 - g0
+        return lo, hi
+
+    scan_offsets(u_ref, pen_ref, out_ref, n_out, 1, 8, q_range)
+
+
+def transpose_kernel(src_ref, out_ref):
+    out_ref[...] = src_ref[...].T
+
+
+def local_call(kernel, out_shape, scratch, *args):
+    vmem = pl.BlockSpec(memory_space=pltpu.VMEM)
+    smem = pl.BlockSpec(memory_space=pltpu.SMEM)
+    specs = [smem if a.ndim == 1 else vmem for a in args]
+    return pl.pallas_call(
+        kernel,
+        out_shape=jax.ShapeDtypeStruct(out_shape, jnp.float32),
+        in_specs=specs,
+        out_specs=vmem,
+        scratch_shapes=[pltpu.VMEM(s, jnp.float32) for s in scratch],
+    )(*args)
+
+
+def regularize(current):
+    levels, nz, ny, nx = current.shape
+    lines = levels * nz * ny
+    assert lines == 128 and nx % 8 == 0
+    n_gz = lax.axis_size("gz")
+    n_gy = lax.axis_size("gy")
+    xq = (KERNEL + 7) // 8
+    nxo = nx // 8
+    pen_x = penalty_table(8 * (xq * 2 + 2), KERNEL)
+    xpad_rows = 8 * (nxo + 2 * xq + 3)
+    t1 = local_call(xpass_kernel, (nxo, 8, lines), [(xpad_rows, lines), (8, nxo + 2 * xq + 2, 8, lines)],
+                    pen_x, current.reshape(lines, nx))
+    assert nxo == n_gz
+    r1 = lax.all_to_all(t1, "gz", 0, 0, tiled=True)
+    nzo = n_gz
+    zq = KERNEL // 4
+    pen_z = penalty_table(4 * (2 * zq + 2), KERNEL)
+    t2 = local_call(zpass_kernel, r1.shape, [(nzo + 2 * zq + 3, 8, lines), (4, nzo + 2 * zq + 2, 8, lines)],
+                    pen_z, r1)
+    r2 = lax.all_to_all(t2, "gz", 0, 0, tiled=True)
+    t3 = r2.reshape(n_gy, nxo // n_gy, 8, lines)
+    r3 = lax.all_to_all(t3, "gy", 0, 0, tiled=True)
+    nyo = n_gy
+    pen_y = penalty_table(8 * (2 * nyo), 8 * nyo)
+    t4 = local_call(ypass_kernel, r3.shape, [(3 * nyo + 1,) + r3.shape[1:], (8, 2 * nyo) + r3.shape[1:]],
+                    pen_y, r3)
+    r4 = lax.all_to_all(t4, "gy", 0, 0, tiled=True)
+    out = local_call(transpose_kernel, (lines, nx), [], r4.reshape(nx, lines))
+    return out.reshape(current.shape)
 
 
 def body(levels, ct_image, region_means):
     current = levels
     for update_round in range(UPDATES):
         current = evolve_step(current, ct_image, region_means)
-    smoothed = minplus_lines(current, 3, KERNEL)
-    slab_back = from_zlines(to_zlines(smoothed))
-    y_done = y_lines(lax.all_to_all(slab_back, "gy", split_axis=3, concat_axis=2, tiled=True))
-    result_field = lax.all_to_all(y_done, "gy", split_axis=2, concat_axis=3, tiled=True)
-    return (current, result_field)
+    return (current, regularize(current))
 
 
 def solution(mesh):

time: 261 us -> 195 us (0.75)
  local copies, waits for them, and re-layouts: 71.3 us -> 7.84 us
  other arithmetic: 41.8 us -> 1.73 us
  Pallas kernels: 5.18 us -> 45.2 us
    pallas_call x0 -> x4, Pallas kernels: none -> 40 us  [local_call(): pl.pallas_call(kernel, out_shape=jax.ShapeDtypeStruct(out_shape, jnp.floa...]
    unnamed x25 -> x20, local copies, waits for them, and re-layouts: 38.2 us -> 3.87 us
    reduce_min x52 -> x0, other arithmetic: 26.4 us -> none  [block_min(): return jnp.min(block_rows[:, None, :] + penalty_table[None, :, :], axis=2)]
    all_to_all x7 -> x0, local copies, waits for them, and re-layouts: 15.8 us -> none  [the longest x2 5.85 us: to_zlines(): lax.all_to_all(slab_data, 'gz', split_axis=3, concat_axis=1, tiled=True)]
    select_n x52 -> x3, other arithmetic: 10.3 us -> 1.73 us  [penalty_table(): jnp.where(jnp.abs(distance) <= KERNEL, PENALTY * (distance * distance), j...]
    transpose x3 -> x0, local copies, waits for them, and re-layouts: 7.47 us -> none  [the longest x1 4.34 us: minplus_lines(): return jnp.moveaxis(result_rows.reshape(line_shape), -1, line_axis)]
    all_to_all x4 -> x0, other arithmetic: 5.14 us -> none  [the longest x1 1.29 us: body(): lax.all_to_all(slab_back, 'gy', split_axis=3, concat_axis=2, tiled=True)]
    reshape x3 -> x0, local copies, waits for them, and re-layouts: 3.59 us -> none  [minplus_lines(): return jnp.moveaxis(result_rows.reshape(line_shape), -1, line_axis)]
where the time goes in v2:
time: 195 us; the launch traced here: 192 us
  starting transfers between devices  52.9 us (27%)
  Pallas kernels  45.2 us (23%)
  blocking collectives  44.9 us (23%)
  waiting for transfers between devices  38.8 us (20%)
  local copies, waits for them, and re-layouts  7.84 us (4%)
    pallas_call x4, Pallas kernels, local_call(): pl.pallas_call(kernel, out_shape=jax.ShapeDtypeStruct(out_shape, jnp.floa...  40 us
    all_to_all x1, blocking collectives, regularize(): r4 = lax.all_to_all(t4, 'gy', 0, 0, tiled=True)  27.7 us
    all_to_all x1, waiting for transfers between devices, regularize(): r3 = lax.all_to_all(t3, 'gy', 0, 0, tiled=True)  18.6 us
    all_to_all x1, blocking collectives, regularize(): r2 = lax.all_to_all(t2, 'gz', 0, 0, tiled=True)  17.2 us
    all_to_all x1, starting transfers between devices, regularize(): r3 = lax.all_to_all(t3, 'gy', 0, 0, tiled=True)  14.8 us
    ppermute x2, waiting for transfers between devices, evolve_step(): yhi = lax.ppermute(current[:, :, 0:1], 'gy', bwd_y)  11.2 us
    ppermute x2, starting transfers between devices, evolve_step(): zhi = lax.ppermute(current[:, 0:1], 'gz', bwd_z)  10.5 us
    all_to_all x1, starting transfers between devices, regularize(): r1 = lax.all_to_all(t1, 'gz', 0, 0, tiled=True)  10.4 us
  transfers between devices with their start and end apart: 10, of which 4 were waited for; matrix products, arithmetic and copies ran while one was open for 1% of the time, Pallas kernels for 0%

profile of v2, /device:TPU:6, one launch (start us, length us, event | category | flops | bytes accessed | tf_op | source)
XLA Modules:
  0.0 192.2 jit_solution(13993557344574681312)
XLA Ops:
  0.6 0.9 fusion.3
  1.5 3.5 %collective-permute-start = (f32[4,1,8,512]{3,2,1,0:T(8,128)S(1)}, f32[4,1,8,512]{3,2,1,0:T(8,128)S(1)}, u32[]{:S(2)}, u32[]{:S(2)}) collective-permute-start(f32[4,1,8,512]{3,2,1,0:T(8,128)S(1)} %get-tuple-element.9), channel_id=1, source_target_pairs={{0,8},{8,16},{16,24},{24,32},{32,40},{40,48},{48,56},{56,64},{64,7... | collective-permute-start | bytes 196616 | tf_op jit(solution)/shard_map/ppermute | solution.py:102
  5.0 4.5 %collective-permute-start.1 = (f32[4,1,8,512]{3,2,1,0:T(8,128)S(1)}, f32[4,1,8,512]{3,2,1,0:T(8,128)S(1)}, u32[]{:S(2)}, u32[]{:S(2)}) collective-permute-start(f32[4,1,8,512]{3,2,1,0:T(8,128)S(1)} %get-tuple-element.8), channel_id=1, source_target_pairs={{8,0},{16,8},{24,16},{32,24},{40,32},{48,40},{56,48},{64,56},{72,6... | collective-permute-start | bytes 196616 | tf_op jit(solution)/shard_map/ppermute | solution.py:103
  9.5 1.1 fusion.2
  10.6 1.3 collective-permute-start.2
  11.9 1.3 collective-permute-start.3
  13.2 9.2 %collective-permute-done.3.yhi_ref = f32[4,4,1,512]{3,2,1,0:T(1,128)S(1)} collective-permute-done((f32[4,4,1,512]{3,2,1,0:T(1,128)S(1)}, f32[4,4,1,512]{3,2,1,0:T(1,128)S(1)}, u32[]{:S(2)}, u32[]{:S(2)}) %collective-permute-start.3) | collective-permute-done | bytes 32800 | tf_op jit(solution)/shard_map/ppermute | solution.py:105
  22.4 0.6 copy-done.9
  23.0 0.6 copy-done.4
  23.7 2.6 %shard_map.50.cur_ref = f32[4,4,8,512]{3,2,1,0:T(8,128)} custom-call(f32[16]{0:T(128)} %means_ref.3, f32[4,4,8,512]{3,2,1,0:T(8,128)} %cur_ref.1, f32[4,1,8,512]{3,2,1,0:T(8,128)} %copy-done.2, f32[4,1,8,512]{3,2,1,0:T(8,128)} %copy-done.4, f32[4,4,1,512]{3,2,1,0:T(1,128)} %copy-done.7, f32[4,4,1,512]{3,2,1,0:T(1,128)} %copy-done.9, f32[4,8,512]{2,1,0:T(8,128)} %ct_ref.3), custom_call_target="tpu_custom_call" | custom-call | tf_op jit(solution)/shard_map/pallas_call | solution.py:107
  26.2 0.9 fusion.1
  27.1 1.1 fusion
  28.3 1.9 collective-permute-start.4
  30.2 6.0 %collective-permute-start.5 = (f32[4,1,8,512]{3,2,1,0:T(8,128)S(1)}, f32[4,1,8,512]{3,2,1,0:T(8,128)S(1)}, u32[]{:S(2)}, u32[]{:S(2)}) collective-permute-start(f32[4,1,8,512]{3,2,1,0:T(8,128)S(1)} %get-tuple-element.4), channel_id=1, source_target_pairs={{8,0},{16,8},{24,16},{32,24},{40,32},{48,40},{56,48},{64,56},{72,6... | collective-permute-start | bytes 196616 | tf_op jit(solution)/shard_map/ppermute | solution.py:103
  36.2 7.9 %collective-permute-start.6 = (f32[4,4,1,512]{3,2,1,0:T(1,128)S(1)}, f32[4,4,1,512]{3,2,1,0:T(1,128)S(1)}, u32[]{:S(2)}, u32[]{:S(2)}) collective-permute-start(f32[4,4,1,512]{3,2,1,0:T(1,128)S(1)} %get-tuple-element.3), channel_id=1, source_target_pairs={{0,1},{1,2},{2,3},{3,4},{4,5},{5,6},{6,7},{8,9},{9,10},{10,11},{11... | collective-permute-start | bytes 98312 | tf_op jit(solution)/shard_map/ppermute | solution.py:104
  44.1 1.3 collective-permute-start.7
  45.4 0.6 multiply_select_fusion.pen_ref
  46.0 2.0 %collective-permute-done.7.yhi_ref = f32[4,4,1,512]{3,2,1,0:T(1,128)S(1)} collective-permute-done((f32[4,4,1,512]{3,2,1,0:T(1,128)S(1)}, f32[4,4,1,512]{3,2,1,0:T(1,128)S(1)}, u32[]{:S(2)}, u32[]{:S(2)}) %collective-permute-start.7) | collective-permute-done | bytes 32800 | tf_op jit(solution)/shard_map/ppermute | solution.py:105
  48.7 0.6 copy-done.5
  49.3 2.6 %shard_map.51 = f32[4,4,8,512]{3,2,1,0:T(8,128)} custom-call(f32[16]{0:T(128)} %means_ref.3, f32[4,4,8,512]{3,2,1,0:T(8,128)} %shard_map.50.cur_ref, f32[4,1,8,512]{3,2,1,0:T(8,128)} %copy-done.3, f32[4,1,8,512]{3,2,1,0:T(8,128)} %copy-done.5, f32[4,4,1,512]{3,2,1,0:T(1,128)} %copy-done.6, f32[4,4,1,512]{3,2,1,0:T(1,128)} %copy-done.8, f32[4,8,512]{2,1,0:T(8,128)} %ct_ref.3), custom_call_target="tpu_custom_call" | custom-call | tf_op jit(solution)/shard_map/pallas_call | solution.py:107
  51.9 10.6 %shard_map.52 = f32[64,8,128]{2,1,0:T(8,128)} custom-call(f32[416]{0:T(512)} %multiply_select_fusion.pen_ref, f32[128,512]{1,0:T(8,128)} %bitcast.5), custom_call_target="tpu_custom_call" | custom-call | tf_op jit(solution)/shard_map/pallas_call | solution.py:236
  62.5 10.4 %all-to-all-start = ((f32[64,8,128]{2,1,0:T(8,128)}), f32[64,8,128]{2,1,0:T(8,128)S(1)}, u32[]{:S(2)}, u32[]{:S(2)}) async-start(f32[64,8,128]{2,1,0:T(8,128)} %shard_map.52), calls=%async_computation | async-start | bytes 524288 | tf_op jit(solution)/shard_map/all_to_all | solution.py:258
  73.4 8.9 %all-to-all-done.src_ref = f32[64,8,128]{2,1,0:T(8,128)S(1)} async-done(((f32[64,8,128]{2,1,0:T(8,128)}), f32[64,8,128]{2,1,0:T(8,128)S(1)}, u32[]{:S(2)}, u32[]{:S(2)}) %all-to-all-start) | async-done | bytes 262176 | tf_op jit(solution)/shard_map/all_to_all | solution.py:258
  82.4 0.7 copy-done.1
  83.1 21.2 %shard_map.53 = f32[64,8,128]{2,1,0:T(8,128)} custom-call(f32[408]{0:T(512)} %multiply_select_fusion.1.pen_ref, f32[64,8,128]{2,1,0:T(8,128)} %copy-done.1), custom_call_target="tpu_custom_call" | custom-call | tf_op jit(solution)/shard_map/pallas_call | solution.py:236
  104.3 17.2 %all_to_all.20 = f32[64,8,128]{2,1,0:T(8,128)} all-to-all(f32[64,8,128]{2,1,0:T(8,128)} %shard_map.53), channel_id=1, replica_groups=mesh['gz'=64,'gy'=8] {'gz'}, dimensions={0} | all-to-all | bytes 524288 | tf_op jit(solution)/shard_map/all_to_all | solution.py:264
  121.5 14.8 %all-to-all-start.2 = ((f32[8,8,8,128]{3,2,1,0:T(8,128)}), f32[8,8,8,128]{3,2,1,0:T(8,128)S(1)}, u32[]{:S(2)}, u32[]{:S(2)}) async-start(f32[8,8,8,128]{3,2,1,0:T(8,128)} %bitcast.1), calls=%async_computation.2 | async-start | bytes 524288 | tf_op jit(solution)/shard_map/all_to_all | solution.py:266
  136.9 18.6 %all-to-all-done.2.src_ref = f32[8,8,8,128]{3,2,1,0:T(8,128)S(1)} async-done(((f32[8,8,8,128]{3,2,1,0:T(8,128)}), f32[8,8,8,128]{3,2,1,0:T(8,128)S(1)}, u32[]{:S(2)}, u32[]{:S(2)}) %all-to-all-start.2) | async-done | bytes 262176 | tf_op jit(solution)/shard_map/all_to_all | solution.py:266
  155.5 0.7 copy-done
  156.2 6.4 %shard_map.54 = f32[8,8,8,128]{3,2,1,0:T(8,128)} custom-call(f32[128]{0:T(128)} %compare_select_fusion.pen_ref, f32[8,8,8,128]{3,2,1,0:T(8,128)} %copy-done), custom_call_target="tpu_custom_call" | custom-call | tf_op jit(solution)/shard_map/pallas_call | solution.py:236
  162.7 27.7 %all_to_all.21 = f32[8,8,8,128]{3,2,1,0:T(8,128)} all-to-all(f32[8,8,8,128]{3,2,1,0:T(8,128)} %shard_map.54), channel_id=1, replica_groups=mesh['gz'=64,'gy'=8] {'gy'}, dimensions={0} | all-to-all | bytes 524288 | tf_op jit(solution)/shard_map/all_to_all | solution.py:271
  190.4 1.8 shard_map.55
  (23 shorter events, 1.8 us)
Async XLA Ops:
  1.5 20.9 %collective-permute-start = (f32[4,1,8,512]{3,2,1,0:T(8,128)S(1)}, f32[4,1,8,512]{3,2,1,0:T(8,128)S(1)}, u32[]{:S(2)}, u32[]{:S(2)}) collective-permute-start(f32[4,1,8,512]{3,2,1,0:T(8,128)S(1)} %get-tuple-element.9), channel_id=1, source_target_pairs={{0,8},{8,16},{16,24},{24,32},{32,40},{40,48},{48,56},{56,64},{64,7... | collective-permute-start | bytes 196616 | tf_op jit(solution)/shard_map/ppermute | solution.py:102
  5.0 17.4 %collective-permute-start.1 = (f32[4,1,8,512]{3,2,1,0:T(8,128)S(1)}, f32[4,1,8,512]{3,2,1,0:T(8,128)S(1)}, u32[]{:S(2)}, u32[]{:S(2)}) collective-permute-start(f32[4,1,8,512]{3,2,1,0:T(8,128)S(1)} %get-tuple-element.8), channel_id=1, source_target_pairs={{8,0},{16,8},{24,16},{32,24},{40,32},{48,40},{56,48},{64,56},{72,6... | collective-permute-start | bytes 196616 | tf_op jit(solution)/shard_map/ppermute | solution.py:103
  10.6 2.6 %collective-permute-start.2 = (f32[4,4,1,512]{3,2,1,0:T(1,128)S(1)}, f32[4,4,1,512]{3,2,1,0:T(1,128)S(1)}, u32[]{:S(2)}, u32[]{:S(2)}) collective-permute-start(f32[4,4,1,512]{3,2,1,0:T(1,128)S(1)} %get-tuple-element.7), channel_id=1, source_target_pairs={{0,1},{1,2},{2,3},{3,4},{4,5},{5,6},{6,7},{8,9},{9,10},{10,11},{11... | collective-permute-start | bytes 98312 | tf_op jit(solution)/shard_map/ppermute | solution.py:104
  11.9 10.5 %collective-permute-start.3 = (f32[4,4,1,512]{3,2,1,0:T(1,128)S(1)}, f32[4,4,1,512]{3,2,1,0:T(1,128)S(1)}, u32[]{:S(2)}, u32[]{:S(2)}) collective-permute-start(f32[4,4,1,512]{3,2,1,0:T(1,128)S(1)} %get-tuple-element.6), channel_id=1, source_target_pairs={{1,0},{2,1},{3,2},{4,3},{5,4},{6,5},{7,6},{9,8},{10,9},{11,10},{12... | collective-permute-start | bytes 98312 | tf_op jit(solution)/shard_map/ppermute | solution.py:105
  13.2 9.2 %copy-start.7 = (f32[4,4,1,512]{3,2,1,0:T(1,128)}, f32[4,4,1,512]{3,2,1,0:T(1,128)S(1)}, u32[]{:S(2)}) copy-start(f32[4,4,1,512]{3,2,1,0:T(1,128)S(1)} %collective-permute-done.2.ylo_ref) | copy-start | bytes 98308
  22.4 0.6 copy-start.9
  22.4 0.6 copy-start.2
  23.0 0.6 copy-start.4
  28.3 19.8 %collective-permute-start.4 = (f32[4,1,8,512]{3,2,1,0:T(8,128)S(1)}, f32[4,1,8,512]{3,2,1,0:T(8,128)S(1)}, u32[]{:S(2)}, u32[]{:S(2)}) collective-permute-start(f32[4,1,8,512]{3,2,1,0:T(8,128)S(1)} %get-tuple-element.5), channel_id=1, source_target_pairs={{0,8},{8,16},{16,24},{24,32},{32,40},{40,48},{48,56},{56,64},{64,7... | collective-permute-start | bytes 196616 | tf_op jit(solution)/shard_map/ppermute | solution.py:102
  30.2 17.9 %collective-permute-start.5 = (f32[4,1,8,512]{3,2,1,0:T(8,128)S(1)}, f32[4,1,8,512]{3,2,1,0:T(8,128)S(1)}, u32[]{:S(2)}, u32[]{:S(2)}) collective-permute-start(f32[4,1,8,512]{3,2,1,0:T(8,128)S(1)} %get-tuple-element.4), channel_id=1, source_target_pairs={{8,0},{16,8},{24,16},{32,24},{40,32},{48,40},{56,48},{64,56},{72,6... | collective-permute-start | bytes 196616 | tf_op jit(solution)/shard_map/ppermute | solution.py:103
  36.2 9.8 %collective-permute-start.6 = (f32[4,4,1,512]{3,2,1,0:T(1,128)S(1)}, f32[4,4,1,512]{3,2,1,0:T(1,128)S(1)}, u32[]{:S(2)}, u32[]{:S(2)}) collective-permute-start(f32[4,4,1,512]{3,2,1,0:T(1,128)S(1)} %get-tuple-element.3), channel_id=1, source_target_pairs={{0,1},{1,2},{2,3},{3,4},{4,5},{5,6},{6,7},{8,9},{9,10},{10,11},{11... | collective-permute-start | bytes 98312 | tf_op jit(solution)/shard_map/ppermute | solution.py:104
  44.1 3.9 %collective-permute-start.7 = (f32[4,4,1,512]{3,2,1,0:T(1,128)S(1)}, f32[4,4,1,512]{3,2,1,0:T(1,128)S(1)}, u32[]{:S(2)}, u32[]{:S(2)}) collective-permute-start(f32[4,4,1,512]{3,2,1,0:T(1,128)S(1)} %get-tuple-element.2), channel_id=1, source_target_pairs={{1,0},{2,1},{3,2},{4,3},{5,4},{6,5},{7,6},{9,8},{10,9},{11,10},{12... | collective-permute-start | bytes 98312 | tf_op jit(solution)/shard_map/ppermute | solution.py:105
  46.0 2.1 %copy-start.6 = (f32[4,4,1,512]{3,2,1,0:T(1,128)}, f32[4,4,1,512]{3,2,1,0:T(1,128)S(1)}, u32[]{:S(2)}) copy-start(f32[4,4,1,512]{3,2,1,0:T(1,128)S(1)} %collective-permute-done.6.ylo_ref) | copy-start | bytes 98308
  48.0 0.6 copy-start.8
  48.1 0.6 copy-start.3
  48.7 0.6 copy-start.5
  62.5 19.9 %all-to-all-start = ((f32[64,8,128]{2,1,0:T(8,128)}), f32[64,8,128]{2,1,0:T(8,128)S(1)}, u32[]{:S(2)}, u32[]{:S(2)}) async-start(f32[64,8,128]{2,1,0:T(8,128)} %shard_map.52), calls=%async_computation | async-start | bytes 524288 | tf_op jit(solution)/shard_map/all_to_all | solution.py:258
  82.4 0.7 copy-start.1
  121.5 34.0 %all-to-all-start.2 = ((f32[8,8,8,128]{3,2,1,0:T(8,128)}), f32[8,8,8,128]{3,2,1,0:T(8,128)S(1)}, u32[]{:S(2)}, u32[]{:S(2)}) async-start(f32[8,8,8,128]{3,2,1,0:T(8,128)} %bitcast.1), calls=%async_computation.2 | async-start | bytes 524288 | tf_op jit(solution)/shard_map/all_to_all | solution.py:266
  155.5 0.7 copy-start

commit v3 on v2

--- a/solution.py
+++ b/solution.py
@@ -134,17 +134,6 @@
         out_ref[g0:g0 + group] = lax.fori_loop(q_lo, q_hi + 1, body, init)
 
 
-def build_rotations(v_ref, u_ref, nrot, pick):
-    def body(b, carry):
-        here = v_ref[b]
-        after = v_ref[b + 1]
-        for r in range(nrot):
-            u_ref[r, b] = pick(r, here, after)
-        return carry
-
-    lax.fori_loop(0, u_ref.shape[1], body, 0)
-
-
 def xpass_kernel(pen_ref, src_ref, out_ref, pad_ref, u_ref):
     lines, nx = src_ref.shape
     reach = KERNEL
@@ -242,34 +231,98 @@
     )(*args)
 
 
+def zy_kernel(pen_z_ref, pen_y_ref, src_ref, out_ref, pad_ref, u_ref, w_ref):
+    n_out = src_ref.shape[0]
+    padc = KERNEL // 4
+    pad_ref[...] = jnp.full(pad_ref.shape, jnp.inf, jnp.float32)
+    pad_ref[padc:padc + n_out] = src_ref[...]
+    lane = lax.broadcasted_iota(jnp.int32, src_ref.shape[1:], 1)
+    sub = lax.broadcasted_iota(jnp.int32, src_ref.shape[1:], 0)
+    sub_z = (lane // 8) % 4
+    sub_y = lane % 8
+
+    def zbody(b, carry):
+        here = pad_ref[b]
+        after = pad_ref[b + 1]
+        u_ref[0, b] = here
+        for r in range(1, 4):
+            u_ref[r, b] = jnp.where(sub_z + r < 4, pltpu.roll(here, 128 - 8 * r, 1),
+                                    pltpu.roll(after, 32 - 8 * r, 1))
+        return carry
+
+    lax.fori_loop(0, u_ref.shape[1], zbody, 0)
+
+    def q_range(g0, group):
+        lo = max(0, padc - 1 - (g0 + group - 1))
+        hi = padc + n_out - 1 - g0
+        return lo, hi
+
+    scan_offsets(u_ref, pen_z_ref, out_ref, n_out, 16, 4, q_range)
+
+    def wbody(a, carry):
+        v = out_ref[a]
+        w_ref[0, a] = v
+        for r in range(1, 8):
+            w_ref[r, a] = jnp.where(sub_y + r < 8, pltpu.roll(v, 128 - r, 1),
+                                    pltpu.roll(pltpu.roll(v, 8 - r, 1), 7, 0))
+        return carry
+
+    lax.fori_loop(0, n_out, wbody, 0)
+    group = 8
+    shifts = []
+    for db in range(-8, 8):
+        for dy in range(8):
+            carry_in = (sub_y + dy >= 8).astype(jnp.int32)
+            row = sub + db + carry_in
+            valid = (row >= 0) & (row <= 7)
+            shifts.append((db, dy, valid))
+
+    def ybody(i, carry):
+        a0 = pl.multiple_of(i * group, group)
+        acc = [jnp.full(src_ref.shape[1:], jnp.inf, jnp.float32) for _ in range(group)]
+        for db, dy, valid in shifts:
+            penvec = jnp.where(valid, pen_y_ref[8 * db + dy + 64], jnp.inf)
+            for g in range(group):
+                v = w_ref[dy, a0 + g]
+                if db % 8:
+                    v = pltpu.roll(v, (8 - db) % 8, 0)
+                acc[g] = jnp.minimum(acc[g], v + penvec)
+        for g in range(group):
+            out_ref[a0 + g] = acc[g]
+        return carry
+
+    lax.fori_loop(0, n_out // group, ybody, 0)
+
+
 def regularize(current):
     levels, nz, ny, nx = current.shape
     lines = levels * nz * ny
     assert lines == 128 and nx % 8 == 0
     n_gz = lax.axis_size("gz")
     n_gy = lax.axis_size("gy")
+    assert n_gz * n_gy == nx and ny == 8 and n_gy == 8
     xq = (KERNEL + 7) // 8
     nxo = nx // 8
     pen_x = penalty_table(8 * (xq * 2 + 2), KERNEL)
     xpad_rows = 8 * (nxo + 2 * xq + 3)
     t1 = local_call(xpass_kernel, (nxo, 8, lines), [(xpad_rows, lines), (8, nxo + 2 * xq + 2, 8, lines)],
                     pen_x, current.reshape(lines, nx))
-    assert nxo == n_gz
-    r1 = lax.all_to_all(t1, "gz", 0, 0, tiled=True)
-    nzo = n_gz
+    r1 = lax.all_to_all(t1.reshape(nx, lines), ("gz", "gy"), 0, 0, tiled=True)
+    r1 = r1.reshape(n_gz, n_gy, lines)
     zq = KERNEL // 4
     pen_z = penalty_table(4 * (2 * zq + 2), KERNEL)
-    t2 = local_call(zpass_kernel, r1.shape, [(nzo + 2 * zq + 3, 8, lines), (4, nzo + 2 * zq + 2, 8, lines)],
-                    pen_z, r1)
-    r2 = lax.all_to_all(t2, "gz", 0, 0, tiled=True)
-    t3 = r2.reshape(n_gy, nxo // n_gy, 8, lines)
-    r3 = lax.all_to_all(t3, "gy", 0, 0, tiled=True)
-    nyo = n_gy
-    pen_y = penalty_table(8 * (2 * nyo), 8 * nyo)
-    t4 = local_call(ypass_kernel, r3.shape, [(3 * nyo + 1,) + r3.shape[1:], (8, 2 * nyo) + r3.shape[1:]],
-                    pen_y, r3)
-    r4 = lax.all_to_all(t4, "gy", 0, 0, tiled=True)
-    out = local_call(transpose_kernel, (lines, nx), [], r4.reshape(nx, lines))
+    pen_y = penalty_table(8 * 2 * n_gy, 8 * n_gy)
+    t2 = pl.pallas_call(
+        zy_kernel,
+        out_shape=jax.ShapeDtypeStruct(r1.shape, jnp.float32),
+        in_specs=[pl.BlockSpec(memory_space=pltpu.SMEM)] * 2 + [pl.BlockSpec(memory_space=pltpu.VMEM)],
+        out_specs=pl.BlockSpec(memory_space=pltpu.VMEM),
+        scratch_shapes=[pltpu.VMEM((n_gz + 2 * zq + 3, 8, lines), jnp.float32),
+                        pltpu.VMEM((4, n_gz + 2 * zq + 2, 8, lines), jnp.float32),
+                        pltpu.VMEM((8, n_gz, 8, lines), jnp.float32)],
+    )(pen_z, pen_y, r1)
+    r2 = lax.all_to_all(t2.reshape(nx, lines), ("gz", "gy"), 0, 0, tiled=True)
+    out = local_call(transpose_kernel, (lines, nx), [], r2)
     return out.reshape(current.shape)
 
 

time: 195 us -> 179 us (0.918)
  blocking collectives: 44.9 us -> 35.2 us
  waiting for transfers between devices: 38.8 us -> 33.6 us
  Pallas kernels: 45.2 us -> 48.4 us
  starting transfers between devices: 52.9 us -> 50.2 us
    pallas_call x0 -> x1, Pallas kernels: none -> 30.8 us  [regularize(): pl.pallas_call(zy_kernel, out_shape=jax.ShapeDtypeStruct(r1.shape, jnp.fl...]
    pallas_call x4 -> x2, Pallas kernels: 40 us -> 12.4 us  [local_call(): pl.pallas_call(kernel, out_shape=jax.ShapeDtypeStruct(out_shape, jnp.floa...]
    all_to_all x2 -> x1, blocking collectives: 44.9 us -> 35.2 us  [regularize(): r2 = lax.all_to_all(t2.reshape(nx, lines), ('gz', 'gy'), 0, 0, tiled=True)]
    all_to_all x2 -> x1, waiting for transfers between devices: 27.5 us -> 22.3 us  [regularize(): r1 = lax.all_to_all(t1.reshape(nx, lines), ('gz', 'gy'), 0, 0, tiled=True)]
    all_to_all x2 -> x1, starting transfers between devices: 25.2 us -> 22.5 us  [regularize(): r1 = lax.all_to_all(t1.reshape(nx, lines), ('gz', 'gy'), 0, 0, tiled=True)]
  transfers between devices with their start and end apart: 10 -> 9, of which waited for: 4 -> 3; matrix products, arithmetic and copies ran while one was open for 1% -> 2% of each run, Pallas kernels for 0% -> 0%
where the time goes in v3:
time: 179 us; the launch traced here: 177 us
  starting transfers between devices  50.2 us (28%)
  Pallas kernels  48.4 us (27%)
  blocking collectives  35.2 us (20%)
  waiting for transfers between devices  33.6 us (19%)
  local copies, waits for them, and re-layouts  7.13 us (4%)
    all_to_all x1, blocking collectives, regularize(): r2 = lax.all_to_all(t2.reshape(nx, lines), ('gz', 'gy'), 0, 0, tiled=True)  35.2 us
    pallas_call x1, Pallas kernels, regularize(): pl.pallas_call(zy_kernel, out_shape=jax.ShapeDtypeStruct(r1.shape, jnp.fl...  30.8 us
    all_to_all x1, starting transfers between devices, regularize(): r1 = lax.all_to_all(t1.reshape(nx, lines), ('gz', 'gy'), 0, 0, tiled=True)  22.5 us
    all_to_all x1, waiting for transfers between devices, regularize(): r1 = lax.all_to_all(t1.reshape(nx, lines), ('gz', 'gy'), 0, 0, tiled=True)  22.3 us
    pallas_call x2, Pallas kernels, local_call(): pl.pallas_call(kernel, out_shape=jax.ShapeDtypeStruct(out_shape, jnp.floa...  12.4 us
    ppermute x2, waiting for transfers between devices, evolve_step(): yhi = lax.ppermute(current[:, :, 0:1], 'gy', bwd_y)  11.3 us
    ppermute x2, starting transfers between devices, evolve_step(): zhi = lax.ppermute(current[:, 0:1], 'gz', bwd_z)  10.5 us
    ppermute x2, starting transfers between devices, evolve_step(): ylo = lax.ppermute(current[:, :, ny - 1:ny], 'gy', fwd_y)  9.17 us
  transfers between devices with their start and end apart: 9, of which 3 were waited for; matrix products, arithmetic and copies ran while one was open for 2% of the time, Pallas kernels for 0%

profile of v3, /device:TPU:6, one launch (start us, length us, event | category | flops | bytes accessed | tf_op | source)
XLA Modules:
  0.0 177.0 jit_solution(13150133866595691835)
XLA Ops:
  0.6 0.9 fusion.3
  1.5 3.5 %collective-permute-start = (f32[4,1,8,512]{3,2,1,0:T(8,128)S(1)}, f32[4,1,8,512]{3,2,1,0:T(8,128)S(1)}, u32[]{:S(2)}, u32[]{:S(2)}) collective-permute-start(f32[4,1,8,512]{3,2,1,0:T(8,128)S(1)} %get-tuple-element.9), channel_id=1, source_target_pairs={{0,8},{8,16},{16,24},{24,32},{32,40},{40,48},{48,56},{56,64},{64,7... | collective-permute-start | bytes 196616 | tf_op jit(solution)/shard_map/ppermute | solution.py:102
  5.0 4.5 %collective-permute-start.1 = (f32[4,1,8,512]{3,2,1,0:T(8,128)S(1)}, f32[4,1,8,512]{3,2,1,0:T(8,128)S(1)}, u32[]{:S(2)}, u32[]{:S(2)}) collective-permute-start(f32[4,1,8,512]{3,2,1,0:T(8,128)S(1)} %get-tuple-element.8), channel_id=1, source_target_pairs={{8,0},{16,8},{24,16},{32,24},{40,32},{48,40},{56,48},{64,56},{72,6... | collective-permute-start | bytes 196616 | tf_op jit(solution)/shard_map/ppermute | solution.py:103
  9.5 1.1 fusion.2
  10.6 1.3 collective-permute-start.2
  11.9 1.3 collective-permute-start.3
  13.2 9.2 %collective-permute-done.3.yhi_ref = f32[4,4,1,512]{3,2,1,0:T(1,128)S(1)} collective-permute-done((f32[4,4,1,512]{3,2,1,0:T(1,128)S(1)}, f32[4,4,1,512]{3,2,1,0:T(1,128)S(1)}, u32[]{:S(2)}, u32[]{:S(2)}) %collective-permute-start.3) | collective-permute-done | bytes 32800 | tf_op jit(solution)/shard_map/ppermute | solution.py:105
  22.4 0.6 copy-done.8
  23.0 0.0 copy-done.1
  23.0 0.6 copy-done.3
  23.7 2.6 %shard_map.50.cur_ref = f32[4,4,8,512]{3,2,1,0:T(8,128)} custom-call(f32[16]{0:T(128)} %means_ref.3, f32[4,4,8,512]{3,2,1,0:T(8,128)} %cur_ref.1, f32[4,1,8,512]{3,2,1,0:T(8,128)} %copy-done.1, f32[4,1,8,512]{3,2,1,0:T(8,128)} %copy-done.3, f32[4,4,1,512]{3,2,1,0:T(1,128)} %copy-done.6, f32[4,4,1,512]{3,2,1,0:T(1,128)} %copy-done.8, f32[4,8,512]{2,1,0:T(8,128)} %ct_ref.3), custom_call_target="tpu_custom_call" | custom-call | tf_op jit(solution)/shard_map/pallas_call | solution.py:107
  26.2 0.9 fusion.1
  27.1 1.1 fusion
  28.2 1.9 %collective-permute-start.4 = (f32[4,1,8,512]{3,2,1,0:T(8,128)S(1)}, f32[4,1,8,512]{3,2,1,0:T(8,128)S(1)}, u32[]{:S(2)}, u32[]{:S(2)}) collective-permute-start(f32[4,1,8,512]{3,2,1,0:T(8,128)S(1)} %get-tuple-element.5), channel_id=1, source_target_pairs={{0,8},{8,16},{16,24},{24,32},{32,40},{40,48},{48,56},{56,64},{64,7... | collective-permute-start | bytes 196616 | tf_op jit(solution)/shard_map/ppermute | solution.py:102
  30.1 6.0 %collective-permute-start.5 = (f32[4,1,8,512]{3,2,1,0:T(8,128)S(1)}, f32[4,1,8,512]{3,2,1,0:T(8,128)S(1)}, u32[]{:S(2)}, u32[]{:S(2)}) collective-permute-start(f32[4,1,8,512]{3,2,1,0:T(8,128)S(1)} %get-tuple-element.4), channel_id=1, source_target_pairs={{8,0},{16,8},{24,16},{32,24},{40,32},{48,40},{56,48},{64,56},{72,6... | collective-permute-start | bytes 196616 | tf_op jit(solution)/shard_map/ppermute | solution.py:103
  36.2 7.9 %collective-permute-start.6 = (f32[4,4,1,512]{3,2,1,0:T(1,128)S(1)}, f32[4,4,1,512]{3,2,1,0:T(1,128)S(1)}, u32[]{:S(2)}, u32[]{:S(2)}) collective-permute-start(f32[4,4,1,512]{3,2,1,0:T(1,128)S(1)} %get-tuple-element.3), channel_id=1, source_target_pairs={{0,1},{1,2},{2,3},{3,4},{4,5},{5,6},{6,7},{8,9},{9,10},{10,11},{11... | collective-permute-start | bytes 98312 | tf_op jit(solution)/shard_map/ppermute | solution.py:104
  44.1 1.3 collective-permute-start.7
  45.4 0.6 multiply_select_fusion.pen_ref
  46.0 2.0 %collective-permute-done.7.yhi_ref = f32[4,4,1,512]{3,2,1,0:T(1,128)S(1)} collective-permute-done((f32[4,4,1,512]{3,2,1,0:T(1,128)S(1)}, f32[4,4,1,512]{3,2,1,0:T(1,128)S(1)}, u32[]{:S(2)}, u32[]{:S(2)}) %collective-permute-start.7) | collective-permute-done | bytes 32800 | tf_op jit(solution)/shard_map/ppermute | solution.py:105
  48.0 0.6 copy-done.7
  48.6 0.0 copy-done.2
  48.7 0.6 copy-done.4
  49.3 2.6 %shard_map.51 = f32[4,4,8,512]{3,2,1,0:T(8,128)} custom-call(f32[16]{0:T(128)} %means_ref.3, f32[4,4,8,512]{3,2,1,0:T(8,128)} %shard_map.50.cur_ref, f32[4,1,8,512]{3,2,1,0:T(8,128)} %copy-done.2, f32[4,1,8,512]{3,2,1,0:T(8,128)} %copy-done.4, f32[4,4,1,512]{3,2,1,0:T(1,128)} %copy-done.5, f32[4,4,1,512]{3,2,1,0:T(1,128)} %copy-done.7, f32[4,8,512]{2,1,0:T(8,128)} %ct_ref.3), custom_call_target="tpu_custom_call" | custom-call | tf_op jit(solution)/shard_map/pallas_call | solution.py:107
  51.9 10.6 %shard_map.52 = f32[64,8,128]{2,1,0:T(8,128)} custom-call(f32[416]{0:T(512)} %multiply_select_fusion.pen_ref, f32[128,512]{1,0:T(8,128)} %bitcast.14), custom_call_target="tpu_custom_call" | custom-call | tf_op jit(solution)/shard_map/pallas_call | solution.py:225
  62.5 22.5 %all-to-all-start = ((f32[512,1,128]{2,1,0:T(1,128)}), f32[512,1,128]{2,1,0:T(1,128)S(1)}, u32[]{:S(2)}, u32[]{:S(2)}) async-start(f32[512,1,128]{2,1,0:T(1,128)} %bitcast.12), calls=%async_computation | async-start | bytes 524288 | tf_op jit(solution)/shard_map/all_to_all | solution.py:310
  85.0 0.5 compare_select_fusion.pen_y_ref
  85.5 0.6 multiply_select_fusion.1.pen_z_ref
  86.1 22.3 %all-to-all-done = f32[512,1,128]{2,1,0:T(1,128)S(1)} async-done(((f32[512,1,128]{2,1,0:T(1,128)}), f32[512,1,128]{2,1,0:T(1,128)S(1)}, u32[]{:S(2)}, u32[]{:S(2)}) %all-to-all-start) | async-done | bytes 262176 | tf_op jit(solution)/shard_map/all_to_all | solution.py:310
  108.5 0.7 copy-done
  109.2 30.8 %shard_map.53 = f32[64,8,128]{2,1,0:T(8,128)} custom-call(f32[408]{0:T(512)} %multiply_select_fusion.1.pen_z_ref, f32[128]{0:T(128)} %compare_select_fusion.pen_y_ref, f32[64,8,128]{2,1,0:T(8,128)} %bitcast.10), custom_call_target="tpu_custom_call" | custom-call | tf_op jit(solution)/shard_map/pallas_call | solution.py:315
  140.0 35.2 %all_to_all.20 = f32[512,1,128]{2,1,0:T(1,128)} all-to-all(f32[512,1,128]{2,1,0:T(1,128)} %bitcast.11), channel_id=1, replica_groups=mesh['gz'=64,'gy'=8] {'gz','gy'}, dimensions={0} | all-to-all | bytes 524288 | tf_op jit(solution)/shard_map/all_to_all | solution.py:324
  175.3 1.8 %shard_map.54 = f32[128,512]{1,0:T(8,128)} custom-call(f32[512,128]{1,0:T(8,128)} %bitcast.13), custom_call_target="tpu_custom_call" | custom-call | tf_op jit(solution)/shard_map/pallas_call | solution.py:225
  (17 shorter events, 0.0 us)
Async XLA Ops:
  1.5 20.9 %collective-permute-start = (f32[4,1,8,512]{3,2,1,0:T(8,128)S(1)}, f32[4,1,8,512]{3,2,1,0:T(8,128)S(1)}, u32[]{:S(2)}, u32[]{:S(2)}) collective-permute-start(f32[4,1,8,512]{3,2,1,0:T(8,128)S(1)} %get-tuple-element.9), channel_id=1, source_target_pairs={{0,8},{8,16},{16,24},{24,32},{32,40},{40,48},{48,56},{56,64},{64,7... | collective-permute-start | bytes 196616 | tf_op jit(solution)/shard_map/ppermute | solution.py:102
  5.0 17.4 %collective-permute-start.1 = (f32[4,1,8,512]{3,2,1,0:T(8,128)S(1)}, f32[4,1,8,512]{3,2,1,0:T(8,128)S(1)}, u32[]{:S(2)}, u32[]{:S(2)}) collective-permute-start(f32[4,1,8,512]{3,2,1,0:T(8,128)S(1)} %get-tuple-element.8), channel_id=1, source_target_pairs={{8,0},{16,8},{24,16},{32,24},{40,32},{48,40},{56,48},{64,56},{72,6... | collective-permute-start | bytes 196616 | tf_op jit(solution)/shard_map/ppermute | solution.py:103
  10.6 2.6 %collective-permute-start.2 = (f32[4,4,1,512]{3,2,1,0:T(1,128)S(1)}, f32[4,4,1,512]{3,2,1,0:T(1,128)S(1)}, u32[]{:S(2)}, u32[]{:S(2)}) collective-permute-start(f32[4,4,1,512]{3,2,1,0:T(1,128)S(1)} %get-tuple-element.7), channel_id=1, source_target_pairs={{0,1},{1,2},{2,3},{3,4},{4,5},{5,6},{6,7},{8,9},{9,10},{10,11},{11... | collective-permute-start | bytes 98312 | tf_op jit(solution)/shard_map/ppermute | solution.py:104
  11.9 10.5 %collective-permute-start.3 = (f32[4,4,1,512]{3,2,1,0:T(1,128)S(1)}, f32[4,4,1,512]{3,2,1,0:T(1,128)S(1)}, u32[]{:S(2)}, u32[]{:S(2)}) collective-permute-start(f32[4,4,1,512]{3,2,1,0:T(1,128)S(1)} %get-tuple-element.6), channel_id=1, source_target_pairs={{1,0},{2,1},{3,2},{4,3},{5,4},{6,5},{7,6},{9,8},{10,9},{11,10},{12... | collective-permute-start | bytes 98312 | tf_op jit(solution)/shard_map/ppermute | solution.py:105
  13.2 9.2 %copy-start.6 = (f32[4,4,1,512]{3,2,1,0:T(1,128)}, f32[4,4,1,512]{3,2,1,0:T(1,128)S(1)}, u32[]{:S(2)}) copy-start(f32[4,4,1,512]{3,2,1,0:T(1,128)S(1)} %collective-permute-done.2.ylo_ref) | copy-start | bytes 98308
  22.4 0.6 copy-start.8
  22.4 0.6 copy-start.1
  23.0 0.6 copy-start.3
  28.2 19.8 %collective-permute-start.4 = (f32[4,1,8,512]{3,2,1,0:T(8,128)S(1)}, f32[4,1,8,512]{3,2,1,0:T(8,128)S(1)}, u32[]{:S(2)}, u32[]{:S(2)}) collective-permute-start(f32[4,1,8,512]{3,2,1,0:T(8,128)S(1)} %get-tuple-element.5), channel_id=1, source_target_pairs={{0,8},{8,16},{16,24},{24,32},{32,40},{40,48},{48,56},{56,64},{64,7... | collective-permute-start | bytes 196616 | tf_op jit(solution)/shard_map/ppermute | solution.py:102
  30.1 17.9 %collective-permute-start.5 = (f32[4,1,8,512]{3,2,1,0:T(8,128)S(1)}, f32[4,1,8,512]{3,2,1,0:T(8,128)S(1)}, u32[]{:S(2)}, u32[]{:S(2)}) collective-permute-start(f32[4,1,8,512]{3,2,1,0:T(8,128)S(1)} %get-tuple-element.4), channel_id=1, source_target_pairs={{8,0},{16,8},{24,16},{32,24},{40,32},{48,40},{56,48},{64,56},{72,6... | collective-permute-start | bytes 196616 | tf_op jit(solution)/shard_map/ppermute | solution.py:103
  36.2 9.8 %collective-permute-start.6 = (f32[4,4,1,512]{3,2,1,0:T(1,128)S(1)}, f32[4,4,1,512]{3,2,1,0:T(1,128)S(1)}, u32[]{:S(2)}, u32[]{:S(2)}) collective-permute-start(f32[4,4,1,512]{3,2,1,0:T(1,128)S(1)} %get-tuple-element.3), channel_id=1, source_target_pairs={{0,1},{1,2},{2,3},{3,4},{4,5},{5,6},{6,7},{8,9},{9,10},{10,11},{11... | collective-permute-start | bytes 98312 | tf_op jit(solution)/shard_map/ppermute | solution.py:104
  44.1 3.9 %collective-permute-start.7 = (f32[4,4,1,512]{3,2,1,0:T(1,128)S(1)}, f32[4,4,1,512]{3,2,1,0:T(1,128)S(1)}, u32[]{:S(2)}, u32[]{:S(2)}) collective-permute-start(f32[4,4,1,512]{3,2,1,0:T(1,128)S(1)} %get-tuple-element.2), channel_id=1, source_target_pairs={{1,0},{2,1},{3,2},{4,3},{5,4},{6,5},{7,6},{9,8},{10,9},{11,10},{12... | collective-permute-start | bytes 98312 | tf_op jit(solution)/shard_map/ppermute | solution.py:105
  46.0 2.1 %copy-start.5 = (f32[4,4,1,512]{3,2,1,0:T(1,128)}, f32[4,4,1,512]{3,2,1,0:T(1,128)S(1)}, u32[]{:S(2)}) copy-start(f32[4,4,1,512]{3,2,1,0:T(1,128)S(1)} %collective-permute-done.6.ylo_ref) | copy-start | bytes 98308
  48.0 0.6 copy-start.7
  48.0 0.6 copy-start.2
  48.7 0.6 copy-start.4
  62.5 46.0 %all-to-all-start = ((f32[512,1,128]{2,1,0:T(1,128)}), f32[512,1,128]{2,1,0:T(1,128)S(1)}, u32[]{:S(2)}, u32[]{:S(2)}) async-start(f32[512,1,128]{2,1,0:T(1,128)} %bitcast.12), calls=%async_computation | async-start | bytes 524288 | tf_op jit(solution)/shard_map/all_to_all | solution.py:310
  108.5 0.7 copy-start

commit v4 on v3

--- a/solution.py
+++ b/solution.py
@@ -32,7 +32,7 @@
     return jnp.where(x < 0, -r, r)
 
 
-def evolve_kernel(means_ref, cur_ref, zlo_ref, zhi_ref, ylo_ref, yhi_ref, ct_ref, out_ref):
+def compute_step(means_ref, cur_ref, zlo_ref, zhi_ref, ylo_ref, yhi_ref, ct_ref, out_ref):
     nz, ny, nx = cur_ref.shape[1], cur_ref.shape[2], cur_ref.shape[3]
     shape = (ny, nx)
     xi = lax.broadcasted_iota(jnp.int32, shape, 1)
@@ -56,8 +56,8 @@
         phis, lap, g1, g0, dl = [], [], [], [], []
         for k in range(LEVELS):
             c = cur_ref[k, z]
-            zm = zlo_ref[k, 0] if z == 0 else cur_ref[k, z - 1]
-            zp = zhi_ref[k, 0] if z == nz - 1 else cur_ref[k, z + 1]
+            zm = zlo_ref[k] if z == 0 else cur_ref[k, z - 1]
+            zp = zhi_ref[k] if z == nz - 1 else cur_ref[k, z + 1]
             edge = jnp.where(low_row, ylo_ref[k, z], yhi_ref[k, z])
             ym = jnp.where(ya_ok, pltpu.roll(c, 1, 0), edge)
             yp = jnp.where(yb_ok, pltpu.roll(c, ny - 1, 0), edge)
@@ -93,23 +93,90 @@
             out_ref[k, z] = phis[k] + STEP_SIZE * dl[k] * (lap[k] - force)
 
 
-def evolve_step(current, picture, region_means):
-    fwd_z = [(i, i + 1) for i in range(lax.axis_size("gz") - 1)]
-    fwd_y = [(i, i + 1) for i in range(lax.axis_size("gy") - 1)]
-    bwd_z = [(t, s) for s, t in fwd_z]
-    bwd_y = [(t, s) for s, t in fwd_y]
-    nz, ny = current.shape[1], current.shape[2]
-    zlo = lax.ppermute(current[:, nz - 1:nz], "gz", fwd_z)
-    zhi = lax.ppermute(current[:, 0:1], "gz", bwd_z)
-    ylo = lax.ppermute(current[:, :, ny - 1:ny], "gy", fwd_y)
-    yhi = lax.ppermute(current[:, :, 0:1], "gy", bwd_y)
+MESH = pl.DeviceIdType.MESH
+
+
+def evolve_kernel(means_ref, cur_ref, ct_ref, out_ref, mid_ref, zlo_buf, zhi_buf, ylo_buf, yhi_buf,
+                  send_sem, recv_sem):
+    nz, ny = cur_ref.shape[1], cur_ref.shape[2]
+    gz, gy = lax.axis_index("gz"), lax.axis_index("gy")
+    n_gz, n_gy = lax.axis_size("gz"), lax.axis_size("gy")
+    peers = [(gz > 0, (gz - 1, gy)), (gz < n_gz - 1, (gz + 1, gy)),
+             (gy > 0, (gz, gy - 1)), (gy < n_gy - 1, (gz, gy + 1))]
+    barrier = pltpu.get_barrier_semaphore()
+    for present, dev in peers:
+        @pl.when(present)
+        def _(dev=dev):
+            pl.semaphore_signal(barrier, inc=1, device_id=dev, device_id_type=MESH)
+    count = sum(present.astype(jnp.int32) for present, _ in peers)
+    pl.semaphore_wait(barrier, count)
+
+    def exchange(step, src_ref):
+        plan = [
+            (gz < n_gz - 1, gz > 0, src_ref.at[:, nz - 1], zlo_buf.at[step], (gz + 1, gy)),
+            (gz > 0, gz < n_gz - 1, src_ref.at[:, 0], zhi_buf.at[step], (gz - 1, gy)),
+            (gy < n_gy - 1, gy > 0, src_ref.at[:, :, pl.ds(ny - 1, 1)], ylo_buf.at[step], (gz, gy + 1)),
+            (gy > 0, gy < n_gy - 1, src_ref.at[:, :, pl.ds(0, 1)], yhi_buf.at[step], (gz, gy - 1)),
+        ]
+        copies = []
+        for d, (sends, receives, src, dst, target) in enumerate(plan):
+            copy = pltpu.make_async_remote_copy(
+                src_ref=src, dst_ref=dst, send_sem=send_sem.at[step, d],
+                recv_sem=recv_sem.at[step, d], device_id=target, device_id_type=MESH)
+
+            @pl.when(sends)
+            def _(copy=copy):
+                copy.start()
+
+            @pl.when(jnp.logical_not(receives))
+            def _(dst=dst):
+                dst[...] = jnp.zeros(dst.shape, jnp.float32)
+
+            copies.append((sends, receives, copy))
+        return copies
+
+    def finish(copies):
+        for sends, receives, copy in copies:
+            @pl.when(receives)
+            def _(copy=copy):
+                copy.wait_recv()
+
+    def drain(copies):
+        for sends, receives, copy in copies:
+            @pl.when(sends)
+            def _(copy=copy):
+                copy.wait_send()
+
+    first = exchange(0, cur_ref)
+    finish(first)
+    compute_step(means_ref, cur_ref, zlo_buf.at[0], zhi_buf.at[0], ylo_buf.at[0], yhi_buf.at[0], ct_ref, mid_ref)
+    drain(first)
+    second = exchange(1, mid_ref)
+    finish(second)
+    compute_step(means_ref, mid_ref, zlo_buf.at[1], zhi_buf.at[1], ylo_buf.at[1], yhi_buf.at[1], ct_ref, out_ref)
+    drain(second)
+
+
+def evolve_all(current, picture, region_means):
+    levels, nz, ny, nx = current.shape
     vmem = pl.BlockSpec(memory_space=pltpu.VMEM)
+    f32 = jnp.float32
     return pl.pallas_call(
         evolve_kernel,
         out_shape=jax.ShapeDtypeStruct(current.shape, current.dtype),
-        in_specs=[pl.BlockSpec(memory_space=pltpu.SMEM)] + [vmem] * 6,
+        in_specs=[pl.BlockSpec(memory_space=pltpu.SMEM), vmem, vmem],
         out_specs=vmem,
-    )(region_means, current, zlo, zhi, ylo, yhi, picture)
+        scratch_shapes=[
+            pltpu.VMEM(current.shape, f32),
+            pltpu.VMEM((2, levels, ny, nx), f32),
+            pltpu.VMEM((2, levels, ny, nx), f32),
+            pltpu.VMEM((2, levels, nz, 1, nx), f32),
+            pltpu.VMEM((2, levels, nz, 1, nx), f32),
+            pltpu.SemaphoreType.DMA((2, 4)),
+            pltpu.SemaphoreType.DMA((2, 4)),
+        ],
+        compiler_params=pltpu.CompilerParams(collective_id=0, has_side_effects=True),
+    )(region_means, current, picture)
 
 
 def penalty_table(count, offset):
@@ -327,9 +394,7 @@
 
 
 def body(levels, ct_image, region_means):
-    current = levels
-    for update_round in range(UPDATES):
-        current = evolve_step(current, ct_image, region_means)
+    current = evolve_all(levels, ct_image, region_means)
     return (current, regularize(current))
 
 

time: 179 us -> 146 us (0.82)
  starting transfers between devices: 50.2 us -> 22.6 us
  Pallas kernels: 48.4 us -> 61 us
  waiting for transfers between devices: 33.6 us -> 22.4 us
  local copies, waits for them, and re-layouts: 7.13 us -> 1.41 us
    ppermute x8 -> x0, starting transfers between devices: 27.7 us -> none  [the longest x2 10.5 us: evolve_step(): zhi = lax.ppermute(current[:, 0:1], 'gz', bwd_z)]
    pallas_call x2 -> x1, Pallas kernels: 5.18 us -> 17.8 us  [evolve_all(): pl.pallas_call(evolve_kernel, out_shape=jax.ShapeDtypeStruct(current.shap...]
    ppermute x8 -> x0, waiting for transfers between devices: 11.3 us -> none  [the longest x2 11.3 us: evolve_step(): yhi = lax.ppermute(current[:, :, 0:1], 'gy', bwd_y)]
    slice x4 -> x0, local copies, waits for them, and re-layouts: 3.93 us -> none  [the longest x2 2.17 us: evolve_step(): yhi = lax.ppermute(current[:, :, 0:1], 'gy', bwd_y)]
    unnamed x18 -> x5, local copies, waits for them, and re-layouts: 3.2 us -> 1.41 us
  transfers between devices with their start and end apart: 9 -> 1, of which waited for: 3 -> 1; matrix products, arithmetic and copies ran while one was open for 2% -> 1% of each run, Pallas kernels for 0% -> 0%
where the time goes in v4:
time: 146 us; the launch traced here: 145 us
  Pallas kernels  61 us (42%)
  blocking collectives  35.3 us (24%)
  starting transfers between devices  22.6 us (15%)
  waiting for transfers between devices  22.4 us (15%)
  other arithmetic  1.69 us (1%)
    all_to_all x1, blocking collectives, regularize(): r2 = lax.all_to_all(t2.reshape(nx, lines), ('gz', 'gy'), 0, 0, tiled=True)  35.3 us
    pallas_call x1, Pallas kernels, regularize(): pl.pallas_call(zy_kernel, out_shape=jax.ShapeDtypeStruct(r1.shape, jnp.fl...  30.8 us
    all_to_all x1, starting transfers between devices, regularize(): r1 = lax.all_to_all(t1.reshape(nx, lines), ('gz', 'gy'), 0, 0, tiled=True)  22.6 us
    all_to_all x1, waiting for transfers between devices, regularize(): r1 = lax.all_to_all(t1.reshape(nx, lines), ('gz', 'gy'), 0, 0, tiled=True)  22.4 us
    pallas_call x1, Pallas kernels, evolve_all(): pl.pallas_call(evolve_kernel, out_shape=jax.ShapeDtypeStruct(current.shap...  17.8 us
    pallas_call x2, Pallas kernels, local_call(): pl.pallas_call(kernel, out_shape=jax.ShapeDtypeStruct(out_shape, jnp.floa...  12.4 us
  transfers between devices with their start and end apart: 1, of which 1 were waited for; matrix products, arithmetic and copies ran while one was open for 1% of the time, Pallas kernels for 0%

profile of v4, /device:TPU:6, one launch (start us, length us, event | category | flops | bytes accessed | tf_op | source)
XLA Modules:
  0.0 145.0 jit_solution(4251229317751899273)
XLA Ops:
  0.6 0.6 multiply_select_fusion.pen_ref
  1.2 17.8 %shard_map.50 = f32[4,4,8,512]{3,2,1,0:T(8,128)} custom-call(f32[16]{0:T(128)} %means_ref.1, f32[4,4,8,512]{3,2,1,0:T(8,128)} %cur_ref.1, f32[4,8,512]{2,1,0:T(8,128)} %ct_ref.1), custom_call_target="tpu_custom_call" | custom-call | tf_op jit(solution)/shard_map/pallas_call | solution.py:164
  19.0 10.6 %shard_map.51 = f32[64,8,128]{2,1,0:T(8,128)} custom-call(f32[416]{0:T(512)} %multiply_select_fusion.pen_ref, f32[128,512]{1,0:T(8,128)} %bitcast.10), custom_call_target="tpu_custom_call" | custom-call | tf_op jit(solution)/shard_map/pallas_call | solution.py:292
  29.6 22.6 %all-to-all-start = ((f32[512,1,128]{2,1,0:T(1,128)}), f32[512,1,128]{2,1,0:T(1,128)S(1)}, u32[]{:S(2)}, u32[]{:S(2)}) async-start(f32[512,1,128]{2,1,0:T(1,128)} %bitcast.13), calls=%async_computation | async-start | bytes 524288 | tf_op jit(solution)/shard_map/all_to_all | solution.py:377
  52.2 0.5 compare_select_fusion.pen_y_ref
  52.7 0.6 multiply_select_fusion.1.pen_z_ref
  53.3 22.4 %all-to-all-done = f32[512,1,128]{2,1,0:T(1,128)S(1)} async-done(((f32[512,1,128]{2,1,0:T(1,128)}), f32[512,1,128]{2,1,0:T(1,128)S(1)}, u32[]{:S(2)}, u32[]{:S(2)}) %all-to-all-start) | async-done | bytes 262176 | tf_op jit(solution)/shard_map/all_to_all | solution.py:377
  75.6 0.0 copy-start.1
  75.6 0.7 copy-done.1
  76.3 30.8 %shard_map.52 = f32[64,8,128]{2,1,0:T(8,128)} custom-call(f32[408]{0:T(512)} %multiply_select_fusion.1.pen_z_ref, f32[128]{0:T(128)} %compare_select_fusion.pen_y_ref, f32[64,8,128]{2,1,0:T(8,128)} %bitcast.11), custom_call_target="tpu_custom_call" | custom-call | tf_op jit(solution)/shard_map/pallas_call | solution.py:382
  107.2 35.3 %all_to_all.20 = f32[512,1,128]{2,1,0:T(1,128)} all-to-all(f32[512,1,128]{2,1,0:T(1,128)} %bitcast.12), channel_id=1, replica_groups=mesh['gz'=64,'gy'=8] {'gz','gy'}, dimensions={0} | all-to-all | bytes 524288 | tf_op jit(solution)/shard_map/all_to_all | solution.py:391
  142.5 0.0 copy-start
  142.5 1.8 %shard_map.53 = f32[128,512]{1,0:T(8,128)} custom-call(f32[512,128]{1,0:T(8,128)} %bitcast.14), custom_call_target="tpu_custom_call" | custom-call | tf_op jit(solution)/shard_map/pallas_call | solution.py:292
  144.3 0.0 copy-done
  144.3 0.7 copy.8
Async XLA Ops:
  29.6 46.0 %all-to-all-start = ((f32[512,1,128]{2,1,0:T(1,128)}), f32[512,1,128]{2,1,0:T(1,128)S(1)}, u32[]{:S(2)}, u32[]{:S(2)}) async-start(f32[512,1,128]{2,1,0:T(1,128)} %bitcast.13), calls=%async_computation | async-start | bytes 524288 | tf_op jit(solution)/shard_map/all_to_all | solution.py:377
  75.6 0.7 copy-start.1
  142.5 1.8 %copy-start = (f32[4,4,8,512]{3,2,1,0:T(8,128)S(1)}, f32[4,4,8,512]{3,2,1,0:T(8,128)}, u32[]{:S(2)}) copy-start(f32[4,4,8,512]{3,2,1,0:T(8,128)} %shard_map.50) | copy-start | bytes 786436

commit v5 on v4

--- a/solution.py
+++ b/solution.py
@@ -198,7 +198,7 @@
             return acc
 
         init = jnp.full((group,) + tuple(out_ref.shape[1:]), jnp.inf, jnp.float32)
-        out_ref[g0:g0 + group] = lax.fori_loop(q_lo, q_hi + 1, body, init)
+        out_ref[g0:g0 + group] = lax.fori_loop(q_lo, q_hi + 1, body, init, unroll=2)
 
 
 def xpass_kernel(pen_ref, src_ref, out_ref, pad_ref, u_ref):

time: 146 us -> 145 us (level)
  Pallas kernels: 61 us -> 59.5 us
where the time goes in v5:
time: 145 us; the launch traced here: 143 us
  Pallas kernels  59.5 us (41%)
  blocking collectives  35.3 us (24%)
  starting transfers between devices  22.6 us (16%)
  waiting for transfers between devices  22.4 us (15%)
  other arithmetic  1.69 us (1%)
    all_to_all x1, blocking collectives, regularize(): r2 = lax.all_to_all(t2.reshape(nx, lines), ('gz', 'gy'), 0, 0, tiled=True)  35.3 us
    pallas_call x1, Pallas kernels, regularize(): pl.pallas_call(zy_kernel, out_shape=jax.ShapeDtypeStruct(r1.shape, jnp.fl...  29.8 us
    all_to_all x1, starting transfers between devices, regularize(): r1 = lax.all_to_all(t1.reshape(nx, lines), ('gz', 'gy'), 0, 0, tiled=True)  22.6 us
    all_to_all x1, waiting for transfers between devices, regularize(): r1 = lax.all_to_all(t1.reshape(nx, lines), ('gz', 'gy'), 0, 0, tiled=True)  22.4 us
    pallas_call x1, Pallas kernels, evolve_all(): pl.pallas_call(evolve_kernel, out_shape=jax.ShapeDtypeStruct(current.shap...  17.8 us
    pallas_call x2, Pallas kernels, local_call(): pl.pallas_call(kernel, out_shape=jax.ShapeDtypeStruct(out_shape, jnp.floa...  11.9 us
  transfers between devices with their start and end apart: 1, of which 1 were waited for; matrix products, arithmetic and copies ran while one was open for 1% of the time, Pallas kernels for 0%

profile of v5, /device:TPU:6, one launch (start us, length us, event | category | flops | bytes accessed | tf_op | source)
XLA Modules:
  0.0 143.4 jit_solution(14727262075464289509)
XLA Ops:
  0.6 0.6 multiply_select_fusion.pen_ref
  1.2 17.8 %shard_map.50 = f32[4,4,8,512]{3,2,1,0:T(8,128)} custom-call(f32[16]{0:T(128)} %means_ref.1, f32[4,4,8,512]{3,2,1,0:T(8,128)} %cur_ref.1, f32[4,8,512]{2,1,0:T(8,128)} %ct_ref.1), custom_call_target="tpu_custom_call" | custom-call | tf_op jit(solution)/shard_map/pallas_call | solution.py:164
  19.0 10.0 %shard_map.51 = f32[64,8,128]{2,1,0:T(8,128)} custom-call(f32[416]{0:T(512)} %multiply_select_fusion.pen_ref, f32[128,512]{1,0:T(8,128)} %bitcast.10), custom_call_target="tpu_custom_call" | custom-call | tf_op jit(solution)/shard_map/pallas_call | solution.py:292
  29.0 22.6 %all-to-all-start = ((f32[512,1,128]{2,1,0:T(1,128)}), f32[512,1,128]{2,1,0:T(1,128)S(1)}, u32[]{:S(2)}, u32[]{:S(2)}) async-start(f32[512,1,128]{2,1,0:T(1,128)} %bitcast.13), calls=%async_computation | async-start | bytes 524288 | tf_op jit(solution)/shard_map/all_to_all | solution.py:377
  51.6 0.5 compare_select_fusion.pen_y_ref
  52.1 0.6 multiply_select_fusion.1.pen_z_ref
  52.7 22.4 %all-to-all-done = f32[512,1,128]{2,1,0:T(1,128)S(1)} async-done(((f32[512,1,128]{2,1,0:T(1,128)}), f32[512,1,128]{2,1,0:T(1,128)S(1)}, u32[]{:S(2)}, u32[]{:S(2)}) %all-to-all-start) | async-done | bytes 262176 | tf_op jit(solution)/shard_map/all_to_all | solution.py:377
  75.1 0.0 copy-start.1
  75.1 0.7 copy-done.1
  75.8 29.8 %shard_map.52 = f32[64,8,128]{2,1,0:T(8,128)} custom-call(f32[408]{0:T(512)} %multiply_select_fusion.1.pen_z_ref, f32[128]{0:T(128)} %compare_select_fusion.pen_y_ref, f32[64,8,128]{2,1,0:T(8,128)} %bitcast.11), custom_call_target="tpu_custom_call" | custom-call | tf_op jit(solution)/shard_map/pallas_call | solution.py:382
  105.6 35.3 %all_to_all.20 = f32[512,1,128]{2,1,0:T(1,128)} all-to-all(f32[512,1,128]{2,1,0:T(1,128)} %bitcast.12), channel_id=1, replica_groups=mesh['gz'=64,'gy'=8] {'gz','gy'}, dimensions={0} | all-to-all | bytes 524288 | tf_op jit(solution)/shard_map/all_to_all | solution.py:391
  140.9 0.0 copy-start
  140.9 1.8 %shard_map.53 = f32[128,512]{1,0:T(8,128)} custom-call(f32[512,128]{1,0:T(8,128)} %bitcast.14), custom_call_target="tpu_custom_call" | custom-call | tf_op jit(solution)/shard_map/pallas_call | solution.py:292
  142.7 0.0 copy-done
  142.7 0.7 copy.8
Async XLA Ops:
  29.0 46.0 %all-to-all-start = ((f32[512,1,128]{2,1,0:T(1,128)}), f32[512,1,128]{2,1,0:T(1,128)S(1)}, u32[]{:S(2)}, u32[]{:S(2)}) async-start(f32[512,1,128]{2,1,0:T(1,128)} %bitcast.13), calls=%async_computation | async-start | bytes 524288 | tf_op jit(solution)/shard_map/all_to_all | solution.py:377
  75.1 0.7 copy-start.1
  140.9 1.8 %copy-start = (f32[4,4,8,512]{3,2,1,0:T(8,128)S(1)}, f32[4,4,8,512]{3,2,1,0:T(8,128)}, u32[]{:S(2)}) copy-start(f32[4,4,8,512]{3,2,1,0:T(8,128)} %shard_map.50) | copy-start | bytes 786436

commit v6 on v5

--- a/solution.py
+++ b/solution.py
@@ -201,22 +201,28 @@
         out_ref[g0:g0 + group] = lax.fori_loop(q_lo, q_hi + 1, body, init, unroll=2)
 
 
+def build_rotations(pad_ref, u_ref, nrot, pick, chunk=8):
+    def body(i, carry):
+        b0 = pl.multiple_of(i * chunk, chunk)
+        here = pad_ref[pl.ds(b0, chunk)]
+        after = pad_ref[pl.ds(b0 + 1, chunk)]
+        u_ref[0, pl.ds(b0, chunk)] = here
+        for r in range(1, nrot):
+            u_ref[r, pl.ds(b0, chunk)] = pick(r, here, after)
+        return carry
+
+    lax.fori_loop(0, u_ref.shape[1] // chunk, body, 0)
+
+
 def xpass_kernel(pen_ref, src_ref, out_ref, pad_ref, u_ref):
     lines, nx = src_ref.shape
     reach = KERNEL
+    padc = reach // 8
     pad_ref[...] = jnp.full(pad_ref.shape, jnp.inf, jnp.float32)
-    pad_ref[reach:reach + nx, :] = src_ref[...].T
-    sub = lax.broadcasted_iota(jnp.int32, (8, lines), 0)
-
-    def body(b, carry):
-        here = pad_ref[pl.ds(pl.multiple_of(b * 8, 8), 8), :]
-        after = pad_ref[pl.ds(pl.multiple_of(b * 8 + 8, 8), 8), :]
-        u_ref[0, b] = here
-        for r in range(1, 8):
-            u_ref[r, b] = jnp.where(sub < 8 - r, pltpu.roll(here, 8 - r, 0), pltpu.roll(after, 8 - r, 0))
-        return carry
-
-    lax.fori_loop(0, u_ref.shape[1], body, 0)
+    pad_ref[padc:padc + nx // 8] = src_ref[...].T.reshape(nx // 8, 8, lines)
+    sub = lax.broadcasted_iota(jnp.int32, (8, 8, lines), 1)
+    build_rotations(pad_ref, u_ref, 8, lambda r, here, after: jnp.where(
+        sub < 8 - r, pltpu.roll(here, 8 - r, 1), pltpu.roll(after, 8 - r, 1)))
     n_out = nx // 8
 
     def q_range(g0, group):
@@ -225,60 +231,6 @@
         return lo, hi
 
     scan_offsets(u_ref, pen_ref, out_ref, n_out, 16, 8, q_range)
-
-
-def zpass_kernel(pen_ref, src_ref, out_ref, pad_ref, u_ref):
-    n_out = src_ref.shape[0]
-    padc = KERNEL // 4
-    pad_ref[...] = jnp.full(pad_ref.shape, jnp.inf, jnp.float32)
-    pad_ref[padc:padc + n_out] = src_ref[...]
-    lane = lax.broadcasted_iota(jnp.int32, src_ref.shape[1:], 1)
-    sub_z = (lane // 8) % 4
-
-    def body(b, carry):
-        here = pad_ref[b]
-        after = pad_ref[b + 1]
-        u_ref[0, b] = here
-        for r in range(1, 4):
-            u_ref[r, b] = jnp.where(sub_z + r < 4, pltpu.roll(here, 128 - 8 * r, 1),
-                                    pltpu.roll(after, 32 - 8 * r, 1))
-        return carry
-
-    lax.fori_loop(0, u_ref.shape[1], body, 0)
-
-    def q_range(g0, group):
-        lo = max(0, padc - 1 - (g0 + group - 1))
-        hi = padc + n_out - 1 - g0
-        return lo, hi
-
-    scan_offsets(u_ref, pen_ref, out_ref, n_out, 16, 4, q_range)
-
-
-def ypass_kernel(pen_ref, src_ref, out_ref, pad_ref, u_ref):
-    n_out = src_ref.shape[0]
-    padc = n_out
-    pad_ref[...] = jnp.full(pad_ref.shape, jnp.inf, jnp.float32)
-    pad_ref[padc:padc + n_out] = src_ref[...]
-    lane = lax.broadcasted_iota(jnp.int32, src_ref.shape[1:], 2)
-    sub_y = lane % 8
-
-    def body(b, carry):
-        here = pad_ref[b]
-        after = pad_ref[b + 1]
-        u_ref[0, b] = here
-        for r in range(1, 8):
-            u_ref[r, b] = jnp.where(sub_y + r < 8, pltpu.roll(here, 128 - r, 2),
-                                    pltpu.roll(after, 8 - r, 2))
-        return carry
-
-    lax.fori_loop(0, u_ref.shape[1], body, 0)
-
-    def q_range(g0, group):
-        lo = max(0, padc - 1 - (g0 + group - 1))
-        hi = padc + n_out - 1 - g0
-        return lo, hi
-
-    scan_offsets(u_ref, pen_ref, out_ref, n_out, 1, 8, q_range)
 
 
 def transpose_kernel(src_ref, out_ref):
@@ -308,16 +260,11 @@
     sub_z = (lane // 8) % 4
     sub_y = lane % 8
 
-    def zbody(b, carry):
-        here = pad_ref[b]
-        after = pad_ref[b + 1]
-        u_ref[0, b] = here
-        for r in range(1, 4):
-            u_ref[r, b] = jnp.where(sub_z + r < 4, pltpu.roll(here, 128 - 8 * r, 1),
-                                    pltpu.roll(after, 32 - 8 * r, 1))
-        return carry
-
-    lax.fori_loop(0, u_ref.shape[1], zbody, 0)
+    lane3 = lax.broadcasted_iota(jnp.int32, (8,) + tuple(src_ref.shape[1:]), 2)
+    sub_z3 = (lane3 // 8) % 4
+    sub_y3 = lane3 % 8
+    build_rotations(pad_ref, u_ref, 4, lambda r, here, after: jnp.where(
+        sub_z3 + r < 4, pltpu.roll(here, 128 - 8 * r, 2), pltpu.roll(after, 32 - 8 * r, 2)))
 
     def q_range(g0, group):
         lo = max(0, padc - 1 - (g0 + group - 1))
@@ -326,15 +273,16 @@
 
     scan_offsets(u_ref, pen_z_ref, out_ref, n_out, 16, 4, q_range)
 
-    def wbody(a, carry):
-        v = out_ref[a]
-        w_ref[0, a] = v
+    def wbody(i, carry):
+        a0 = pl.multiple_of(i * 8, 8)
+        v = out_ref[pl.ds(a0, 8)]
+        w_ref[0, pl.ds(a0, 8)] = v
         for r in range(1, 8):
-            w_ref[r, a] = jnp.where(sub_y + r < 8, pltpu.roll(v, 128 - r, 1),
-                                    pltpu.roll(pltpu.roll(v, 8 - r, 1), 7, 0))
+            w_ref[r, pl.ds(a0, 8)] = jnp.where(sub_y3 + r < 8, pltpu.roll(v, 128 - r, 2),
+                                               pltpu.roll(pltpu.roll(v, 8 - r, 2), 7, 1))
         return carry
 
-    lax.fori_loop(0, n_out, wbody, 0)
+    lax.fori_loop(0, n_out // 8, wbody, 0)
     group = 8
     shifts = []
     for db in range(-8, 8):
@@ -371,21 +319,22 @@
     xq = (KERNEL + 7) // 8
     nxo = nx // 8
     pen_x = penalty_table(8 * (xq * 2 + 2), KERNEL)
-    xpad_rows = 8 * (nxo + 2 * xq + 3)
-    t1 = local_call(xpass_kernel, (nxo, 8, lines), [(xpad_rows, lines), (8, nxo + 2 * xq + 2, 8, lines)],
+    xu = -(-(nxo + 2 * xq + 2) // 8) * 8
+    t1 = local_call(xpass_kernel, (nxo, 8, lines), [(xu + 8, 8, lines), (8, xu, 8, lines)],
                     pen_x, current.reshape(lines, nx))
     r1 = lax.all_to_all(t1.reshape(nx, lines), ("gz", "gy"), 0, 0, tiled=True)
     r1 = r1.reshape(n_gz, n_gy, lines)
     zq = KERNEL // 4
     pen_z = penalty_table(4 * (2 * zq + 2), KERNEL)
+    zu = -(-(n_gz + 2 * zq + 2) // 8) * 8
     pen_y = penalty_table(8 * 2 * n_gy, 8 * n_gy)
     t2 = pl.pallas_call(
         zy_kernel,
         out_shape=jax.ShapeDtypeStruct(r1.shape, jnp.float32),
         in_specs=[pl.BlockSpec(memory_space=pltpu.SMEM)] * 2 + [pl.BlockSpec(memory_space=pltpu.VMEM)],
         out_specs=pl.BlockSpec(memory_space=pltpu.VMEM),
-        scratch_shapes=[pltpu.VMEM((n_gz + 2 * zq + 3, 8, lines), jnp.float32),
-                        pltpu.VMEM((4, n_gz + 2 * zq + 2, 8, lines), jnp.float32),
+        scratch_shapes=[pltpu.VMEM((zu + 8, 8, lines), jnp.float32),
+                        pltpu.VMEM((4, zu, 8, lines), jnp.float32),
                         pltpu.VMEM((8, n_gz, 8, lines), jnp.float32)],
     )(pen_z, pen_y, r1)
     r2 = lax.all_to_all(t2.reshape(nx, lines), ("gz", "gy"), 0, 0, tiled=True)

time: 145 us -> 130 us (0.90)
  Pallas kernels: 59.5 us -> 44.9 us
    pallas_call x1, Pallas kernels: 29.8 us -> 15.9 us  [regularize(): pl.pallas_call(zy_kernel, out_shape=jax.ShapeDtypeStruct(r1.shape, jnp.fl...]
where the time goes in v6:
time: 130 us; the launch traced here: 129 us
  Pallas kernels  44.9 us (35%)
  blocking collectives  35.3 us (27%)
  starting transfers between devices  22.6 us (17%)
  waiting for transfers between devices  22.4 us (17%)
  other arithmetic  1.69 us (1%)
  local copies, waits for them, and re-layouts  1.41 us (1%)
    all_to_all x1, blocking collectives, regularize(): r2 = lax.all_to_all(t2.reshape(nx, lines), ('gz', 'gy'), 0, 0, tiled=True)  35.3 us
    all_to_all x1, starting transfers between devices, regularize(): r1 = lax.all_to_all(t1.reshape(nx, lines), ('gz', 'gy'), 0, 0, tiled=True)  22.6 us
    all_to_all x1, waiting for transfers between devices, regularize(): r1 = lax.all_to_all(t1.reshape(nx, lines), ('gz', 'gy'), 0, 0, tiled=True)  22.4 us
    pallas_call x1, Pallas kernels, evolve_all(): pl.pallas_call(evolve_kernel, out_shape=jax.ShapeDtypeStruct(current.shap...  17.8 us
    pallas_call x1, Pallas kernels, regularize(): pl.pallas_call(zy_kernel, out_shape=jax.ShapeDtypeStruct(r1.shape, jnp.fl...  15.9 us
    pallas_call x2, Pallas kernels, local_call(): pl.pallas_call(kernel, out_shape=jax.ShapeDtypeStruct(out_shape, jnp.floa...  11.2 us
  transfers between devices with their start and end apart: 1, of which 1 were waited for; matrix products, arithmetic and copies ran while one was open for 1% of the time, Pallas kernels for 0%

profile of v6, /device:TPU:6, one launch (start us, length us, event | category | flops | bytes accessed | tf_op | source)
XLA Modules:
  0.0 128.9 jit_solution(8349100581617779064)
XLA Ops:
  0.6 0.6 multiply_select_fusion.pen_ref
  1.2 17.8 %shard_map.50 = f32[4,4,8,512]{3,2,1,0:T(8,128)} custom-call(f32[16]{0:T(128)} %means_ref.1, f32[4,4,8,512]{3,2,1,0:T(8,128)} %cur_ref.1, f32[4,8,512]{2,1,0:T(8,128)} %ct_ref.1), custom_call_target="tpu_custom_call" | custom-call | tf_op jit(solution)/shard_map/pallas_call | solution.py:164
  19.0 9.4 %shard_map.51 = f32[64,8,128]{2,1,0:T(8,128)} custom-call(f32[416]{0:T(512)} %multiply_select_fusion.pen_ref, f32[128,512]{1,0:T(8,128)} %bitcast.10), custom_call_target="tpu_custom_call" | custom-call | tf_op jit(solution)/shard_map/pallas_call | solution.py:244
  28.4 22.6 %all-to-all-start = ((f32[512,1,128]{2,1,0:T(1,128)}), f32[512,1,128]{2,1,0:T(1,128)S(1)}, u32[]{:S(2)}, u32[]{:S(2)}) async-start(f32[512,1,128]{2,1,0:T(1,128)} %bitcast.13), calls=%async_computation | async-start | bytes 524288 | tf_op jit(solution)/shard_map/all_to_all | solution.py:325
  50.9 0.5 compare_select_fusion.pen_y_ref
  51.5 0.6 multiply_select_fusion.1.pen_z_ref
  52.1 22.4 %all-to-all-done = f32[512,1,128]{2,1,0:T(1,128)S(1)} async-done(((f32[512,1,128]{2,1,0:T(1,128)}), f32[512,1,128]{2,1,0:T(1,128)S(1)}, u32[]{:S(2)}, u32[]{:S(2)}) %all-to-all-start) | async-done | bytes 262176 | tf_op jit(solution)/shard_map/all_to_all | solution.py:325
  74.4 0.0 copy-start.1
  74.4 0.7 copy-done.1
  75.1 15.9 %shard_map.52 = f32[64,8,128]{2,1,0:T(8,128)} custom-call(f32[408]{0:T(512)} %multiply_select_fusion.1.pen_z_ref, f32[128]{0:T(128)} %compare_select_fusion.pen_y_ref, f32[64,8,128]{2,1,0:T(8,128)} %bitcast.11), custom_call_target="tpu_custom_call" | custom-call | tf_op jit(solution)/shard_map/pallas_call | solution.py:331
  91.0 35.3 %all_to_all.20 = f32[512,1,128]{2,1,0:T(1,128)} all-to-all(f32[512,1,128]{2,1,0:T(1,128)} %bitcast.12), channel_id=1, replica_groups=mesh['gz'=64,'gy'=8] {'gz','gy'}, dimensions={0} | all-to-all | bytes 524288 | tf_op jit(solution)/shard_map/all_to_all | solution.py:340
  126.3 0.0 copy-start
  126.3 1.8 %shard_map.53 = f32[128,512]{1,0:T(8,128)} custom-call(f32[512,128]{1,0:T(8,128)} %bitcast.14), custom_call_target="tpu_custom_call" | custom-call | tf_op jit(solution)/shard_map/pallas_call | solution.py:244
  128.2 0.0 copy-done
  128.2 0.7 copy.8
Async XLA Ops:
  28.4 46.0 %all-to-all-start = ((f32[512,1,128]{2,1,0:T(1,128)}), f32[512,1,128]{2,1,0:T(1,128)S(1)}, u32[]{:S(2)}, u32[]{:S(2)}) async-start(f32[512,1,128]{2,1,0:T(1,128)} %bitcast.13), calls=%async_computation | async-start | bytes 524288 | tf_op jit(solution)/shard_map/all_to_all | solution.py:325
  74.4 0.7 copy-start.1
  126.3 1.8 %copy-start = (f32[4,4,8,512]{3,2,1,0:T(8,128)S(1)}, f32[4,4,8,512]{3,2,1,0:T(8,128)}, u32[]{:S(2)}) copy-start(f32[4,4,8,512]{3,2,1,0:T(8,128)} %shard_map.50) | copy-start | bytes 786436

commit v7 on v6

--- a/solution.py
+++ b/solution.py
@@ -309,6 +309,58 @@
     lax.fori_loop(0, n_out // group, ybody, 0)
 
 
+def exchange_rows_kernel(src_ref, out_ref, recv_buf, send_sem, recv_sem, own_sem):
+    n_gy = lax.axis_size("gy")
+    n = src_ref.shape[0]
+    me = lax.axis_index("gz") * n_gy + lax.axis_index("gy")
+
+    def device(k):
+        p = lax.rem(me + k, n)
+        return p, (p // n_gy, lax.rem(p, n_gy))
+
+    barrier = pltpu.get_barrier_semaphore()
+
+    def greet(k, carry):
+        _, dev = device(k)
+        pl.semaphore_signal(barrier, inc=1, device_id=dev, device_id_type=MESH)
+        return carry
+
+    lax.fori_loop(1, n, greet, 0)
+    pl.semaphore_wait(barrier, n - 1)
+
+    def send(k, carry):
+        p, dev = device(k)
+        pltpu.make_async_remote_copy(
+            src_ref=src_ref.at[pl.ds(p, 1)], dst_ref=recv_buf.at[pl.ds(me, 1)],
+            send_sem=send_sem, recv_sem=recv_sem, device_id=dev, device_id_type=MESH).start()
+        return carry
+
+    lax.fori_loop(1, n, send, 0, unroll=8)
+    own = pltpu.make_async_copy(src_ref.at[pl.ds(me, 1)], recv_buf.at[pl.ds(me, 1)], own_sem)
+    own.start()
+    own.wait()
+    _, dev = device(1)
+    total = pltpu.make_async_remote_copy(
+        src_ref=src_ref.at[pl.ds(0, n - 1)], dst_ref=recv_buf.at[pl.ds(0, n - 1)],
+        send_sem=send_sem, recv_sem=recv_sem, device_id=dev, device_id_type=MESH)
+    total.wait_send()
+    total.wait_recv()
+    out_ref[...] = recv_buf[...]
+
+
+def exchange_rows(rows, collective_id):
+    vmem = pl.BlockSpec(memory_space=pltpu.VMEM)
+    return pl.pallas_call(
+        exchange_rows_kernel,
+        out_shape=jax.ShapeDtypeStruct(rows.shape, rows.dtype),
+        in_specs=[vmem],
+        out_specs=vmem,
+        scratch_shapes=[pltpu.VMEM(rows.shape, rows.dtype), pltpu.SemaphoreType.DMA(()),
+                        pltpu.SemaphoreType.DMA(()), pltpu.SemaphoreType.DMA(())],
+        compiler_params=pltpu.CompilerParams(collective_id=collective_id, has_side_effects=True),
+    )(rows)
+
+
 def regularize(current):
     levels, nz, ny, nx = current.shape
     lines = levels * nz * ny
@@ -322,8 +374,7 @@
     xu = -(-(nxo + 2 * xq + 2) // 8) * 8
     t1 = local_call(xpass_kernel, (nxo, 8, lines), [(xu + 8, 8, lines), (8, xu, 8, lines)],
                     pen_x, current.reshape(lines, nx))
-    r1 = lax.all_to_all(t1.reshape(nx, lines), ("gz", "gy"), 0, 0, tiled=True)
-    r1 = r1.reshape(n_gz, n_gy, lines)
+    r1 = exchange_rows(t1.reshape(nx, lines), 1).reshape(n_gz, n_gy, lines)
     zq = KERNEL // 4
     pen_z = penalty_table(4 * (2 * zq + 2), KERNEL)
     zu = -(-(n_gz + 2 * zq + 2) // 8) * 8
@@ -337,7 +388,7 @@
                         pltpu.VMEM((4, zu, 8, lines), jnp.float32),
                         pltpu.VMEM((8, n_gz, 8, lines), jnp.float32)],
     )(pen_z, pen_y, r1)
-    r2 = lax.all_to_all(t2.reshape(nx, lines), ("gz", "gy"), 0, 0, tiled=True)
+    r2 = exchange_rows(t2.reshape(nx, lines), 2)
     out = local_call(transpose_kernel, (lines, nx), [], r2)
     return out.reshape(current.shape)
 

time: 130 us -> 134 us (1.031)
  Pallas kernels: 44.9 us -> 129 us
  blocking collectives: 35.3 us -> 0 us
  starting transfers between devices: 22.6 us -> 0 us
  waiting for transfers between devices: 22.4 us -> 0 us
    pallas_call x0 -> x2, Pallas kernels: none -> 84.3 us  [exchange_rows(): pl.pallas_call(exchange_rows_kernel, out_shape=jax.ShapeDtypeStruct(rows....]
    all_to_all x1 -> x0, blocking collectives: 35.3 us -> none  [regularize(): r2 = lax.all_to_all(t2.reshape(nx, lines), ('gz', 'gy'), 0, 0, tiled=True)]
    all_to_all x1 -> x0, starting transfers between devices: 22.6 us -> none  [regularize(): r1 = lax.all_to_all(t1.reshape(nx, lines), ('gz', 'gy'), 0, 0, tiled=True)]
    all_to_all x1 -> x0, waiting for transfers between devices: 22.4 us -> none  [regularize(): r1 = lax.all_to_all(t1.reshape(nx, lines), ('gz', 'gy'), 0, 0, tiled=True)]
  transfers between devices with their start and end apart: 1 -> 0, of which waited for: 1 -> 0; matrix products, arithmetic and copies ran while one was open for 1% -> 0% of each run, Pallas kernels for 0% -> 0%
where the time goes in v7:
time: 134 us; the launch traced here: 132 us
  Pallas kernels  129 us (96%)
  other arithmetic  1.68 us (1%)
    pallas_call x2, Pallas kernels, exchange_rows(): pl.pallas_call(exchange_rows_kernel, out_shape=jax.ShapeDtypeStruct(rows....  84.3 us
    pallas_call x1, Pallas kernels, evolve_all(): pl.pallas_call(evolve_kernel, out_shape=jax.ShapeDtypeStruct(current.shap...  17.8 us
    pallas_call x1, Pallas kernels, regularize(): pl.pallas_call(zy_kernel, out_shape=jax.ShapeDtypeStruct(r1.shape, jnp.fl...  15.9 us
    pallas_call x2, Pallas kernels, local_call(): pl.pallas_call(kernel, out_shape=jax.ShapeDtypeStruct(out_shape, jnp.floa...  11.2 us

profile of v7, /device:TPU:6, one launch (start us, length us, event | category | flops | bytes accessed | tf_op | source)
XLA Modules:
  0.0 132.3 jit_solution(8486664103833657665)
XLA Ops:
  0.6 0.5 compare_select_fusion.pen_y_ref
  1.1 0.6 multiply_select_fusion.1.pen_z_ref
  1.7 0.6 multiply_select_fusion.pen_ref
  2.3 17.8 %shard_map.50 = f32[4,4,8,512]{3,2,1,0:T(8,128)} custom-call(f32[16]{0:T(128)} %means_ref.1, f32[4,4,8,512]{3,2,1,0:T(8,128)} %cur_ref.1, f32[4,8,512]{2,1,0:T(8,128)} %ct_ref.1), custom_call_target="tpu_custom_call" | custom-call | tf_op jit(solution)/shard_map/pallas_call | solution.py:164
  20.1 9.4 %shard_map.51 = f32[64,8,128]{2,1,0:T(8,128)} custom-call(f32[416]{0:T(512)} %multiply_select_fusion.pen_ref, f32[128,512]{1,0:T(8,128)} %bitcast.5), custom_call_target="tpu_custom_call" | custom-call | tf_op jit(solution)/shard_map/pallas_call | solution.py:244
  29.5 45.9 %shard_map.52 = f32[512,128]{1,0:T(8,128)} custom-call(f32[512,128]{1,0:T(8,128)} %bitcast.8), custom_call_target="tpu_custom_call" | custom-call | tf_op jit(solution)/shard_map/pallas_call | solution.py:353
  75.4 15.9 %shard_map.53 = f32[64,8,128]{2,1,0:T(8,128)} custom-call(f32[408]{0:T(512)} %multiply_select_fusion.1.pen_z_ref, f32[128]{0:T(128)} %compare_select_fusion.pen_y_ref, f32[64,8,128]{2,1,0:T(8,128)} %bitcast.6), custom_call_target="tpu_custom_call" | custom-call | tf_op jit(solution)/shard_map/pallas_call | solution.py:382
  91.3 38.5 %shard_map.54.src_ref = f32[512,128]{1,0:T(8,128)} custom-call(f32[512,128]{1,0:T(8,128)} %bitcast.7), custom_call_target="tpu_custom_call" | custom-call | tf_op jit(solution)/shard_map/pallas_call | solution.py:353
  129.8 0.0 copy-start
  129.8 1.8 %shard_map.55 = f32[128,512]{1,0:T(8,128)} custom-call(f32[512,128]{1,0:T(8,128)} %shard_map.54.src_ref), custom_call_target="tpu_custom_call" | custom-call | tf_op jit(solution)/shard_map/pallas_call | solution.py:244
  131.6 0.0 copy-done
  131.6 0.7 copy.6
Async XLA Ops:
  129.8 1.8 %copy-start = (f32[4,4,8,512]{3,2,1,0:T(8,128)S(1)}, f32[4,4,8,512]{3,2,1,0:T(8,128)}, u32[]{:S(2)}) copy-start(f32[4,4,8,512]{3,2,1,0:T(8,128)} %shard_map.50) | copy-start | bytes 786436

commit v8 on v6

--- a/solution.py
+++ b/solution.py
@@ -1,3 +1,4 @@
+import functools
 import math
 
 import jax
@@ -309,6 +310,81 @@
     lax.fori_loop(0, n_out // group, ybody, 0)
 
 
+def transpose_kernel_stages(forward, src_ref, out_ref, mid_ref, sems):
+    n_gz, n_gy = lax.axis_size("gz"), lax.axis_size("gy")
+    a, b = lax.axis_index("gz"), lax.axis_index("gy")
+    barrier = pltpu.get_barrier_semaphore()
+
+    def greet_gy(k, carry):
+        pl.semaphore_signal(barrier, inc=1, device_id=(a, lax.rem(b + k, n_gy)), device_id_type=MESH)
+        return carry
+
+    def greet_gz(k, carry):
+        pl.semaphore_signal(barrier, inc=1, device_id=(lax.rem(a + k, n_gz), b), device_id_type=MESH)
+        return carry
+
+    lax.fori_loop(1, n_gy, greet_gy, 0)
+    lax.fori_loop(1, n_gz, greet_gz, 0)
+    pl.semaphore_wait(barrier, n_gy - 1 + n_gz - 1)
+
+    def stage_gy(src, dst, send_sem, recv_sem, own_sem):
+        def send(k, carry):
+            p = lax.rem(b + k, n_gy)
+            pltpu.make_async_remote_copy(
+                src_ref=src.at[:, pl.ds(p, 1)], dst_ref=dst.at[:, pl.ds(b, 1)], send_sem=send_sem,
+                recv_sem=recv_sem, device_id=(a, p), device_id_type=MESH).start()
+            return carry
+
+        lax.fori_loop(1, n_gy, send, 0)
+        own = pltpu.make_async_copy(src.at[:, pl.ds(b, 1)], dst.at[:, pl.ds(b, 1)], own_sem)
+        own.start()
+        own.wait()
+        total = pltpu.make_async_remote_copy(
+            src_ref=src.at[:, pl.ds(0, n_gy - 1)], dst_ref=dst.at[:, pl.ds(0, n_gy - 1)],
+            send_sem=send_sem, recv_sem=recv_sem, device_id=(a, lax.rem(b + 1, n_gy)),
+            device_id_type=MESH)
+        total.wait_recv()
+        total.wait_send()
+
+    def stage_gz(src, dst, send_sem, recv_sem, own_sem):
+        def send(k, carry):
+            p = lax.rem(a + k, n_gz)
+            pltpu.make_async_remote_copy(
+                src_ref=src.at[pl.ds(p, 1)], dst_ref=dst.at[pl.ds(a, 1)], send_sem=send_sem,
+                recv_sem=recv_sem, device_id=(p, b), device_id_type=MESH).start()
+            return carry
+
+        lax.fori_loop(1, n_gz, send, 0, unroll=4)
+        own = pltpu.make_async_copy(src.at[pl.ds(a, 1)], dst.at[pl.ds(a, 1)], own_sem)
+        own.start()
+        own.wait()
+        total = pltpu.make_async_remote_copy(
+            src_ref=src.at[pl.ds(0, n_gz - 1)], dst_ref=dst.at[pl.ds(0, n_gz - 1)],
+            send_sem=send_sem, recv_sem=recv_sem, device_id=(lax.rem(a + 1, n_gz), b),
+            device_id_type=MESH)
+        total.wait_recv()
+        total.wait_send()
+
+    if forward:
+        stage_gy(src_ref, mid_ref, sems.at[0], sems.at[1], sems.at[2])
+        stage_gz(mid_ref, out_ref, sems.at[3], sems.at[4], sems.at[5])
+    else:
+        stage_gz(src_ref, mid_ref, sems.at[0], sems.at[1], sems.at[2])
+        stage_gy(mid_ref, out_ref, sems.at[3], sems.at[4], sems.at[5])
+
+
+def exchange_rows(rows, forward, collective_id):
+    vmem = pl.BlockSpec(memory_space=pltpu.VMEM)
+    return pl.pallas_call(
+        functools.partial(transpose_kernel_stages, forward),
+        out_shape=jax.ShapeDtypeStruct(rows.shape, rows.dtype),
+        in_specs=[vmem],
+        out_specs=vmem,
+        scratch_shapes=[pltpu.VMEM(rows.shape, rows.dtype), pltpu.SemaphoreType.DMA((6,))],
+        compiler_params=pltpu.CompilerParams(collective_id=collective_id, has_side_effects=True),
+    )(rows)
+
+
 def regularize(current):
     levels, nz, ny, nx = current.shape
     lines = levels * nz * ny
@@ -322,8 +398,7 @@
     xu = -(-(nxo + 2 * xq + 2) // 8) * 8
     t1 = local_call(xpass_kernel, (nxo, 8, lines), [(xu + 8, 8, lines), (8, xu, 8, lines)],
                     pen_x, current.reshape(lines, nx))
-    r1 = lax.all_to_all(t1.reshape(nx, lines), ("gz", "gy"), 0, 0, tiled=True)
-    r1 = r1.reshape(n_gz, n_gy, lines)
+    r1 = exchange_rows(t1, True, 1)
     zq = KERNEL // 4
     pen_z = penalty_table(4 * (2 * zq + 2), KERNEL)
     zu = -(-(n_gz + 2 * zq + 2) // 8) * 8
@@ -337,7 +412,7 @@
                         pltpu.VMEM((4, zu, 8, lines), jnp.float32),
                         pltpu.VMEM((8, n_gz, 8, lines), jnp.float32)],
     )(pen_z, pen_y, r1)
-    r2 = lax.all_to_all(t2.reshape(nx, lines), ("gz", "gy"), 0, 0, tiled=True)
+    r2 = exchange_rows(t2, False, 2).reshape(nx, lines)
     out = local_call(transpose_kernel, (lines, nx), [], r2)
     return out.reshape(current.shape)
 

time: 130 us -> 120 us (0.923)
  the two profiles are of different devices: /device:TPU:6 before, /device:TPU:67 now
where the time goes in v8:
time: 120 us
  Pallas kernels  117 us (98%)
  other arithmetic  1.68 us (1%)
    pallas_call x2, Pallas kernels, exchange_rows(): pl.pallas_call(functools.partial(transpose_kernel_stages, forward), out_s...  69 us
    pallas_call x1, Pallas kernels, evolve_all(): pl.pallas_call(evolve_kernel, out_shape=jax.ShapeDtypeStruct(current.shap...  20.6 us
    pallas_call x1, Pallas kernels, regularize(): pl.pallas_call(zy_kernel, out_shape=jax.ShapeDtypeStruct(r1.shape, jnp.fl...  15.9 us
    pallas_call x2, Pallas kernels, local_call(): pl.pallas_call(kernel, out_shape=jax.ShapeDtypeStruct(out_shape, jnp.floa...  11.2 us

profile of v8, /device:TPU:67, one launch (start us, length us, event | category | flops | bytes accessed | tf_op | source)
XLA Modules:
  0.0 119.8 jit_solution(8421306852396414546)
XLA Ops:
  0.6 0.5 compare_select_fusion.pen_y_ref
  1.1 0.6 multiply_select_fusion.1.pen_z_ref
  1.7 0.6 multiply_select_fusion.pen_ref
  2.3 20.6 %shard_map.50 = f32[4,4,8,512]{3,2,1,0:T(8,128)} custom-call(f32[16]{0:T(128)} %means_ref.1, f32[4,4,8,512]{3,2,1,0:T(8,128)} %cur_ref.1, f32[4,8,512]{2,1,0:T(8,128)} %ct_ref.1), custom_call_target="tpu_custom_call" | custom-call | tf_op jit(solution)/shard_map/pallas_call | solution.py:165
  22.9 9.4 %shard_map.51.src_ref = f32[64,8,128]{2,1,0:T(8,128)} custom-call(f32[416]{0:T(512)} %multiply_select_fusion.pen_ref, f32[128,512]{1,0:T(8,128)} %bitcast.3), custom_call_target="tpu_custom_call" | custom-call | tf_op jit(solution)/shard_map/pallas_call | solution.py:245
  32.3 34.9 %shard_map.52.src_ref = f32[64,8,128]{2,1,0:T(8,128)} custom-call(f32[64,8,128]{2,1,0:T(8,128)} %shard_map.51.src_ref), custom_call_target="tpu_custom_call" | custom-call | tf_op jit(solution)/shard_map/pallas_call | solution.py:378
  67.1 15.9 %shard_map.53.src_ref = f32[64,8,128]{2,1,0:T(8,128)} custom-call(f32[408]{0:T(512)} %multiply_select_fusion.1.pen_z_ref, f32[128]{0:T(128)} %compare_select_fusion.pen_y_ref, f32[64,8,128]{2,1,0:T(8,128)} %shard_map.52.src_ref), custom_call_target="tpu_custom_call" | custom-call | tf_op jit(solution)/shard_map/pallas_call | solution.py:406
  83.1 34.2 %shard_map.54 = f32[64,8,128]{2,1,0:T(8,128)} custom-call(f32[64,8,128]{2,1,0:T(8,128)} %shard_map.53.src_ref), custom_call_target="tpu_custom_call" | custom-call | tf_op jit(solution)/shard_map/pallas_call | solution.py:378
  117.3 0.0 copy-start
  117.3 1.8 %shard_map.55 = f32[128,512]{1,0:T(8,128)} custom-call(f32[512,128]{1,0:T(8,128)} %bitcast.4), custom_call_target="tpu_custom_call" | custom-call | tf_op jit(solution)/shard_map/pallas_call | solution.py:245
  119.1 0.0 copy-done
  119.1 0.7 copy.6
Async XLA Ops:
  117.3 1.8 %copy-start = (f32[4,4,8,512]{3,2,1,0:T(8,128)S(1)}, f32[4,4,8,512]{3,2,1,0:T(8,128)}, u32[]{:S(2)}) copy-start(f32[4,4,8,512]{3,2,1,0:T(8,128)} %shard_map.50) | copy-start | bytes 786436

commit v9 on v6

--- a/solution.py
+++ b/solution.py
@@ -1,3 +1,4 @@
+import functools
 import math
 
 import jax
@@ -309,6 +310,64 @@
     lax.fori_loop(0, n_out // group, ybody, 0)
 
 
+def global_transpose_kernel(src_ref, out_ref, mid_ref, blk_ref, recv_ref, sems):
+    n_gz, n_gy = lax.axis_size("gz"), lax.axis_size("gy")
+    a, b = lax.axis_index("gz"), lax.axis_index("gy")
+    barrier = pltpu.get_barrier_semaphore()
+
+    def greet_gy(k, carry):
+        pl.semaphore_signal(barrier, inc=1, device_id=(a, lax.rem(b + k, n_gy)), device_id_type=MESH)
+        return carry
+
+    def greet_gz(k, carry):
+        pl.semaphore_signal(barrier, inc=1, device_id=(lax.rem(a + k, n_gz), b), device_id_type=MESH)
+        return carry
+
+    lax.fori_loop(1, n_gy, greet_gy, 0)
+    lax.fori_loop(1, n_gz, greet_gz, 0)
+    pl.semaphore_wait(barrier, n_gy - 1 + n_gz - 1)
+
+    def stage(src, dst, size, me, peers, target, send_sem, recv_sem, own_sem, unroll):
+        def send(k, carry):
+            p = lax.rem(me + k, peers)
+            pltpu.make_async_remote_copy(
+                src_ref=src.at[pl.ds(pl.multiple_of(p * size, 8), size)],
+                dst_ref=dst.at[pl.ds(pl.multiple_of(me * size, 8), size)], send_sem=send_sem,
+                recv_sem=recv_sem, device_id=target(p), device_id_type=MESH).start()
+            return carry
+
+        lax.fori_loop(1, peers, send, 0, unroll=unroll)
+        own_rows = pl.ds(pl.multiple_of(me * size, 8), size)
+        own = pltpu.make_async_copy(src.at[own_rows], dst.at[own_rows], own_sem)
+        own.start()
+        own.wait()
+        rest = pl.ds(0, (peers - 1) * size)
+        total = pltpu.make_async_remote_copy(
+            src_ref=src.at[rest], dst_ref=dst.at[rest], send_sem=send_sem, recv_sem=recv_sem,
+            device_id=target(lax.rem(me + 1, peers)), device_id_type=MESH)
+        total.wait_recv()
+        total.wait_send()
+
+    stage(src_ref, mid_ref, n_gy, a, n_gz, lambda p: (p, b), sems.at[0], sems.at[1], sems.at[2], 4)
+    for i in range(n_gy):
+        blk_ref[i * n_gz:(i + 1) * n_gz] = mid_ref[pl.ds(i, n_gz, stride=n_gy)]
+    stage(blk_ref, recv_ref, n_gz, b, n_gy, lambda p: (a, p), sems.at[3], sems.at[4], sems.at[5], 1)
+    for j in range(n_gz):
+        out_ref[j * n_gy:(j + 1) * n_gy] = recv_ref[pl.ds(j, n_gy, stride=n_gz)]
+
+
+def exchange_rows(rows, collective_id):
+    vmem = pl.BlockSpec(memory_space=pltpu.VMEM)
+    return pl.pallas_call(
+        global_transpose_kernel,
+        out_shape=jax.ShapeDtypeStruct(rows.shape, rows.dtype),
+        in_specs=[vmem],
+        out_specs=vmem,
+        scratch_shapes=[pltpu.VMEM(rows.shape, rows.dtype)] * 3 + [pltpu.SemaphoreType.DMA((6,))],
+        compiler_params=pltpu.CompilerParams(collective_id=collective_id, has_side_effects=True),
+    )(rows)
+
+
 def regularize(current):
     levels, nz, ny, nx = current.shape
     lines = levels * nz * ny
@@ -322,8 +381,7 @@
     xu = -(-(nxo + 2 * xq + 2) // 8) * 8
     t1 = local_call(xpass_kernel, (nxo, 8, lines), [(xu + 8, 8, lines), (8, xu, 8, lines)],
                     pen_x, current.reshape(lines, nx))
-    r1 = lax.all_to_all(t1.reshape(nx, lines), ("gz", "gy"), 0, 0, tiled=True)
-    r1 = r1.reshape(n_gz, n_gy, lines)
+    r1 = exchange_rows(t1.reshape(nx, lines), 1).reshape(n_gz, n_gy, lines)
     zq = KERNEL // 4
     pen_z = penalty_table(4 * (2 * zq + 2), KERNEL)
     zu = -(-(n_gz + 2 * zq + 2) // 8) * 8
@@ -337,7 +395,7 @@
                         pltpu.VMEM((4, zu, 8, lines), jnp.float32),
                         pltpu.VMEM((8, n_gz, 8, lines), jnp.float32)],
     )(pen_z, pen_y, r1)
-    r2 = lax.all_to_all(t2.reshape(nx, lines), ("gz", "gy"), 0, 0, tiled=True)
+    r2 = exchange_rows(t2.reshape(nx, lines), 2)
     out = local_call(transpose_kernel, (lines, nx), [], r2)
     return out.reshape(current.shape)
 

time: 130 us -> 120 us (0.923)
  the two profiles are of different devices: /device:TPU:6 before, /device:TPU:39 now
where the time goes in v9:
time: 120 us; the launch traced here: 119 us
  Pallas kernels  116 us (97%)
  other arithmetic  1.68 us (1%)
    pallas_call x2, Pallas kernels, exchange_rows(): pl.pallas_call(global_transpose_kernel, out_shape=jax.ShapeDtypeStruct(ro...  68.6 us
    pallas_call x1, Pallas kernels, evolve_all(): pl.pallas_call(evolve_kernel, out_shape=jax.ShapeDtypeStruct(current.shap...  20.6 us
    pallas_call x1, Pallas kernels, regularize(): pl.pallas_call(zy_kernel, out_shape=jax.ShapeDtypeStruct(r1.shape, jnp.fl...  15.9 us
    pallas_call x2, Pallas kernels, local_call(): pl.pallas_call(kernel, out_shape=jax.ShapeDtypeStruct(out_shape, jnp.floa...  11.2 us

profile of v9, /device:TPU:39, one launch (start us, length us, event | category | flops | bytes accessed | tf_op | source)
XLA Modules:
  0.0 119.4 jit_solution(17539082925175978651)
XLA Ops:
  0.6 0.5 compare_select_fusion.pen_y_ref
  1.1 0.6 multiply_select_fusion.1.pen_z_ref
  1.7 0.6 multiply_select_fusion.pen_ref
  2.3 20.6 %shard_map.50 = f32[4,4,8,512]{3,2,1,0:T(8,128)} custom-call(f32[16]{0:T(128)} %means_ref.1, f32[4,4,8,512]{3,2,1,0:T(8,128)} %cur_ref.1, f32[4,8,512]{2,1,0:T(8,128)} %ct_ref.1), custom_call_target="tpu_custom_call" | custom-call | tf_op jit(solution)/shard_map/pallas_call | solution.py:165
  22.9 9.4 %shard_map.51 = f32[64,8,128]{2,1,0:T(8,128)} custom-call(f32[416]{0:T(512)} %multiply_select_fusion.pen_ref, f32[128,512]{1,0:T(8,128)} %bitcast.5), custom_call_target="tpu_custom_call" | custom-call | tf_op jit(solution)/shard_map/pallas_call | solution.py:245
  32.3 36.1 %shard_map.52 = f32[512,128]{1,0:T(8,128)} custom-call(f32[512,128]{1,0:T(8,128)} %bitcast.8), custom_call_target="tpu_custom_call" | custom-call | tf_op jit(solution)/shard_map/pallas_call | solution.py:361
  68.4 15.9 %shard_map.53 = f32[64,8,128]{2,1,0:T(8,128)} custom-call(f32[408]{0:T(512)} %multiply_select_fusion.1.pen_z_ref, f32[128]{0:T(128)} %compare_select_fusion.pen_y_ref, f32[64,8,128]{2,1,0:T(8,128)} %bitcast.6), custom_call_target="tpu_custom_call" | custom-call | tf_op jit(solution)/shard_map/pallas_call | solution.py:389
  84.4 32.5 %shard_map.54.src_ref = f32[512,128]{1,0:T(8,128)} custom-call(f32[512,128]{1,0:T(8,128)} %bitcast.7), custom_call_target="tpu_custom_call" | custom-call | tf_op jit(solution)/shard_map/pallas_call | solution.py:361
  116.8 0.0 copy-start
  116.8 1.8 %shard_map.55 = f32[128,512]{1,0:T(8,128)} custom-call(f32[512,128]{1,0:T(8,128)} %shard_map.54.src_ref), custom_call_target="tpu_custom_call" | custom-call | tf_op jit(solution)/shard_map/pallas_call | solution.py:245
  118.7 0.0 copy-done
  118.7 0.7 copy.6
Async XLA Ops:
  116.8 1.8 %copy-start = (f32[4,4,8,512]{3,2,1,0:T(8,128)S(1)}, f32[4,4,8,512]{3,2,1,0:T(8,128)}, u32[]{:S(2)}) copy-start(f32[4,4,8,512]{3,2,1,0:T(8,128)} %shard_map.50) | copy-start | bytes 786436

commit v10 on v6

--- a/solution.py
+++ b/solution.py
@@ -1,3 +1,4 @@
+import functools
 import math
 
 import jax
@@ -186,7 +187,7 @@
     ).astype(jnp.float32)
 
 
-def scan_offsets(u_ref, pen_ref, out_ref, n_out, group, nrot, q_range):
+def scan_offsets(u_ref, pen_ref, out_ref, n_out, group, nrot, q_range, after_group=None):
     for g0 in range(0, n_out, group):
         q_lo, q_hi = q_range(g0, group)
         q_hi = min(q_hi, pen_ref.shape[0] // nrot - 1, u_ref.shape[1] - g0 - group)
@@ -199,6 +200,8 @@
 
         init = jnp.full((group,) + tuple(out_ref.shape[1:]), jnp.inf, jnp.float32)
         out_ref[g0:g0 + group] = lax.fori_loop(q_lo, q_hi + 1, body, init, unroll=2)
+        if after_group is not None:
+            after_group(g0, group)
 
 
 def build_rotations(pad_ref, u_ref, nrot, pick, chunk=8):
@@ -214,7 +217,7 @@
     lax.fori_loop(0, u_ref.shape[1] // chunk, body, 0)
 
 
-def xpass_kernel(pen_ref, src_ref, out_ref, pad_ref, u_ref):
+def xpass_kernel(pen_ref, src_ref, out_ref, pad_ref, u_ref, after_group=None):
     lines, nx = src_ref.shape
     reach = KERNEL
     padc = reach // 8
@@ -230,7 +233,7 @@
         hi = (reach + nx - 1 - 8 * g0) // 8
         return lo, hi
 
-    scan_offsets(u_ref, pen_ref, out_ref, n_out, 16, 8, q_range)
+    scan_offsets(u_ref, pen_ref, out_ref, n_out, 16, 8, q_range, after_group)
 
 
 def transpose_kernel(src_ref, out_ref):
@@ -250,7 +253,7 @@
     )(*args)
 
 
-def zy_kernel(pen_z_ref, pen_y_ref, src_ref, out_ref, pad_ref, u_ref, w_ref):
+def zy_kernel(pen_z_ref, pen_y_ref, src_ref, out_ref, pad_ref, u_ref, w_ref, before_y=None, after_group=None):
     n_out = src_ref.shape[0]
     padc = KERNEL // 4
     pad_ref[...] = jnp.full(pad_ref.shape, jnp.inf, jnp.float32)
@@ -283,6 +286,8 @@
         return carry
 
     lax.fori_loop(0, n_out // 8, wbody, 0)
+    if before_y is not None:
+        before_y()
     group = 8
     shifts = []
     for db in range(-8, 8):
@@ -304,40 +309,158 @@
                 acc[g] = jnp.minimum(acc[g], v + penvec)
         for g in range(group):
             out_ref[a0 + g] = acc[g]
+        if after_group is not None:
+            after_group(a0, group)
         return carry
 
     lax.fori_loop(0, n_out // group, ybody, 0)
+
+
+class Exchange:
+    def __init__(self, mid_ref, blk_ref, recv_ref, sems):
+        self.n_gz, self.n_gy = lax.axis_size("gz"), lax.axis_size("gy")
+        self.a, self.b = lax.axis_index("gz"), lax.axis_index("gy")
+        self.mid_ref, self.blk_ref, self.recv_ref, self.sems = mid_ref, blk_ref, recv_ref, sems
+        self.barrier = pltpu.get_barrier_semaphore()
+
+    def greet(self):
+        a, b, n_gz, n_gy = self.a, self.b, self.n_gz, self.n_gy
+
+        def greet_gy(k, carry):
+            pl.semaphore_signal(self.barrier, inc=1, device_id=(a, lax.rem(b + k, n_gy)),
+                                device_id_type=MESH)
+            return carry
+
+        def greet_gz(k, carry):
+            pl.semaphore_signal(self.barrier, inc=1, device_id=(lax.rem(a + k, n_gz), b),
+                                device_id_type=MESH)
+            return carry
+
+        lax.fori_loop(1, n_gy, greet_gy, 0)
+        lax.fori_loop(1, n_gz, greet_gz, 0)
+
+    def wait_greetings(self):
+        pl.semaphore_wait(self.barrier, self.n_gy - 1 + self.n_gz - 1)
+
+    def tile_copy(self, tiles_ref, p):
+        rows = pl.ds(pl.multiple_of(self.a * self.n_gy, 8), self.n_gy)
+        return pltpu.make_async_remote_copy(
+            src_ref=tiles_ref.at[p], dst_ref=self.mid_ref.at[rows], send_sem=self.sems.at[0],
+            recv_sem=self.sems.at[1], device_id=(p, self.b), device_id_type=MESH)
+
+    def send_tile(self, tiles_ref, p):
+        @pl.when(p != self.a)
+        def _():
+            self.tile_copy(tiles_ref, p).start()
+
+    def finish(self, tiles_ref, out_ref):
+        a, b, n_gz, n_gy = self.a, self.b, self.n_gz, self.n_gy
+        mid_ref, blk_ref, recv_ref, sems = self.mid_ref, self.blk_ref, self.recv_ref, self.sems
+        own_rows = pl.ds(pl.multiple_of(a * n_gy, 8), n_gy)
+        own = pltpu.make_async_copy(tiles_ref.at[a], mid_ref.at[own_rows], sems.at[2])
+        own.start()
+        own.wait()
+        rest = pl.ds(0, (n_gz - 1) * n_gy)
+        total = pltpu.make_async_remote_copy(
+            src_ref=mid_ref.at[rest], dst_ref=mid_ref.at[rest], send_sem=sems.at[0],
+            recv_sem=sems.at[1], device_id=(lax.rem(a + 1, n_gz), b), device_id_type=MESH)
+        total.wait_recv()
+        total.wait_send()
+        for i in range(n_gy):
+            blk_ref[i * n_gz:(i + 1) * n_gz] = mid_ref[pl.ds(i, n_gz, stride=n_gy)]
+
+        def send(k, carry):
+            p = lax.rem(b + k, n_gy)
+            pltpu.make_async_remote_copy(
+                src_ref=blk_ref.at[pl.ds(pl.multiple_of(p * n_gz, 8), n_gz)],
+                dst_ref=recv_ref.at[pl.ds(pl.multiple_of(b * n_gz, 8), n_gz)], send_sem=sems.at[3],
+                recv_sem=sems.at[4], device_id=(a, p), device_id_type=MESH).start()
+            return carry
+
+        lax.fori_loop(1, n_gy, send, 0)
+        block = pl.ds(pl.multiple_of(b * n_gz, 8), n_gz)
+        own = pltpu.make_async_copy(blk_ref.at[block], recv_ref.at[block], sems.at[5])
+        own.start()
+        own.wait()
+        rest = pl.ds(0, (n_gy - 1) * n_gz)
+        total = pltpu.make_async_remote_copy(
+            src_ref=blk_ref.at[rest], dst_ref=recv_ref.at[rest], send_sem=sems.at[3],
+            recv_sem=sems.at[4], device_id=(a, lax.rem(b + 1, n_gy)), device_id_type=MESH)
+        total.wait_recv()
+        total.wait_send()
+        for j in range(n_gz):
+            out_ref[j * n_gy:(j + 1) * n_gy] = recv_ref[pl.ds(j, n_gy, stride=n_gz)]
+
+
+def exchange_scratch(tiles_shape):
+    rows = (tiles_shape[0] * tiles_shape[1], tiles_shape[2])
+    return [pltpu.VMEM(tiles_shape, jnp.float32)] + [pltpu.VMEM(rows, jnp.float32)] * 3 + [
+        pltpu.SemaphoreType.DMA((6,))]
+
+
+def xpass_send_kernel(pen_ref, src_ref, out_ref, pad_ref, u_ref, tiles_ref, mid_ref, blk_ref, recv_ref, sems):
+    ex = Exchange(mid_ref, blk_ref, recv_ref, sems)
+    ex.greet()
+
+    def after_group(g0, group):
+        if g0 == 0:
+            ex.wait_greetings()
+        for t in range(g0, g0 + group):
+            ex.send_tile(tiles_ref, t)
+
+    xpass_kernel(pen_ref, src_ref, tiles_ref, pad_ref, u_ref, after_group)
+    ex.finish(tiles_ref, out_ref)
+
+
+def zy_send_kernel(pen_z_ref, pen_y_ref, src_ref, out_ref, pad_ref, u_ref, w_ref, tiles_ref, mid_ref,
+                   blk_ref, recv_ref, sems):
+    ex = Exchange(mid_ref, blk_ref, recv_ref, sems)
+    ex.greet()
+
+    def after_group(a0, group):
+        for g in range(group):
+            ex.send_tile(tiles_ref, a0 + g)
+
+    zy_kernel(pen_z_ref, pen_y_ref, src_ref, tiles_ref, pad_ref, u_ref, w_ref, ex.wait_greetings, after_group)
+    ex.finish(tiles_ref, out_ref)
 
 
 def regularize(current):
     levels, nz, ny, nx = current.shape
     lines = levels * nz * ny
-    assert lines == 128 and nx % 8 == 0
     n_gz = lax.axis_size("gz")
     n_gy = lax.axis_size("gy")
-    assert n_gz * n_gy == nx and ny == 8 and n_gy == 8
+    assert lines == 128 and ny == 8 and n_gy == 8 and n_gz * n_gy == nx
+    smem = pl.BlockSpec(memory_space=pltpu.SMEM)
+    vmem = pl.BlockSpec(memory_space=pltpu.VMEM)
+    tiles = (n_gz, n_gy, lines)
     xq = (KERNEL + 7) // 8
     nxo = nx // 8
     pen_x = penalty_table(8 * (xq * 2 + 2), KERNEL)
     xu = -(-(nxo + 2 * xq + 2) // 8) * 8
-    t1 = local_call(xpass_kernel, (nxo, 8, lines), [(xu + 8, 8, lines), (8, xu, 8, lines)],
-                    pen_x, current.reshape(lines, nx))
-    r1 = lax.all_to_all(t1.reshape(nx, lines), ("gz", "gy"), 0, 0, tiled=True)
-    r1 = r1.reshape(n_gz, n_gy, lines)
+    r1 = pl.pallas_call(
+        xpass_send_kernel,
+        out_shape=jax.ShapeDtypeStruct((nx, lines), jnp.float32),
+        in_specs=[smem, vmem],
+        out_specs=vmem,
+        scratch_shapes=[pltpu.VMEM((xu + 8, 8, lines), jnp.float32),
+                        pltpu.VMEM((8, xu, 8, lines), jnp.float32)] + exchange_scratch(tiles),
+        compiler_params=pltpu.CompilerParams(collective_id=1, has_side_effects=True),
+    )(pen_x, current.reshape(lines, nx))
     zq = KERNEL // 4
     pen_z = penalty_table(4 * (2 * zq + 2), KERNEL)
     zu = -(-(n_gz + 2 * zq + 2) // 8) * 8
     pen_y = penalty_table(8 * 2 * n_gy, 8 * n_gy)
-    t2 = pl.pallas_call(
-        zy_kernel,
-        out_shape=jax.ShapeDtypeStruct(r1.shape, jnp.float32),
-        in_specs=[pl.BlockSpec(memory_space=pltpu.SMEM)] * 2 + [pl.BlockSpec(memory_space=pltpu.VMEM)],
-        out_specs=pl.BlockSpec(memory_space=pltpu.VMEM),
+    r2 = pl.pallas_call(
+        zy_send_kernel,
+        out_shape=jax.ShapeDtypeStruct((nx, lines), jnp.float32),
+        in_specs=[smem, smem, vmem],
+        out_specs=vmem,
         scratch_shapes=[pltpu.VMEM((zu + 8, 8, lines), jnp.float32),
                         pltpu.VMEM((4, zu, 8, lines), jnp.float32),
-                        pltpu.VMEM((8, n_gz, 8, lines), jnp.float32)],
-    )(pen_z, pen_y, r1)
-    r2 = lax.all_to_all(t2.reshape(nx, lines), ("gz", "gy"), 0, 0, tiled=True)
+                        pltpu.VMEM((8, n_gz, 8, lines), jnp.float32)] + exchange_scratch(tiles),
+        compiler_params=pltpu.CompilerParams(collective_id=2, has_side_effects=True),
+    )(pen_z, pen_y, r1.reshape(tiles))
     out = local_call(transpose_kernel, (lines, nx), [], r2)
     return out.reshape(current.shape)
 

time: 130 us -> 105 us (0.81)
  the two profiles are of different devices: /device:TPU:6 before, /device:TPU:63 now
where the time goes in v10:
time: 105 us
  Pallas kernels  102 us (97%)
  other arithmetic  1.66 us (2%)
    pallas_call x1, Pallas kernels, regularize(): pl.pallas_call(zy_send_kernel, out_shape=jax.ShapeDtypeStruct((nx, lines)...  46.1 us
    pallas_call x1, Pallas kernels, regularize(): pl.pallas_call(xpass_send_kernel, out_shape=jax.ShapeDtypeStruct((nx, lin...  30.9 us
    pallas_call x1, Pallas kernels, evolve_all(): pl.pallas_call(evolve_kernel, out_shape=jax.ShapeDtypeStruct(current.shap...  22.8 us

profile of v10, /device:TPU:63, one launch (start us, length us, event | category | flops | bytes accessed | tf_op | source)
XLA Modules:
  0.0 104.7 jit_solution(10875122999848402833)
XLA Ops:
  0.6 0.5 compare_select_fusion.pen_y_ref
  1.1 0.6 multiply_select_fusion.1.pen_z_ref
  1.7 0.6 multiply_select_fusion.pen_ref
  2.3 22.8 %shard_map.50 = f32[4,4,8,512]{3,2,1,0:T(8,128)} custom-call(f32[16]{0:T(128)} %means_ref.1, f32[4,4,8,512]{3,2,1,0:T(8,128)} %cur_ref.1, f32[4,8,512]{2,1,0:T(8,128)} %ct_ref.1), custom_call_target="tpu_custom_call" | custom-call | tf_op jit(solution)/shard_map/pallas_call | solution.py:165
  25.1 30.9 %shard_map.51 = f32[512,128]{1,0:T(8,128)} custom-call(f32[416]{0:T(512)} %multiply_select_fusion.pen_ref, f32[128,512]{1,0:T(8,128)} %bitcast.3), custom_call_target="tpu_custom_call" | custom-call | tf_op jit(solution)/shard_map/pallas_call | solution.py:441
  56.0 46.1 %shard_map.52.src_ref = f32[512,128]{1,0:T(8,128)} custom-call(f32[408]{0:T(512)} %multiply_select_fusion.1.pen_z_ref, f32[128]{0:T(128)} %compare_select_fusion.pen_y_ref, f32[64,8,128]{2,1,0:T(8,128)} %bitcast.4), custom_call_target="tpu_custom_call" | custom-call | tf_op jit(solution)/shard_map/pallas_call | solution.py:454
  102.1 0.0 copy-start
  102.1 1.8 %shard_map.53 = f32[128,512]{1,0:T(8,128)} custom-call(f32[512,128]{1,0:T(8,128)} %shard_map.52.src_ref), custom_call_target="tpu_custom_call" | custom-call | tf_op jit(solution)/shard_map/pallas_call | solution.py:247
  104.0 0.0 copy-done
  104.0 0.7 copy.6
Async XLA Ops:
  102.1 1.8 %copy-start = (f32[4,4,8,512]{3,2,1,0:T(8,128)S(1)}, f32[4,4,8,512]{3,2,1,0:T(8,128)}, u32[]{:S(2)}) copy-start(f32[4,4,8,512]{3,2,1,0:T(8,128)} %shard_map.50) | copy-start | bytes 786436

commit v11 on v10

--- a/solution.py
+++ b/solution.py
@@ -317,10 +317,10 @@
 
 
 class Exchange:
-    def __init__(self, mid_ref, blk_ref, recv_ref, sems):
+    def __init__(self, mid_ref, recv_ref, sems):
         self.n_gz, self.n_gy = lax.axis_size("gz"), lax.axis_size("gy")
         self.a, self.b = lax.axis_index("gz"), lax.axis_index("gy")
-        self.mid_ref, self.blk_ref, self.recv_ref, self.sems = mid_ref, blk_ref, recv_ref, sems
+        self.mid_ref, self.recv_ref, self.sems = mid_ref, recv_ref, sems
         self.barrier = pltpu.get_barrier_semaphore()
 
     def greet(self):
@@ -342,84 +342,72 @@
     def wait_greetings(self):
         pl.semaphore_wait(self.barrier, self.n_gy - 1 + self.n_gz - 1)
 
-    def tile_copy(self, tiles_ref, p):
-        rows = pl.ds(pl.multiple_of(self.a * self.n_gy, 8), self.n_gy)
-        return pltpu.make_async_remote_copy(
-            src_ref=tiles_ref.at[p], dst_ref=self.mid_ref.at[rows], send_sem=self.sems.at[0],
-            recv_sem=self.sems.at[1], device_id=(p, self.b), device_id_type=MESH)
-
-    def send_tile(self, tiles_ref, p):
-        @pl.when(p != self.a)
-        def _():
-            self.tile_copy(tiles_ref, p).start()
+    def send_rows(self, tiles_ref, t0, count):
+        a, b, n_gy = self.a, self.b, self.n_gy
+        for k in range(1, n_gy):
+            p = lax.rem(b + k, n_gy)
+            pltpu.make_async_remote_copy(
+                src_ref=tiles_ref.at[pl.ds(t0, count), pl.ds(p, 1)],
+                dst_ref=self.mid_ref.at[pl.ds(t0, count), pl.ds(b, 1)], send_sem=self.sems.at[0],
+                recv_sem=self.sems.at[1], device_id=(a, p), device_id_type=MESH).start()
 
     def finish(self, tiles_ref, out_ref):
         a, b, n_gz, n_gy = self.a, self.b, self.n_gz, self.n_gy
-        mid_ref, blk_ref, recv_ref, sems = self.mid_ref, self.blk_ref, self.recv_ref, self.sems
-        own_rows = pl.ds(pl.multiple_of(a * n_gy, 8), n_gy)
-        own = pltpu.make_async_copy(tiles_ref.at[a], mid_ref.at[own_rows], sems.at[2])
+        mid_ref, recv_ref, sems = self.mid_ref, self.recv_ref, self.sems
+        own = pltpu.make_async_copy(tiles_ref.at[:, pl.ds(b, 1)], mid_ref.at[:, pl.ds(b, 1)], sems.at[2])
         own.start()
         own.wait()
-        rest = pl.ds(0, (n_gz - 1) * n_gy)
         total = pltpu.make_async_remote_copy(
-            src_ref=mid_ref.at[rest], dst_ref=mid_ref.at[rest], send_sem=sems.at[0],
-            recv_sem=sems.at[1], device_id=(lax.rem(a + 1, n_gz), b), device_id_type=MESH)
+            src_ref=tiles_ref.at[:, pl.ds(0, n_gy - 1)], dst_ref=mid_ref.at[:, pl.ds(0, n_gy - 1)],
+            send_sem=sems.at[0], recv_sem=sems.at[1], device_id=(a, lax.rem(b + 1, n_gy)),
+            device_id_type=MESH)
         total.wait_recv()
         total.wait_send()
-        for i in range(n_gy):
-            blk_ref[i * n_gz:(i + 1) * n_gz] = mid_ref[pl.ds(i, n_gz, stride=n_gy)]
 
         def send(k, carry):
-            p = lax.rem(b + k, n_gy)
+            p = lax.rem(a + k, n_gz)
             pltpu.make_async_remote_copy(
-                src_ref=blk_ref.at[pl.ds(pl.multiple_of(p * n_gz, 8), n_gz)],
-                dst_ref=recv_ref.at[pl.ds(pl.multiple_of(b * n_gz, 8), n_gz)], send_sem=sems.at[3],
-                recv_sem=sems.at[4], device_id=(a, p), device_id_type=MESH).start()
+                src_ref=mid_ref.at[pl.ds(p, 1)], dst_ref=recv_ref.at[pl.ds(a, 1)], send_sem=sems.at[3],
+                recv_sem=sems.at[4], device_id=(p, b), device_id_type=MESH).start()
             return carry
 
-        lax.fori_loop(1, n_gy, send, 0)
-        block = pl.ds(pl.multiple_of(b * n_gz, 8), n_gz)
-        own = pltpu.make_async_copy(blk_ref.at[block], recv_ref.at[block], sems.at[5])
+        lax.fori_loop(1, n_gz, send, 0, unroll=4)
+        own = pltpu.make_async_copy(mid_ref.at[pl.ds(a, 1)], recv_ref.at[pl.ds(a, 1)], sems.at[5])
         own.start()
         own.wait()
-        rest = pl.ds(0, (n_gy - 1) * n_gz)
         total = pltpu.make_async_remote_copy(
-            src_ref=blk_ref.at[rest], dst_ref=recv_ref.at[rest], send_sem=sems.at[3],
-            recv_sem=sems.at[4], device_id=(a, lax.rem(b + 1, n_gy)), device_id_type=MESH)
+            src_ref=mid_ref.at[pl.ds(0, n_gz - 1)], dst_ref=recv_ref.at[pl.ds(0, n_gz - 1)],
+            send_sem=sems.at[3], recv_sem=sems.at[4], device_id=(lax.rem(a + 1, n_gz), b),
+            device_id_type=MESH)
         total.wait_recv()
         total.wait_send()
-        for j in range(n_gz):
-            out_ref[j * n_gy:(j + 1) * n_gy] = recv_ref[pl.ds(j, n_gy, stride=n_gz)]
+        out_ref[...] = recv_ref[...]
 
 
 def exchange_scratch(tiles_shape):
-    rows = (tiles_shape[0] * tiles_shape[1], tiles_shape[2])
-    return [pltpu.VMEM(tiles_shape, jnp.float32)] + [pltpu.VMEM(rows, jnp.float32)] * 3 + [
-        pltpu.SemaphoreType.DMA((6,))]
-
-
-def xpass_send_kernel(pen_ref, src_ref, out_ref, pad_ref, u_ref, tiles_ref, mid_ref, blk_ref, recv_ref, sems):
-    ex = Exchange(mid_ref, blk_ref, recv_ref, sems)
+    return [pltpu.VMEM(tiles_shape, jnp.float32)] * 3 + [pltpu.SemaphoreType.DMA((6,))]
+
+
+def xpass_send_kernel(pen_ref, src_ref, out_ref, pad_ref, u_ref, tiles_ref, mid_ref, recv_ref, sems):
+    ex = Exchange(mid_ref, recv_ref, sems)
     ex.greet()
 
     def after_group(g0, group):
         if g0 == 0:
             ex.wait_greetings()
-        for t in range(g0, g0 + group):
-            ex.send_tile(tiles_ref, t)
+        ex.send_rows(tiles_ref, g0, group)
 
     xpass_kernel(pen_ref, src_ref, tiles_ref, pad_ref, u_ref, after_group)
     ex.finish(tiles_ref, out_ref)
 
 
 def zy_send_kernel(pen_z_ref, pen_y_ref, src_ref, out_ref, pad_ref, u_ref, w_ref, tiles_ref, mid_ref,
-                   blk_ref, recv_ref, sems):
-    ex = Exchange(mid_ref, blk_ref, recv_ref, sems)
+                   recv_ref, sems):
+    ex = Exchange(mid_ref, recv_ref, sems)
     ex.greet()
 
     def after_group(a0, group):
-        for g in range(group):
-            ex.send_tile(tiles_ref, a0 + g)
+        ex.send_rows(tiles_ref, a0, group)
 
     zy_kernel(pen_z_ref, pen_y_ref, src_ref, tiles_ref, pad_ref, u_ref, w_ref, ex.wait_greetings, after_group)
     ex.finish(tiles_ref, out_ref)
@@ -440,7 +428,7 @@
     xu = -(-(nxo + 2 * xq + 2) // 8) * 8
     r1 = pl.pallas_call(
         xpass_send_kernel,
-        out_shape=jax.ShapeDtypeStruct((nx, lines), jnp.float32),
+        out_shape=jax.ShapeDtypeStruct(tiles, jnp.float32),
         in_specs=[smem, vmem],
         out_specs=vmem,
         scratch_shapes=[pltpu.VMEM((xu + 8, 8, lines), jnp.float32),
@@ -453,15 +441,15 @@
     pen_y = penalty_table(8 * 2 * n_gy, 8 * n_gy)
     r2 = pl.pallas_call(
         zy_send_kernel,
-        out_shape=jax.ShapeDtypeStruct((nx, lines), jnp.float32),
+        out_shape=jax.ShapeDtypeStruct(tiles, jnp.float32),
         in_specs=[smem, smem, vmem],
         out_specs=vmem,
         scratch_shapes=[pltpu.VMEM((zu + 8, 8, lines), jnp.float32),
                         pltpu.VMEM((4, zu, 8, lines), jnp.float32),
                         pltpu.VMEM((8, n_gz, 8, lines), jnp.float32)] + exchange_scratch(tiles),
         compiler_params=pltpu.CompilerParams(collective_id=2, has_side_effects=True),
-    )(pen_z, pen_y, r1.reshape(tiles))
-    out = local_call(transpose_kernel, (lines, nx), [], r2)
+    )(pen_z, pen_y, r1)
+    out = local_call(transpose_kernel, (lines, nx), [], r2.reshape(nx, lines))
     return out.reshape(current.shape)
 
 

time: 105 us -> 103 us (0.981)
  the two profiles are of different devices: /device:TPU:63 before, /device:TPU:6 now
where the time goes in v11:
time: 103 us
  Pallas kernels  99.9 us (97%)
  other arithmetic  1.66 us (2%)
    pallas_call x1, Pallas kernels, regularize(): pl.pallas_call(xpass_send_kernel, out_shape=jax.ShapeDtypeStruct(tiles, j...  41.4 us
    pallas_call x1, Pallas kernels, regularize(): pl.pallas_call(zy_send_kernel, out_shape=jax.ShapeDtypeStruct(tiles, jnp....  38.9 us
    pallas_call x1, Pallas kernels, evolve_all(): pl.pallas_call(evolve_kernel, out_shape=jax.ShapeDtypeStruct(current.shap...  17.8 us

profile of v11, /device:TPU:6, one launch (start us, length us, event | category | flops | bytes accessed | tf_op | source)
XLA Modules:
  0.0 102.9 jit_solution(9282427777625749904)
XLA Ops:
  0.6 0.5 compare_select_fusion.pen_y_ref
  1.1 0.6 multiply_select_fusion.1.pen_z_ref
  1.7 0.6 multiply_select_fusion.pen_ref
  2.3 17.8 %shard_map.50 = f32[4,4,8,512]{3,2,1,0:T(8,128)} custom-call(f32[16]{0:T(128)} %means_ref.1, f32[4,4,8,512]{3,2,1,0:T(8,128)} %cur_ref.1, f32[4,8,512]{2,1,0:T(8,128)} %ct_ref.1), custom_call_target="tpu_custom_call" | custom-call | tf_op jit(solution)/shard_map/pallas_call | solution.py:165
  20.1 41.4 %shard_map.51.src_ref = f32[64,8,128]{2,1,0:T(8,128)} custom-call(f32[416]{0:T(512)} %multiply_select_fusion.pen_ref, f32[128,512]{1,0:T(8,128)} %bitcast.3), custom_call_target="tpu_custom_call" | custom-call | tf_op jit(solution)/shard_map/pallas_call | solution.py:429
  61.5 38.9 %shard_map.52 = f32[64,8,128]{2,1,0:T(8,128)} custom-call(f32[408]{0:T(512)} %multiply_select_fusion.1.pen_z_ref, f32[128]{0:T(128)} %compare_select_fusion.pen_y_ref, f32[64,8,128]{2,1,0:T(8,128)} %shard_map.51.src_ref), custom_call_target="tpu_custom_call" | custom-call | tf_op jit(solution)/shard_map/pallas_call | solution.py:442
  100.4 0.0 copy-start
  100.4 1.8 %shard_map.53 = f32[128,512]{1,0:T(8,128)} custom-call(f32[512,128]{1,0:T(8,128)} %bitcast.4), custom_call_target="tpu_custom_call" | custom-call | tf_op jit(solution)/shard_map/pallas_call | solution.py:247
  102.2 0.0 copy-done
  102.2 0.7 copy.6
Async XLA Ops:
  100.4 1.8 %copy-start = (f32[4,4,8,512]{3,2,1,0:T(8,128)S(1)}, f32[4,4,8,512]{3,2,1,0:T(8,128)}, u32[]{:S(2)}) copy-start(f32[4,4,8,512]{3,2,1,0:T(8,128)} %shard_map.50) | copy-start | bytes 786436

commit v12 on v11

--- a/solution.py
+++ b/solution.py
@@ -2,6 +2,7 @@
 import math
 
 import jax
+import numpy as np
 import jax.numpy as jnp
 from jax import lax
 from jax.experimental import pallas as pl
@@ -181,10 +182,9 @@
 
 
 def penalty_table(count, offset):
-    distance = (jnp.arange(count, dtype=jnp.int32) - offset).astype(jnp.float32)
-    return jnp.where(
-        jnp.abs(distance) <= KERNEL, PENALTY * (distance * distance), jnp.inf
-    ).astype(jnp.float32)
+    distance = (np.arange(count, dtype=np.int32) - offset).astype(np.float32)
+    table = np.where(np.abs(distance) <= KERNEL, np.float32(PENALTY) * (distance * distance), np.float32(np.inf))
+    return jnp.asarray(table.astype(np.float32))
 
 
 def scan_offsets(u_ref, pen_ref, out_ref, n_out, group, nrot, q_range, after_group=None):
@@ -351,7 +351,7 @@
                 dst_ref=self.mid_ref.at[pl.ds(t0, count), pl.ds(b, 1)], send_sem=self.sems.at[0],
                 recv_sem=self.sems.at[1], device_id=(a, p), device_id_type=MESH).start()
 
-    def finish(self, tiles_ref, out_ref):
+    def finish(self, tiles_ref, out_ref, transpose=False):
         a, b, n_gz, n_gy = self.a, self.b, self.n_gz, self.n_gy
         mid_ref, recv_ref, sems = self.mid_ref, self.recv_ref, self.sems
         own = pltpu.make_async_copy(tiles_ref.at[:, pl.ds(b, 1)], mid_ref.at[:, pl.ds(b, 1)], sems.at[2])
@@ -381,7 +381,10 @@
             device_id_type=MESH)
         total.wait_recv()
         total.wait_send()
-        out_ref[...] = recv_ref[...]
+        if transpose:
+            out_ref[...] = recv_ref[...].reshape(out_ref.shape[::-1]).T
+        else:
+            out_ref[...] = recv_ref[...]
 
 
 def exchange_scratch(tiles_shape):
@@ -410,7 +413,7 @@
         ex.send_rows(tiles_ref, a0, group)
 
     zy_kernel(pen_z_ref, pen_y_ref, src_ref, tiles_ref, pad_ref, u_ref, w_ref, ex.wait_greetings, after_group)
-    ex.finish(tiles_ref, out_ref)
+    ex.finish(tiles_ref, out_ref, transpose=True)
 
 
 def regularize(current):
@@ -441,7 +444,7 @@
     pen_y = penalty_table(8 * 2 * n_gy, 8 * n_gy)
     r2 = pl.pallas_call(
         zy_send_kernel,
-        out_shape=jax.ShapeDtypeStruct(tiles, jnp.float32),
+        out_shape=jax.ShapeDtypeStruct((lines, nx), jnp.float32),
         in_specs=[smem, smem, vmem],
         out_specs=vmem,
         scratch_shapes=[pltpu.VMEM((zu + 8, 8, lines), jnp.float32),
@@ -449,8 +452,7 @@
                         pltpu.VMEM((8, n_gz, 8, lines), jnp.float32)] + exchange_scratch(tiles),
         compiler_params=pltpu.CompilerParams(collective_id=2, has_side_effects=True),
     )(pen_z, pen_y, r1)
-    out = local_call(transpose_kernel, (lines, nx), [], r2.reshape(nx, lines))
-    return out.reshape(current.shape)
+    return r2.reshape(current.shape)
 
 
 def body(levels, ct_image, region_means):

time: 103 us -> 101 us (0.981)
  other arithmetic: 1.66 us -> 0 us
  Pallas kernels: 99.9 us -> 98.3 us
  local copies, waits for them, and re-layouts: 0.71 us -> 1.74 us
    select_n x3 -> x0, other arithmetic: 1.66 us -> none  [penalty_table(): jnp.where(jnp.abs(distance) <= KERNEL, PENALTY * (distance * distance), j...]
    pallas_call x2 -> x1, Pallas kernels: 40.7 us -> 39.1 us  [regularize(): pl.pallas_call(zy_send_kernel, out_shape=jax.ShapeDtypeStruct((lines, nx)...]
    unnamed x3 -> x6, local copies, waits for them, and re-layouts: 0.71 us -> 1.74 us
where the time goes in v12:
time: 101 us
  Pallas kernels  98.3 us (97%)
  local copies, waits for them, and re-layouts  1.74 us (2%)
    pallas_call x1, Pallas kernels, regularize(): pl.pallas_call(xpass_send_kernel, out_shape=jax.ShapeDtypeStruct(tiles, j...  41.4 us
    pallas_call x1, Pallas kernels, regularize(): pl.pallas_call(zy_send_kernel, out_shape=jax.ShapeDtypeStruct((lines, nx)...  39.1 us
    pallas_call x1, Pallas kernels, evolve_all(): pl.pallas_call(evolve_kernel, out_shape=jax.ShapeDtypeStruct(current.shap...  17.8 us

profile of v12, /device:TPU:6, one launch (start us, length us, event | category | flops | bytes accessed | tf_op | source)
XLA Modules:
  0.0 100.7 jit_solution(7497963400653212218)
XLA Ops:
  0.6 17.8 %shard_map.77 = f32[4,4,8,512]{3,2,1,0:T(8,128)} custom-call(f32[16]{0:T(128)} %means_ref.1, f32[4,4,8,512]{3,2,1,0:T(8,128)} %cur_ref.1, f32[4,8,512]{2,1,0:T(8,128)} %ct_ref.1), custom_call_target="tpu_custom_call" | custom-call | tf_op jit(solution)/shard_map/pallas_call | solution.py:166
  18.4 41.4 %shard_map.78.src_ref = f32[64,8,128]{2,1,0:T(8,128)} custom-call(f32[416]{0:T(512)} %constant.6.clone.pen_ref, f32[128,512]{1,0:T(8,128)} %bitcast.2), custom_call_target="tpu_custom_call" | custom-call | tf_op jit(solution)/shard_map/pallas_call | solution.py:432
  59.8 0.0 copy-start
  59.8 39.1 %shard_map.79 = f32[128,512]{1,0:T(8,128)} custom-call(f32[408]{0:T(512)} %constant.7.clone.pen_z_ref, f32[128]{0:T(128)} %constant.8.clone.pen_y_ref, f32[64,8,128]{2,1,0:T(8,128)} %shard_map.78.src_ref), custom_call_target="tpu_custom_call" | custom-call | tf_op jit(solution)/shard_map/pallas_call | solution.py:445
  99.0 0.0 copy-done
  99.0 0.0 copy-start.1
  99.0 0.7 copy.10
  99.7 0.3 copy-done.1
  100.0 0.7 copy.11
Async XLA Ops:
  59.8 39.2 %copy-start = (f32[4,4,8,512]{3,2,1,0:T(8,128)S(1)}, f32[4,4,8,512]{3,2,1,0:T(8,128)}, u32[]{:S(2)}) copy-start(f32[4,4,8,512]{3,2,1,0:T(8,128)} %shard_map.77) | copy-start | bytes 786436
  99.0 1.0 %copy-start.1 = (f32[128,512]{1,0:T(8,128)S(1)}, f32[128,512]{1,0:T(8,128)}, u32[]{:S(2)}) copy-start(f32[128,512]{1,0:T(8,128)} %shard_map.79) | copy-start | bytes 786436

commit v13 on v12

--- a/solution.py
+++ b/solution.py
@@ -317,10 +317,11 @@
 
 
 class Exchange:
-    def __init__(self, mid_ref, recv_ref, sems):
+    def __init__(self, mid_ref, recv_ref, sems, grp_sems, count):
         self.n_gz, self.n_gy = lax.axis_size("gz"), lax.axis_size("gy")
         self.a, self.b = lax.axis_index("gz"), lax.axis_index("gy")
         self.mid_ref, self.recv_ref, self.sems = mid_ref, recv_ref, sems
+        self.grp_sems, self.count = grp_sems, count
         self.barrier = pltpu.get_barrier_semaphore()
 
     def greet(self):
@@ -342,36 +343,45 @@
     def wait_greetings(self):
         pl.semaphore_wait(self.barrier, self.n_gy - 1 + self.n_gz - 1)
 
-    def send_rows(self, tiles_ref, t0, count):
-        a, b, n_gy = self.a, self.b, self.n_gy
+    def send_rows(self, tiles_ref, g, t0):
+        a, b, n_gy, count = self.a, self.b, self.n_gy, self.count
         for k in range(1, n_gy):
             p = lax.rem(b + k, n_gy)
             pltpu.make_async_remote_copy(
                 src_ref=tiles_ref.at[pl.ds(t0, count), pl.ds(p, 1)],
                 dst_ref=self.mid_ref.at[pl.ds(t0, count), pl.ds(b, 1)], send_sem=self.sems.at[0],
-                recv_sem=self.sems.at[1], device_id=(a, p), device_id_type=MESH).start()
+                recv_sem=self.grp_sems.at[g], device_id=(a, p), device_id_type=MESH).start()
+        own = pltpu.make_async_copy(tiles_ref.at[pl.ds(t0, count), pl.ds(b, 1)],
+                                    self.mid_ref.at[pl.ds(t0, count), pl.ds(b, 1)], self.sems.at[2])
+        own.start()
+        own.wait()
+
+    def forward_group(self, g, t0):
+        a, b, n_gy, count = self.a, self.b, self.n_gy, self.count
+        pltpu.make_async_remote_copy(
+            src_ref=self.mid_ref.at[pl.ds(t0, count), pl.ds(0, n_gy - 1)],
+            dst_ref=self.mid_ref.at[pl.ds(t0, count), pl.ds(0, n_gy - 1)], send_sem=self.sems.at[0],
+            recv_sem=self.grp_sems.at[g], device_id=(a, lax.rem(b + 1, n_gy)),
+            device_id_type=MESH).wait_recv()
+        for j in range(count):
+            p = t0 + j
+
+            @pl.when(p != a)
+            def _(p=p):
+                pltpu.make_async_remote_copy(
+                    src_ref=self.mid_ref.at[pl.ds(p, 1)], dst_ref=self.recv_ref.at[pl.ds(a, 1)],
+                    send_sem=self.sems.at[3], recv_sem=self.sems.at[4], device_id=(p, b),
+                    device_id_type=MESH).start()
 
     def finish(self, tiles_ref, out_ref, transpose=False):
         a, b, n_gz, n_gy = self.a, self.b, self.n_gz, self.n_gy
         mid_ref, recv_ref, sems = self.mid_ref, self.recv_ref, self.sems
-        own = pltpu.make_async_copy(tiles_ref.at[:, pl.ds(b, 1)], mid_ref.at[:, pl.ds(b, 1)], sems.at[2])
-        own.start()
-        own.wait()
-        total = pltpu.make_async_remote_copy(
+        last = n_gz // self.count - 1
+        self.forward_group(last, last * self.count)
+        pltpu.make_async_remote_copy(
             src_ref=tiles_ref.at[:, pl.ds(0, n_gy - 1)], dst_ref=mid_ref.at[:, pl.ds(0, n_gy - 1)],
             send_sem=sems.at[0], recv_sem=sems.at[1], device_id=(a, lax.rem(b + 1, n_gy)),
-            device_id_type=MESH)
-        total.wait_recv()
-        total.wait_send()
-
-        def send(k, carry):
-            p = lax.rem(a + k, n_gz)
-            pltpu.make_async_remote_copy(
-                src_ref=mid_ref.at[pl.ds(p, 1)], dst_ref=recv_ref.at[pl.ds(a, 1)], send_sem=sems.at[3],
-                recv_sem=sems.at[4], device_id=(p, b), device_id_type=MESH).start()
-            return carry
-
-        lax.fori_loop(1, n_gz, send, 0, unroll=4)
+            device_id_type=MESH).wait_send()
         own = pltpu.make_async_copy(mid_ref.at[pl.ds(a, 1)], recv_ref.at[pl.ds(a, 1)], sems.at[5])
         own.start()
         own.wait()
@@ -387,30 +397,41 @@
             out_ref[...] = recv_ref[...]
 
 
-def exchange_scratch(tiles_shape):
-    return [pltpu.VMEM(tiles_shape, jnp.float32)] * 3 + [pltpu.SemaphoreType.DMA((6,))]
-
-
-def xpass_send_kernel(pen_ref, src_ref, out_ref, pad_ref, u_ref, tiles_ref, mid_ref, recv_ref, sems):
-    ex = Exchange(mid_ref, recv_ref, sems)
+def exchange_scratch(tiles_shape, groups):
+    return [pltpu.VMEM(tiles_shape, jnp.float32)] * 3 + [pltpu.SemaphoreType.DMA((6,)),
+                                                         pltpu.SemaphoreType.DMA((groups,))]
+
+
+def xpass_send_kernel(pen_ref, src_ref, out_ref, pad_ref, u_ref, tiles_ref, mid_ref, recv_ref, sems, grp_sems):
+    ex = Exchange(mid_ref, recv_ref, sems, grp_sems, 16)
     ex.greet()
 
     def after_group(g0, group):
-        if g0 == 0:
+        assert group == ex.count
+        g = g0 // group
+        if g == 0:
             ex.wait_greetings()
-        ex.send_rows(tiles_ref, g0, group)
+        ex.send_rows(tiles_ref, g, g0)
+        if g >= 1:
+            ex.forward_group(g - 1, g0 - group)
 
     xpass_kernel(pen_ref, src_ref, tiles_ref, pad_ref, u_ref, after_group)
     ex.finish(tiles_ref, out_ref)
 
 
 def zy_send_kernel(pen_z_ref, pen_y_ref, src_ref, out_ref, pad_ref, u_ref, w_ref, tiles_ref, mid_ref,
-                   recv_ref, sems):
-    ex = Exchange(mid_ref, recv_ref, sems)
+                   recv_ref, sems, grp_sems):
+    ex = Exchange(mid_ref, recv_ref, sems, grp_sems, 8)
     ex.greet()
 
     def after_group(a0, group):
-        ex.send_rows(tiles_ref, a0, group)
+        assert group == ex.count
+        g = a0 // group
+        ex.send_rows(tiles_ref, g, a0)
+
+        @pl.when(g >= 1)
+        def _():
+            ex.forward_group(g - 1, a0 - group)
 
     zy_kernel(pen_z_ref, pen_y_ref, src_ref, tiles_ref, pad_ref, u_ref, w_ref, ex.wait_greetings, after_group)
     ex.finish(tiles_ref, out_ref, transpose=True)
@@ -435,7 +456,7 @@
         in_specs=[smem, vmem],
         out_specs=vmem,
         scratch_shapes=[pltpu.VMEM((xu + 8, 8, lines), jnp.float32),
-                        pltpu.VMEM((8, xu, 8, lines), jnp.float32)] + exchange_scratch(tiles),
+                        pltpu.VMEM((8, xu, 8, lines), jnp.float32)] + exchange_scratch(tiles, n_gz // 16),
         compiler_params=pltpu.CompilerParams(collective_id=1, has_side_effects=True),
     )(pen_x, current.reshape(lines, nx))
     zq = KERNEL // 4
@@ -449,7 +470,7 @@
         out_specs=vmem,
         scratch_shapes=[pltpu.VMEM((zu + 8, 8, lines), jnp.float32),
                         pltpu.VMEM((4, zu, 8, lines), jnp.float32),
-                        pltpu.VMEM((8, n_gz, 8, lines), jnp.float32)] + exchange_scratch(tiles),
+                        pltpu.VMEM((8, n_gz, 8, lines), jnp.float32)] + exchange_scratch(tiles, n_gz // 8),
         compiler_params=pltpu.CompilerParams(collective_id=2, has_side_effects=True),
     )(pen_z, pen_y, r1)
     return r2.reshape(current.shape)

time: 101 us -> 116 us (1.15)
  the two profiles are of different devices: /device:TPU:6 before, /device:TPU:96 now
where the time goes in v13:
time: 116 us
  Pallas kernels  113 us (97%)
  local copies, waits for them, and re-layouts  1.74 us (2%)
    pallas_call x1, Pallas kernels, regularize(): pl.pallas_call(zy_send_kernel, out_shape=jax.ShapeDtypeStruct((lines, nx)...  51.4 us
    pallas_call x1, Pallas kernels, regularize(): pl.pallas_call(xpass_send_kernel, out_shape=jax.ShapeDtypeStruct(tiles, j...  42.2 us
    pallas_call x1, Pallas kernels, evolve_all(): pl.pallas_call(evolve_kernel, out_shape=jax.ShapeDtypeStruct(current.shap...  19.7 us

profile of v13, /device:TPU:96, one launch (start us, length us, event | category | flops | bytes accessed | tf_op | source)
XLA Modules:
  0.0 115.7 jit_solution(15129979783619778150)
XLA Ops:
  0.6 19.7 %shard_map.77 = f32[4,4,8,512]{3,2,1,0:T(8,128)} custom-call(f32[16]{0:T(128)} %means_ref.1, f32[4,4,8,512]{3,2,1,0:T(8,128)} %cur_ref.1, f32[4,8,512]{2,1,0:T(8,128)} %ct_ref.1), custom_call_target="tpu_custom_call" | custom-call | tf_op jit(solution)/shard_map/pallas_call | solution.py:166
  20.4 42.2 %shard_map.78.src_ref = f32[64,8,128]{2,1,0:T(8,128)} custom-call(f32[416]{0:T(512)} %constant.6.clone.pen_ref, f32[128,512]{1,0:T(8,128)} %bitcast.2), custom_call_target="tpu_custom_call" | custom-call | tf_op jit(solution)/shard_map/pallas_call | solution.py:453
  62.5 0.0 copy-start
  62.5 51.4 %shard_map.79 = f32[128,512]{1,0:T(8,128)} custom-call(f32[408]{0:T(512)} %constant.7.clone.pen_z_ref, f32[128]{0:T(128)} %constant.8.clone.pen_y_ref, f32[64,8,128]{2,1,0:T(8,128)} %shard_map.78.src_ref), custom_call_target="tpu_custom_call" | custom-call | tf_op jit(solution)/shard_map/pallas_call | solution.py:466
  114.0 0.0 copy-done
  114.0 0.0 copy-start.1
  114.0 0.7 copy.10
  114.7 0.3 copy-done.1
  115.0 0.7 copy.11
Async XLA Ops:
  62.5 51.4 %copy-start = (f32[4,4,8,512]{3,2,1,0:T(8,128)S(1)}, f32[4,4,8,512]{3,2,1,0:T(8,128)}, u32[]{:S(2)}) copy-start(f32[4,4,8,512]{3,2,1,0:T(8,128)} %shard_map.77) | copy-start | bytes 786436
  114.0 1.0 copy-start.1

commit v14 on v13

--- a/solution.py
+++ b/solution.py
@@ -373,11 +373,12 @@
                     send_sem=self.sems.at[3], recv_sem=self.sems.at[4], device_id=(p, b),
                     device_id_type=MESH).start()
 
-    def finish(self, tiles_ref, out_ref, transpose=False):
+    def finish(self, tiles_ref, out_ref, pending, transpose=False):
         a, b, n_gz, n_gy = self.a, self.b, self.n_gz, self.n_gy
         mid_ref, recv_ref, sems = self.mid_ref, self.recv_ref, self.sems
-        last = n_gz // self.count - 1
-        self.forward_group(last, last * self.count)
+        groups = n_gz // self.count
+        for g in range(groups - pending, groups):
+            self.forward_group(g, g * self.count)
         pltpu.make_async_remote_copy(
             src_ref=tiles_ref.at[:, pl.ds(0, n_gy - 1)], dst_ref=mid_ref.at[:, pl.ds(0, n_gy - 1)],
             send_sem=sems.at[0], recv_sem=sems.at[1], device_id=(a, lax.rem(b + 1, n_gy)),
@@ -397,6 +398,10 @@
             out_ref[...] = recv_ref[...]
 
 
+def n_gz_groups(ex):
+    return ex.n_gz // ex.count
+
+
 def exchange_scratch(tiles_shape, groups):
     return [pltpu.VMEM(tiles_shape, jnp.float32)] * 3 + [pltpu.SemaphoreType.DMA((6,)),
                                                          pltpu.SemaphoreType.DMA((groups,))]
@@ -416,7 +421,7 @@
             ex.forward_group(g - 1, g0 - group)
 
     xpass_kernel(pen_ref, src_ref, tiles_ref, pad_ref, u_ref, after_group)
-    ex.finish(tiles_ref, out_ref)
+    ex.finish(tiles_ref, out_ref, 1)
 
 
 def zy_send_kernel(pen_z_ref, pen_y_ref, src_ref, out_ref, pad_ref, u_ref, w_ref, tiles_ref, mid_ref,
@@ -429,12 +434,8 @@
         g = a0 // group
         ex.send_rows(tiles_ref, g, a0)
 
-        @pl.when(g >= 1)
-        def _():
-            ex.forward_group(g - 1, a0 - group)
-
     zy_kernel(pen_z_ref, pen_y_ref, src_ref, tiles_ref, pad_ref, u_ref, w_ref, ex.wait_greetings, after_group)
-    ex.finish(tiles_ref, out_ref, transpose=True)
+    ex.finish(tiles_ref, out_ref, n_gz_groups(ex), transpose=True)
 
 
 def regularize(current):

time: 116 us -> 99.5 us (0.86)
  the two profiles are of different devices: /device:TPU:96 before, /device:TPU:6 now
where the time goes in v14:
time: 99.5 us; the launch traced here: 99.3 us
  Pallas kernels  96.9 us (97%)
  local copies, waits for them, and re-layouts  1.74 us (2%)
    pallas_call x1, Pallas kernels, regularize(): pl.pallas_call(xpass_send_kernel, out_shape=jax.ShapeDtypeStruct(tiles, j...  40.1 us
    pallas_call x1, Pallas kernels, regularize(): pl.pallas_call(zy_send_kernel, out_shape=jax.ShapeDtypeStruct((lines, nx)...  39 us
    pallas_call x1, Pallas kernels, evolve_all(): pl.pallas_call(evolve_kernel, out_shape=jax.ShapeDtypeStruct(current.shap...  17.8 us

profile of v14, /device:TPU:6, one launch (start us, length us, event | category | flops | bytes accessed | tf_op | source)
XLA Modules:
  0.0 99.3 jit_solution(4230659863606351475)
XLA Ops:
  0.6 17.8 %shard_map.77 = f32[4,4,8,512]{3,2,1,0:T(8,128)} custom-call(f32[16]{0:T(128)} %means_ref.1, f32[4,4,8,512]{3,2,1,0:T(8,128)} %cur_ref.1, f32[4,8,512]{2,1,0:T(8,128)} %ct_ref.1), custom_call_target="tpu_custom_call" | custom-call | tf_op jit(solution)/shard_map/pallas_call | solution.py:166
  18.4 40.1 %shard_map.78.src_ref = f32[64,8,128]{2,1,0:T(8,128)} custom-call(f32[416]{0:T(512)} %constant.6.clone.pen_ref, f32[128,512]{1,0:T(8,128)} %bitcast.2), custom_call_target="tpu_custom_call" | custom-call | tf_op jit(solution)/shard_map/pallas_call | solution.py:454
  58.5 0.0 copy-start
  58.5 39.0 %shard_map.79 = f32[128,512]{1,0:T(8,128)} custom-call(f32[408]{0:T(512)} %constant.7.clone.pen_z_ref, f32[128]{0:T(128)} %constant.8.clone.pen_y_ref, f32[64,8,128]{2,1,0:T(8,128)} %shard_map.78.src_ref), custom_call_target="tpu_custom_call" | custom-call | tf_op jit(solution)/shard_map/pallas_call | solution.py:467
  97.5 0.0 copy-done
  97.5 0.0 copy-start.1
  97.5 0.7 copy.10
  98.2 0.3 copy-done.1
  98.6 0.7 copy.11
Async XLA Ops:
  58.5 39.0 %copy-start = (f32[4,4,8,512]{3,2,1,0:T(8,128)S(1)}, f32[4,4,8,512]{3,2,1,0:T(8,128)}, u32[]{:S(2)}) copy-start(f32[4,4,8,512]{3,2,1,0:T(8,128)} %shard_map.77) | copy-start | bytes 786436
  97.5 1.0 %copy-start.1 = (f32[128,512]{1,0:T(8,128)S(1)}, f32[128,512]{1,0:T(8,128)}, u32[]{:S(2)}) copy-start(f32[128,512]{1,0:T(8,128)} %shard_map.79) | copy-start | bytes 786436

commit v15 on v14

--- a/solution.py
+++ b/solution.py
@@ -377,8 +377,26 @@
         a, b, n_gz, n_gy = self.a, self.b, self.n_gz, self.n_gy
         mid_ref, recv_ref, sems = self.mid_ref, self.recv_ref, self.sems
         groups = n_gz // self.count
-        for g in range(groups - pending, groups):
-            self.forward_group(g, g * self.count)
+        if pending < groups:
+            for g in range(groups - pending, groups):
+                self.forward_group(g, g * self.count)
+        else:
+            for g in range(groups):
+                t0 = g * self.count
+                pltpu.make_async_remote_copy(
+                    src_ref=mid_ref.at[pl.ds(t0, self.count), pl.ds(0, n_gy - 1)],
+                    dst_ref=mid_ref.at[pl.ds(t0, self.count), pl.ds(0, n_gy - 1)], send_sem=sems.at[0],
+                    recv_sem=self.grp_sems.at[g], device_id=(a, lax.rem(b + 1, n_gy)),
+                    device_id_type=MESH).wait_recv()
+
+            def send(k, carry):
+                p = lax.rem(a + k, n_gz)
+                pltpu.make_async_remote_copy(
+                    src_ref=mid_ref.at[pl.ds(p, 1)], dst_ref=recv_ref.at[pl.ds(a, 1)], send_sem=sems.at[3],
+                    recv_sem=sems.at[4], device_id=(p, b), device_id_type=MESH).start()
+                return carry
+
+            lax.fori_loop(1, n_gz, send, 0, unroll=4)
         pltpu.make_async_remote_copy(
             src_ref=tiles_ref.at[:, pl.ds(0, n_gy - 1)], dst_ref=mid_ref.at[:, pl.ds(0, n_gy - 1)],
             send_sem=sems.at[0], recv_sem=sems.at[1], device_id=(a, lax.rem(b + 1, n_gy)),

time: 99.5 us -> 103 us (1.035)
  Pallas kernels: 96.9 us -> 99.9 us
    pallas_call x1, Pallas kernels: 39 us -> 42.1 us  [regularize(): pl.pallas_call(zy_send_kernel, out_shape=jax.ShapeDtypeStruct((lines, nx)...]
where the time goes in v15:
time: 103 us; the launch traced here: 102 us
  Pallas kernels  99.9 us (97%)
  local copies, waits for them, and re-layouts  1.74 us (2%)
    pallas_call x1, Pallas kernels, regularize(): pl.pallas_call(zy_send_kernel, out_shape=jax.ShapeDtypeStruct((lines, nx)...  42.1 us
    pallas_call x1, Pallas kernels, regularize(): pl.pallas_call(xpass_send_kernel, out_shape=jax.ShapeDtypeStruct(tiles, j...  40.1 us
    pallas_call x1, Pallas kernels, evolve_all(): pl.pallas_call(evolve_kernel, out_shape=jax.ShapeDtypeStruct(current.shap...  17.8 us

profile of v15, /device:TPU:6, one launch (start us, length us, event | category | flops | bytes accessed | tf_op | source)
XLA Modules:
  0.0 102.3 jit_solution(12412323760398957010)
XLA Ops:
  0.6 17.8 %shard_map.77 = f32[4,4,8,512]{3,2,1,0:T(8,128)} custom-call(f32[16]{0:T(128)} %means_ref.1, f32[4,4,8,512]{3,2,1,0:T(8,128)} %cur_ref.1, f32[4,8,512]{2,1,0:T(8,128)} %ct_ref.1), custom_call_target="tpu_custom_call" | custom-call | tf_op jit(solution)/shard_map/pallas_call | solution.py:166
  18.4 40.1 %shard_map.78.src_ref = f32[64,8,128]{2,1,0:T(8,128)} custom-call(f32[416]{0:T(512)} %constant.6.clone.pen_ref, f32[128,512]{1,0:T(8,128)} %bitcast.2), custom_call_target="tpu_custom_call" | custom-call | tf_op jit(solution)/shard_map/pallas_call | solution.py:472
  58.5 0.0 copy-start
  58.5 42.1 %shard_map.79 = f32[128,512]{1,0:T(8,128)} custom-call(f32[408]{0:T(512)} %constant.7.clone.pen_z_ref, f32[128]{0:T(128)} %constant.8.clone.pen_y_ref, f32[64,8,128]{2,1,0:T(8,128)} %shard_map.78.src_ref), custom_call_target="tpu_custom_call" | custom-call | tf_op jit(solution)/shard_map/pallas_call | solution.py:485
  100.6 0.0 copy-done
  100.6 0.0 copy-start.1
  100.6 0.7 copy.10
  101.3 0.3 copy-done.1
  101.6 0.7 copy.11
Async XLA Ops:
  58.5 42.1 %copy-start = (f32[4,4,8,512]{3,2,1,0:T(8,128)S(1)}, f32[4,4,8,512]{3,2,1,0:T(8,128)}, u32[]{:S(2)}) copy-start(f32[4,4,8,512]{3,2,1,0:T(8,128)} %shard_map.77) | copy-start | bytes 786436
  100.6 1.0 %copy-start.1 = (f32[128,512]{1,0:T(8,128)S(1)}, f32[128,512]{1,0:T(8,128)}, u32[]{:S(2)}) copy-start(f32[128,512]{1,0:T(8,128)} %shard_map.79) | copy-start | bytes 786436

commit v16 on v14

--- a/solution.py
+++ b/solution.py
@@ -233,7 +233,7 @@
         hi = (reach + nx - 1 - 8 * g0) // 8
         return lo, hi
 
-    scan_offsets(u_ref, pen_ref, out_ref, n_out, 16, 8, q_range, after_group)
+    scan_offsets(u_ref, pen_ref, out_ref, n_out, 8, 8, q_range, after_group)
 
 
 def transpose_kernel(src_ref, out_ref):
@@ -408,7 +408,7 @@
 
 
 def xpass_send_kernel(pen_ref, src_ref, out_ref, pad_ref, u_ref, tiles_ref, mid_ref, recv_ref, sems, grp_sems):
-    ex = Exchange(mid_ref, recv_ref, sems, grp_sems, 16)
+    ex = Exchange(mid_ref, recv_ref, sems, grp_sems, 8)
     ex.greet()
 
     def after_group(g0, group):
@@ -417,11 +417,11 @@
         if g == 0:
             ex.wait_greetings()
         ex.send_rows(tiles_ref, g, g0)
-        if g >= 1:
-            ex.forward_group(g - 1, g0 - group)
+        if g >= 2:
+            ex.forward_group(g - 2, g0 - 2 * group)
 
     xpass_kernel(pen_ref, src_ref, tiles_ref, pad_ref, u_ref, after_group)
-    ex.finish(tiles_ref, out_ref, 1)
+    ex.finish(tiles_ref, out_ref, 2)
 
 
 def zy_send_kernel(pen_z_ref, pen_y_ref, src_ref, out_ref, pad_ref, u_ref, w_ref, tiles_ref, mid_ref,
@@ -457,7 +457,7 @@
         in_specs=[smem, vmem],
         out_specs=vmem,
         scratch_shapes=[pltpu.VMEM((xu + 8, 8, lines), jnp.float32),
-                        pltpu.VMEM((8, xu, 8, lines), jnp.float32)] + exchange_scratch(tiles, n_gz // 16),
+                        pltpu.VMEM((8, xu, 8, lines), jnp.float32)] + exchange_scratch(tiles, n_gz // 8),
         compiler_params=pltpu.CompilerParams(collective_id=1, has_side_effects=True),
     )(pen_x, current.reshape(lines, nx))
     zq = KERNEL // 4

time: 99.5 us -> 103 us (1.035)
  the two profiles are of different devices: /device:TPU:6 before, /device:TPU:33 now
where the time goes in v16:
time: 103 us
  Pallas kernels  101 us (98%)
  local copies, waits for them, and re-layouts  1.74 us (2%)
    pallas_call x1, Pallas kernels, regularize(): pl.pallas_call(xpass_send_kernel, out_shape=jax.ShapeDtypeStruct(tiles, j...  41.8 us
    pallas_call x1, Pallas kernels, regularize(): pl.pallas_call(zy_send_kernel, out_shape=jax.ShapeDtypeStruct((lines, nx)...  36.3 us
    pallas_call x1, Pallas kernels, evolve_all(): pl.pallas_call(evolve_kernel, out_shape=jax.ShapeDtypeStruct(current.shap...  22.5 us

profile of v16, /device:TPU:33, one launch (start us, length us, event | category | flops | bytes accessed | tf_op | source)
XLA Modules:
  0.0 103.0 jit_solution(13490478309140183539)
XLA Ops:
  0.6 22.5 %shard_map.77 = f32[4,4,8,512]{3,2,1,0:T(8,128)} custom-call(f32[16]{0:T(128)} %means_ref.1, f32[4,4,8,512]{3,2,1,0:T(8,128)} %cur_ref.1, f32[4,8,512]{2,1,0:T(8,128)} %ct_ref.1), custom_call_target="tpu_custom_call" | custom-call | tf_op jit(solution)/shard_map/pallas_call | solution.py:166
  23.1 41.8 %shard_map.78.src_ref = f32[64,8,128]{2,1,0:T(8,128)} custom-call(f32[416]{0:T(512)} %constant.6.clone.pen_ref, f32[128,512]{1,0:T(8,128)} %bitcast.2), custom_call_target="tpu_custom_call" | custom-call | tf_op jit(solution)/shard_map/pallas_call | solution.py:454
  65.0 0.0 copy-start
  65.0 36.3 %shard_map.79 = f32[128,512]{1,0:T(8,128)} custom-call(f32[408]{0:T(512)} %constant.7.clone.pen_z_ref, f32[128]{0:T(128)} %constant.8.clone.pen_y_ref, f32[64,8,128]{2,1,0:T(8,128)} %shard_map.78.src_ref), custom_call_target="tpu_custom_call" | custom-call | tf_op jit(solution)/shard_map/pallas_call | solution.py:467
  101.3 0.0 copy-done
  101.3 0.0 copy-start.1
  101.3 0.7 copy.10
  102.0 0.3 copy-done.1
  102.3 0.7 copy.11
Async XLA Ops:
  65.0 36.3 %copy-start = (f32[4,4,8,512]{3,2,1,0:T(8,128)S(1)}, f32[4,4,8,512]{3,2,1,0:T(8,128)}, u32[]{:S(2)}) copy-start(f32[4,4,8,512]{3,2,1,0:T(8,128)} %shard_map.77) | copy-start | bytes 786436
  101.3 1.0 %copy-start.1 = (f32[128,512]{1,0:T(8,128)S(1)}, f32[128,512]{1,0:T(8,128)}, u32[]{:S(2)}) copy-start(f32[128,512]{1,0:T(8,128)} %shard_map.79) | copy-start | bytes 786436

commit v17 on v14

--- a/solution.py
+++ b/solution.py
@@ -23,9 +23,9 @@
     ax = jnp.abs(x)
     big = ax > 2.414213562373095
     mid = ax > 0.4142135623730950
-    z_big = -1.0 / jnp.where(big, ax, 1.0)
-    z_mid = (ax - 1.0) / (ax + 1.0)
-    z = jnp.where(big, z_big, jnp.where(mid, z_mid, ax))
+    num = jnp.where(big, -1.0, jnp.where(mid, ax - 1.0, ax))
+    den = jnp.where(big, ax, jnp.where(mid, ax + 1.0, 1.0))
+    z = num / den
     base = jnp.where(big, math.pi / 2, jnp.where(mid, math.pi / 4, 0.0))
     zz = z * z
     poly = (((8.05374449538e-2 * zz - 1.38776856032e-1) * zz + 1.99777106478e-1) * zz

time: 99.5 us -> 99.5 us (level)
  no operation moved by 1% of the time
where the time goes in v17:
time: 99.5 us; the launch traced here: 99.3 us
  Pallas kernels  96.8 us (97%)
  local copies, waits for them, and re-layouts  1.74 us (2%)
    pallas_call x1, Pallas kernels, regularize(): pl.pallas_call(xpass_send_kernel, out_shape=jax.ShapeDtypeStruct(tiles, j...  40.1 us
    pallas_call x1, Pallas kernels, regularize(): pl.pallas_call(zy_send_kernel, out_shape=jax.ShapeDtypeStruct((lines, nx)...  39 us
    pallas_call x1, Pallas kernels, evolve_all(): pl.pallas_call(evolve_kernel, out_shape=jax.ShapeDtypeStruct(current.shap...  17.8 us

profile of v17, /device:TPU:6, one launch (start us, length us, event | category | flops | bytes accessed | tf_op | source)
XLA Modules:
  0.0 99.3 jit_solution(8507289249696062428)
XLA Ops:
  0.6 17.8 %shard_map.77 = f32[4,4,8,512]{3,2,1,0:T(8,128)} custom-call(f32[16]{0:T(128)} %means_ref.1, f32[4,4,8,512]{3,2,1,0:T(8,128)} %cur_ref.1, f32[4,8,512]{2,1,0:T(8,128)} %ct_ref.1), custom_call_target="tpu_custom_call" | custom-call | tf_op jit(solution)/shard_map/pallas_call | solution.py:166
  18.4 40.1 %shard_map.78.src_ref = f32[64,8,128]{2,1,0:T(8,128)} custom-call(f32[416]{0:T(512)} %constant.6.clone.pen_ref, f32[128,512]{1,0:T(8,128)} %bitcast.2), custom_call_target="tpu_custom_call" | custom-call | tf_op jit(solution)/shard_map/pallas_call | solution.py:454
  58.5 0.0 copy-start
  58.5 39.0 %shard_map.79 = f32[128,512]{1,0:T(8,128)} custom-call(f32[408]{0:T(512)} %constant.7.clone.pen_z_ref, f32[128]{0:T(128)} %constant.8.clone.pen_y_ref, f32[64,8,128]{2,1,0:T(8,128)} %shard_map.78.src_ref), custom_call_target="tpu_custom_call" | custom-call | tf_op jit(solution)/shard_map/pallas_call | solution.py:467
  97.5 0.0 copy-done
  97.5 0.0 copy-start.1
  97.5 0.7 copy.10
  98.2 0.3 copy-done.1
  98.6 0.7 copy.11
Async XLA Ops:
  58.5 39.0 %copy-start = (f32[4,4,8,512]{3,2,1,0:T(8,128)S(1)}, f32[4,4,8,512]{3,2,1,0:T(8,128)}, u32[]{:S(2)}) copy-start(f32[4,4,8,512]{3,2,1,0:T(8,128)} %shard_map.77) | copy-start | bytes 786436
  97.5 1.0 %copy-start.1 = (f32[128,512]{1,0:T(8,128)S(1)}, f32[128,512]{1,0:T(8,128)}, u32[]{:S(2)}) copy-start(f32[128,512]{1,0:T(8,128)} %shard_map.79) | copy-start | bytes 786436

commit v18 on v14

--- a/solution.py
+++ b/solution.py
@@ -288,7 +288,7 @@
     lax.fori_loop(0, n_out // 8, wbody, 0)
     if before_y is not None:
         before_y()
-    group = 8
+    group = 16
     shifts = []
     for db in range(-8, 8):
         for dy in range(8):
@@ -426,7 +426,7 @@
 
 def zy_send_kernel(pen_z_ref, pen_y_ref, src_ref, out_ref, pad_ref, u_ref, w_ref, tiles_ref, mid_ref,
                    recv_ref, sems, grp_sems):
-    ex = Exchange(mid_ref, recv_ref, sems, grp_sems, 8)
+    ex = Exchange(mid_ref, recv_ref, sems, grp_sems, 16)
     ex.greet()
 
     def after_group(a0, group):
@@ -471,7 +471,7 @@
         out_specs=vmem,
         scratch_shapes=[pltpu.VMEM((zu + 8, 8, lines), jnp.float32),
                         pltpu.VMEM((4, zu, 8, lines), jnp.float32),
-                        pltpu.VMEM((8, n_gz, 8, lines), jnp.float32)] + exchange_scratch(tiles, n_gz // 8),
+                        pltpu.VMEM((8, n_gz, 8, lines), jnp.float32)] + exchange_scratch(tiles, n_gz // 16),
         compiler_params=pltpu.CompilerParams(collective_id=2, has_side_effects=True),
     )(pen_z, pen_y, r1)
     return r2.reshape(current.shape)

time: 99.5 us -> 99.9 us (level)
  no operation moved by 1% of the time
where the time goes in v18:
time: 99.9 us; the launch traced here: 99.5 us
  Pallas kernels  97.1 us (97%)
  local copies, waits for them, and re-layouts  1.74 us (2%)
    pallas_call x1, Pallas kernels, regularize(): pl.pallas_call(xpass_send_kernel, out_shape=jax.ShapeDtypeStruct(tiles, j...  40.1 us
    pallas_call x1, Pallas kernels, regularize(): pl.pallas_call(zy_send_kernel, out_shape=jax.ShapeDtypeStruct((lines, nx)...  39.2 us
    pallas_call x1, Pallas kernels, evolve_all(): pl.pallas_call(evolve_kernel, out_shape=jax.ShapeDtypeStruct(current.shap...  17.8 us

profile of v18, /device:TPU:6, one launch (start us, length us, event | category | flops | bytes accessed | tf_op | source)
XLA Modules:
  0.0 99.5 jit_solution(11393655092174583225)
XLA Ops:
  0.6 17.8 %shard_map.77 = f32[4,4,8,512]{3,2,1,0:T(8,128)} custom-call(f32[16]{0:T(128)} %means_ref.1, f32[4,4,8,512]{3,2,1,0:T(8,128)} %cur_ref.1, f32[4,8,512]{2,1,0:T(8,128)} %ct_ref.1), custom_call_target="tpu_custom_call" | custom-call | tf_op jit(solution)/shard_map/pallas_call | solution.py:166
  18.4 40.1 %shard_map.78.src_ref = f32[64,8,128]{2,1,0:T(8,128)} custom-call(f32[416]{0:T(512)} %constant.6.clone.pen_ref, f32[128,512]{1,0:T(8,128)} %bitcast.2), custom_call_target="tpu_custom_call" | custom-call | tf_op jit(solution)/shard_map/pallas_call | solution.py:454
  58.5 0.0 copy-start
  58.5 39.2 %shard_map.79 = f32[128,512]{1,0:T(8,128)} custom-call(f32[408]{0:T(512)} %constant.7.clone.pen_z_ref, f32[128]{0:T(128)} %constant.8.clone.pen_y_ref, f32[64,8,128]{2,1,0:T(8,128)} %shard_map.78.src_ref), custom_call_target="tpu_custom_call" | custom-call | tf_op jit(solution)/shard_map/pallas_call | solution.py:467
  97.7 0.0 copy-done
  97.7 0.0 copy-start.1
  97.8 0.7 copy.10
  98.5 0.3 copy-done.1
  98.8 0.7 copy.11
Async XLA Ops:
  58.5 39.2 %copy-start = (f32[4,4,8,512]{3,2,1,0:T(8,128)S(1)}, f32[4,4,8,512]{3,2,1,0:T(8,128)}, u32[]{:S(2)}) copy-start(f32[4,4,8,512]{3,2,1,0:T(8,128)} %shard_map.77) | copy-start | bytes 786436
  97.7 1.0 %copy-start.1 = (f32[128,512]{1,0:T(8,128)S(1)}, f32[128,512]{1,0:T(8,128)}, u32[]{:S(2)}) copy-start(f32[128,512]{1,0:T(8,128)} %shard_map.79) | copy-start | bytes 786436

commit v19 on v14

--- a/solution.py
+++ b/solution.py
@@ -434,8 +434,12 @@
         g = a0 // group
         ex.send_rows(tiles_ref, g, a0)
 
+        @pl.when(g >= 4)
+        def _():
+            ex.forward_group(g - 4, a0 - 4 * group)
+
     zy_kernel(pen_z_ref, pen_y_ref, src_ref, tiles_ref, pad_ref, u_ref, w_ref, ex.wait_greetings, after_group)
-    ex.finish(tiles_ref, out_ref, n_gz_groups(ex), transpose=True)
+    ex.finish(tiles_ref, out_ref, 4, transpose=True)
 
 
 def regularize(current):

time: 99.5 us -> 103 us (1.035)
  the two profiles are of different devices: /device:TPU:6 before, /device:TPU:96 now
where the time goes in v19:
time: 103 us
  Pallas kernels  101 us (98%)
  local copies, waits for them, and re-layouts  1.74 us (2%)
    pallas_call x1, Pallas kernels, regularize(): pl.pallas_call(xpass_send_kernel, out_shape=jax.ShapeDtypeStruct(tiles, j...  42.2 us
    pallas_call x1, Pallas kernels, regularize(): pl.pallas_call(zy_send_kernel, out_shape=jax.ShapeDtypeStruct((lines, nx)...  38.8 us
    pallas_call x1, Pallas kernels, evolve_all(): pl.pallas_call(evolve_kernel, out_shape=jax.ShapeDtypeStruct(current.shap...  19.7 us

profile of v19, /device:TPU:96, one launch (start us, length us, event | category | flops | bytes accessed | tf_op | source)
XLA Modules:
  0.0 103.1 jit_solution(9753723568250024490)
XLA Ops:
  0.6 19.7 %shard_map.77 = f32[4,4,8,512]{3,2,1,0:T(8,128)} custom-call(f32[16]{0:T(128)} %means_ref.1, f32[4,4,8,512]{3,2,1,0:T(8,128)} %cur_ref.1, f32[4,8,512]{2,1,0:T(8,128)} %ct_ref.1), custom_call_target="tpu_custom_call" | custom-call | tf_op jit(solution)/shard_map/pallas_call | solution.py:166
  20.4 42.2 %shard_map.78.src_ref = f32[64,8,128]{2,1,0:T(8,128)} custom-call(f32[416]{0:T(512)} %constant.6.clone.pen_ref, f32[128,512]{1,0:T(8,128)} %bitcast.2), custom_call_target="tpu_custom_call" | custom-call | tf_op jit(solution)/shard_map/pallas_call | solution.py:458
  62.5 0.0 copy-start
  62.5 38.8 %shard_map.79 = f32[128,512]{1,0:T(8,128)} custom-call(f32[408]{0:T(512)} %constant.7.clone.pen_z_ref, f32[128]{0:T(128)} %constant.8.clone.pen_y_ref, f32[64,8,128]{2,1,0:T(8,128)} %shard_map.78.src_ref), custom_call_target="tpu_custom_call" | custom-call | tf_op jit(solution)/shard_map/pallas_call | solution.py:471
  101.4 0.0 copy-done
  101.4 0.0 copy-start.1
  101.4 0.7 copy.10
  102.1 0.3 copy-done.1
  102.4 0.7 copy.11
Async XLA Ops:
  62.5 38.8 %copy-start = (f32[4,4,8,512]{3,2,1,0:T(8,128)S(1)}, f32[4,4,8,512]{3,2,1,0:T(8,128)}, u32[]{:S(2)}) copy-start(f32[4,4,8,512]{3,2,1,0:T(8,128)} %shard_map.77) | copy-start | bytes 786436
  101.4 1.0 %copy-start.1 = (f32[128,512]{1,0:T(8,128)S(1)}, f32[128,512]{1,0:T(8,128)}, u32[]{:S(2)}) copy-start(f32[128,512]{1,0:T(8,128)} %shard_map.79) | copy-start | bytes 786436
